TPU v7x, 32 devices: a whole 2x2x4 slice. The times are simulated.
32 devices in a mesh: gx: 4 (over z), gy: 8 (over y, x, core).
Axes of the slice: x: 2, y: 2, z: 4, core: 2. Of those that a mesh axis runs over, the one named last changes fastest.
Arguments:
- particles: bfloat16 [2048, 4096], P(('gx', 'gy')), may hold values from -6 to 6
- references: bfloat16 [4, 12, 4096], P('gx'), may hold values from -1 to 1
- slot_class: int32 [4], replicated, may hold values from 0 to 3, each once
- log_prior: float32 [4], replicated, may hold values from -2 to 2
- shift_offsets: int32 [8, 2], replicated, may hold values from -8 to 8
- group_ids: int32 [2048], P(('gx', 'gy')), may hold values from 0 to 127
- ctf_table: float32 [128, 2048], replicated, may hold values from -1 to 1
- noise_power: float32 [2048], replicated, may hold values from 0.5 to 2
Outputs:
- class_sums: float32 [4, 12, 4096], P('gx')
- ctf_power: float32 [4, 2048], P('gx')
- log_evidence: float32 [], replicated
Inputs may be any that keep to these rules, and one draw needn't show every extreme that they name: `slot_class`: each class id stands at exactly one slot.
All inputs are finite; a program needn't handle non-finite values.
Results may differ from a plain program's by a relative error of at most 0.006.
Values may be sent and summed in bfloat16 or wider, within the bound.
No kernel may reach another device: no remote copies, remote signals or barrier semaphores. Data moves between devices by JAX's collectives and lax.ppermute only.
A program may use at most 64 MiB of HBM per device.

v0:
```python
import jax
import jax.numpy as jnp
from jax import lax
from jax.sharding import PartitionSpec as P

L = 64
R = 12
NS = 8
G = 128
HALF = 2048
FR = 4096


def phase_tables(shift_offsets, edge_len):
    half_size = edge_len * edge_len // 2
    freq_index = jnp.arange(half_size, dtype=jnp.int32)
    row_freq = freq_index // (edge_len // 2)
    col_freq = freq_index % (edge_len // 2)
    phase_turns = jnp.mod(
        row_freq[None, :] * shift_offsets[:, 0:1] + col_freq[None, :] * shift_offsets[:, 1:2],
        edge_len,
    )
    angles = phase_turns.astype(jnp.float32) * (2.0 * jnp.pi / edge_len)
    return (jnp.cos(angles), jnp.sin(angles))


def spectra(particles, edge_len):
    rows_here = particles.shape[0]
    half_side = edge_len // 2
    images = particles.astype(jnp.float32).reshape(rows_here * edge_len, edge_len)
    pixel_index = jnp.arange(edge_len, dtype=jnp.int32)
    column_turns = jnp.mod(pixel_index[:, None] * pixel_index[None, :half_side], edge_len).astype(
        jnp.float32
    ) * (2.0 * jnp.pi / edge_len)
    column_table = jnp.concatenate([jnp.cos(column_turns), -jnp.sin(column_turns)], axis=1)
    partial_x = jnp.dot(
        images, column_table, precision=lax.Precision.HIGHEST, preferred_element_type=jnp.float32
    )
    partial_x = partial_x.reshape(rows_here, edge_len, edge_len)
    row_turns = jnp.mod(pixel_index[:, None] * pixel_index[None, :], edge_len).astype(
        jnp.float32
    ) * (2.0 * jnp.pi / edge_len)
    with_cos = jnp.einsum(
        "uy,pyw->puw", jnp.cos(row_turns), partial_x, precision=lax.Precision.HIGHEST
    )
    with_sin = jnp.einsum(
        "uy,pyw->puw", jnp.sin(row_turns), partial_x, precision=lax.Precision.HIGHEST
    )
    real_part = (with_cos[..., :half_side] + with_sin[..., half_side:]) / edge_len
    imag_part = (with_cos[..., half_side:] - with_sin[..., :half_side]) / edge_len
    return (real_part.reshape(rows_here, -1), imag_part.reshape(rows_here, -1))


def shards(
    particles, references, slot_class, log_prior, shift_offsets, group_ids, ctf_table, noise_power
):
    rows_here = particles.shape[0]
    classes = lax.axis_size("gx") * references.shape[0]
    row_width = R * NS
    real_part, imag_part = spectra(particles, L)
    inv_noise = 1.0 / noise_power
    group_hot = (group_ids[:, None] == jnp.arange(G, dtype=jnp.int32)[None, :]).astype(jnp.float32)
    ctf_rows = jnp.dot(
        group_hot, ctf_table, precision=lax.Precision.HIGHEST, preferred_element_type=jnp.float32
    )
    whiten = ctf_rows * inv_noise
    weighted = jnp.concatenate([real_part * whiten, imag_part * whiten], axis=1).astype(
        jnp.bfloat16
    )
    data_power = jnp.sum((real_part * real_part + imag_part * imag_part) * inv_noise, axis=1)
    cosines, sine_table = phase_tables(shift_offsets, L)
    power_table = ctf_table * ctf_table * inv_noise
    blank = jnp.zeros((rows_here, classes * row_width), jnp.float32)
    piece = lax.all_gather(references, "gx", axis=0, tiled=True)

    def add_class(offset, table):
        stack_row = lax.dynamic_index_in_dim(piece, offset, 0, keepdims=False).astype(jnp.float32)
        stack_real = stack_row[:, :HALF]
        stack_imag = stack_row[:, HALF:]
        shifted_real = (
            stack_real[:, None, :] * cosines[None] + stack_imag[:, None, :] * sine_table[None]
        )
        shifted_imag = (
            stack_imag[:, None, :] * cosines[None] - stack_real[:, None, :] * sine_table[None]
        )
        shifted = (
            jnp.concatenate([shifted_real, shifted_imag], axis=2)
            .astype(jnp.bfloat16)
            .reshape(row_width, FR)
        )
        intersection = lax.dot_general(
            weighted, shifted, (((1,), (1,)), ((), ())), preferred_element_type=jnp.float32
        )
        amplitude = stack_real * stack_real + stack_imag * stack_imag
        ref_power = jnp.dot(
            power_table,
            amplitude.T,
            precision=lax.Precision.HIGHEST,
            preferred_element_type=jnp.float32,
        )
        own_power = jnp.dot(
            group_hot,
            ref_power,
            precision=lax.Precision.HIGHEST,
            preferred_element_type=jnp.float32,
        )
        logits = intersection.reshape(rows_here, R, NS) - 0.5 * own_power[:, :, None]
        return lax.dynamic_update_slice_in_dim(
            table, logits.reshape(rows_here, row_width), offset * row_width, 1
        )

    scores = lax.fori_loop(0, piece.shape[0], add_class, blank)
    slot_prior = jnp.sum(
        jnp.where(
            slot_class[:, None] == jnp.arange(classes, dtype=jnp.int32)[None, :],
            log_prior[None, :],
            0.0,
        ),
        axis=1,
    )
    logits = (
        scores.reshape(rows_here, classes, row_width)
        - 0.5 * data_power[:, None, None]
        + slot_prior[None, :, None]
    )
    row_max = jnp.max(logits, axis=(1, 2), keepdims=True)
    raised = jnp.exp(logits - row_max)
    normaliser = jnp.sum(raised, axis=(1, 2), keepdims=True)
    weights = raised / normaliser
    evidence = row_max[:, 0, 0] + jnp.log(normaliser[:, 0, 0])
    weights_low = weights.astype(jnp.bfloat16)
    group_weights = jnp.dot(
        jnp.sum(weights, axis=2).T,
        group_hot,
        precision=lax.Precision.HIGHEST,
        preferred_element_type=jnp.float32,
    )

    def class_terms(slot_index):
        weight_cols = lax.dynamic_index_in_dim(weights_low, slot_index, 1, keepdims=False)
        moment = lax.dot_general(
            weight_cols, weighted, (((0,), (0,)), ((), ())), preferred_element_type=jnp.float32
        )
        moment = moment.reshape(R, NS, FR)
        moment_real = moment[..., :HALF]
        moment_imag = moment[..., HALF:]
        back_real = jnp.sum(moment_real * cosines[None] - moment_imag * sine_table[None], axis=1)
        back_imag = jnp.sum(moment_imag * cosines[None] + moment_real * sine_table[None], axis=1)
        return jnp.concatenate([back_real, back_imag], axis=1)

    owned = lax.psum_scatter(
        lax.map(
            lambda offset: class_terms(offset),
            jnp.arange(references.shape[0] * lax.axis_size("gx"), dtype=jnp.int32),
        ),
        "gx",
        scatter_dimension=0,
        tiled=True,
    )
    class_sums = lax.psum(owned, "gy")
    totals, evidence_sum = lax.psum((group_weights, jnp.sum(evidence)), ("gx", "gy"))
    own_groups = lax.dynamic_slice_in_dim(totals, lax.axis_index("gx"), 1, 0)
    ctf_power = jnp.dot(
        own_groups,
        ctf_table * ctf_table,
        precision=lax.Precision.HIGHEST,
        preferred_element_type=jnp.float32,
    )
    log_evidence = evidence_sum / (rows_here * lax.axis_size("gx") * lax.axis_size("gy") * HALF)
    return (class_sums, ctf_power, log_evidence)


def solution(mesh):
    return jax.shard_map(
        shards,
        mesh=mesh,
        in_specs=(
            P(("gx", "gy"), None),
            P("gx", None, None),
            P(),
            P(),
            P(),
            P(("gx", "gy")),
            P(),
            P(),
        ),
        out_specs=(P("gx", None, None), P("gx", None), P()),
        check_vma=False,
    )
```

profile of v0, /device:TPU:0, one launch (start us, length us, event | category | flops | bytes accessed | tf_op | source)
XLA Modules:
  0.0 206.5 jit_solution(13460478304987082292)
XLA Ops:
  7.4 2.1 reshape.111
  9.4 1.3 convolution_bitcast_fusion.1
  11.6 4.6 %fusion.46 = f32[64,64,64]{1,2,0:T(8,128)} fusion(f32[64,64,64]{1,0,2:T(8,128)S(1)} %reshape.112), kind=kOutput, calls=%fused_computation.59 | convolution fusion | flops 201383936 | bytes 2097152 | tf_op jit(solution)/shard_map/uy,pyw->puw/dot_general | solution.py:43
  16.2 4.7 %fusion.49 = f32[64,64,64]{1,2,0:T(8,128)} fusion(f32[64,64,64]{1,0,2:T(8,128)S(1)} %reshape.112), kind=kOutput, calls=%fused_computation.60 | convolution fusion | flops 201383936 | bytes 2097152 | tf_op jit(solution)/shard_map/uy,pyw->puw/dot_general | solution.py:46
  21.7 3.4 %multiply_reduce_fusion = (f32[64]{0:T(128)}, f32[64,64,32]{1,2,0:T(8,128)S(1)}, f32[64,64,32]{1,2,0:T(8,128)S(1)}) fusion(f32[64,32]{0,1:T(8,128)S(1)} %copy.44, f32[64,64,64]{1,2,0:T(8,128)} %fusion.49, f32[64,64,64]{1,2,0:T(8,128)} %fusion.46), kind=kLoop, calls=%fused_computation.65 | loop fusion | flops 1179584 | bytes 3154176 | tf_op jit(solution)/shard_map/reduce_sum | solution.py:70
  25.1 1.1 copy.39
  26.1 1.1 copy.40
  27.3 1.1 copy.41
  28.4 1.1 copy.42
  30.3 18.2 %all_gather.3 = bf16[4,12,4096]{2,1,0:T(8,128)(2,1)} all-gather(bf16[1,12,4096]{2,1,0:T(8,128)(2,1)S(1)} %copy-done.3), channel_id=1, replica_groups=mesh['gx'=4,'gy'=8] {'gx'}, dimensions={0}, use_global_device_ids=true | all-gather | bytes 491520 | tf_op jit(solution)/shard_map/all_gather | solution.py:74
  48.4 1.2 multiply_convert_fusion.1
  49.7 25.9 %while.27 = (s32[]{:T(128)}, f32[64,384]{1,0:T(8,128)S(1)}, bf16[4,12,4096]{2,1,0:T(8,128)(2,1)}, bf16[64,4096]{1,0:T(8,128)(2,1)S(1)}, f32[128,2048]{1,0:T(8,12...) while((s32[]{:T(128)}, f32[64,384]{1,0:T(8,128)S(1)}, ...), condition=%wide.region_1.2_spmd.clone.clone, body=%wide.region_0.1_spmd.clone.clone.sunk | while | flops 92814080 | bytes 4696571 | solution.py:112
  49.7 0.9 bitcast_convert_fusion.2
  50.7 1.1 fusion.137
  54.5 1.2 fusion.140
  56.1 0.9 bitcast_convert_fusion.2
  57.1 1.1 fusion.137
  60.9 1.2 fusion.140
  62.7 0.9 bitcast_convert_fusion.2
  63.6 1.1 fusion.137
  67.4 1.2 fusion.140
  70.2 1.1 fusion.137
  74.0 1.2 fusion.140
  78.0 21.0 %while.28 = (s32[]{:T(128)}, f32[4,12,4096]{2,1,0:T(8,128)}, s32[4]{0:T(128)S(1)}, bf16[64,4,96]{0,2,1:T(8,128)(2,1)S(1)}, bf16[64,4096]{1,0:T(8,128)(2,1)S(1)},...) while((s32[]{:T(128)}, f32[4,12,4096]{2,1,0:T(8,128)}, ...), condition=%wide.region_9.10_spmd.clone.clone, body=%wide.region_6.9_spmd.clone.clone.sunk | while | flops 52166660 | bytes 4629223 | solution.py:152
  80.9 1.1 fusion.144
  86.1 1.1 fusion.144
  91.4 1.1 fusion.144
  96.6 1.1 fusion.144
  100.5 42.4 %all-reduce = (f32[4,128]{1,0:T(4,128)S(1)}, f32[]{:T(128)}) all-reduce(f32[4,128]{1,0:T(4,128)S(1)} %fusion.68, f32[]{:T(128)} %add_reduce_fusion.1), channel_id=1, replica_groups=mesh['gx'=4,'gy'=8] {'gx','gy'}, use_global_device_ids=true, to_apply=%region_13.14 | all-reduce | flops 513 | bytes 4104 | tf_op jit(solution)/shard_map/psum | solution.py:161
  143.0 1.2 fusion.54
  144.9 51.8 %all-reduce.3.cloned.1.call-done = f32[1,12,4096]{2,1,0:T(8,128)} async-done(((f32[1,12,4096]{2,1,0:T(8,128)}), f32[1,12,4096]{2,1,0:T(8,128)}) %all-reduce.3.cloned.1.call-update) | async-done | bytes 196624 | tf_op jit(solution)/shard_map/psum | solution.py:160
  196.7 1.8 copy.45
  (85 shorter events, 29.3 us)
Async XLA Ops:
  7.2 135.8 %reduce-scatter.2.cloned.1.call-start = ((), (), s32[]{:S(2)}) async-start(), calls=%async_computation.1 | async-start | bytes 1310720 | tf_op jit(solution)/shard_map/reduce_scatter | solution.py:151
  16.2 5.3 %copy-start.4 = (f32[2048]{0:T(1024)S(1)}, f32[2048]{0:T(1024)}, u32[]{:S(2)}) copy-start(f32[2048]{0:T(1024)} %param.19) | copy-start | bytes 24580
  27.3 2.3 %copy-start = (f32[128,2048]{1,0:T(8,128)S(1)}, f32[128,2048]{1,0:T(8,128)}, u32[]{:S(2)}) copy-start(f32[128,2048]{1,0:T(8,128)} %param.18) | copy-start | bytes 3145732
  28.4 1.3 copy-start.5
  28.4 1.9 copy-start.3
  29.5 18.9 %copy-start.1 = (f32[64,2048]{1,0:T(8,128)S(1)}, f32[64,2048]{1,0:T(8,128)}, u32[]{:S(2)}) copy-start(f32[64,2048]{1,0:T(8,128)} %copy.40) | copy-start | bytes 1572868
  29.5 18.9 %copy-start.2 = (f32[64,2048]{1,0:T(8,128)S(1)}, f32[64,2048]{1,0:T(8,128)}, u32[]{:S(2)}) copy-start(f32[64,2048]{1,0:T(8,128)} %copy.42) | copy-start | bytes 1572868
  99.0 97.7 %all-reduce.3.cloned.1.call-start = ((), (), s32[]{:S(2)}) async-start(), calls=%async_computation.2 | async-start | bytes 524288 | tf_op jit(solution)/shard_map/psum | solution.py:160
Sparse Core Ops, SparseCore 0:
  99.2 29.8 reduce-scatter.1
  143.1 53.5 all-reduce.2
where the time goes:
time: 208 us; the launch traced here: 206 us
  blocking collectives  60.6 us (29%)
  waiting for transfers between devices  51.9 us (25%)
  matrix products  27.2 us (13%)
  other arithmetic  25.1 us (12%)
  local copies, waits for them, and re-layouts  17.6 us (8%)
  between operations  16 us (8%)
  loops' own time  8.13 us (4%)
    psum x1, waiting for transfers between devices, shards(): class_sums = lax.psum(owned, 'gy')  51.8 us
    psum x1, blocking collectives, shards(): lax.psum((group_weights, jnp.sum(evidence)), ('gx', 'gy'))  42.4 us
    all_gather x1, blocking collectives, shards(): piece = lax.all_gather(references, 'gx', axis=0, tiled=True)  18.2 us
    cos x8, other arithmetic, phase_tables(): return (jnp.cos(angles), jnp.sin(angles))  8.53 us
    another operation x1, loops' own time, shards(): lax.map(lambda offset: class_terms(offset), jnp.arange(references.shape[0...  7.85 us
    dot_general x1, matrix products, spectra(): jnp.einsum('uy,pyw->puw', jnp.sin(row_turns), partial_x, precision=lax.Pr...  4.7 us
    dot_general x1, matrix products, spectra(): jnp.einsum('uy,pyw->puw', jnp.cos(row_turns), partial_x, precision=lax.Pr...  4.65 us
    dot_general x4, matrix products, add_class(): lax.dot_general(weighted, shifted, (((1,), (1,)), ((), ())), preferred_el...  4.62 us
  transfers between devices with their start and end apart: 2, of which 1 were waited for; matrix products, arithmetic and copies ran while one was open for 1% of the time, Pallas kernels for 0%

commit v1 on v0

v1 whole, which is shorter than its diff:
```python
import functools
import math

import jax
import jax.numpy as jnp
import numpy as np
from jax import lax
from jax.experimental import pallas as pl
from jax.experimental.pallas import tpu as pltpu
from jax.sharding import PartitionSpec as P

F32 = jnp.float32
BF16 = jnp.bfloat16
LANES = 128
SLOT = 16
FIXED = 6


def dft_tables(side):
    half = side // 2
    fold = LANES // half
    outer = side // fold
    per_row = LANES // side
    y_hi, parity, x = np.meshgrid(np.arange(fold), np.arange(per_row), np.arange(side), indexing="ij")
    y_hi, parity, x = y_hi.reshape(-1, 1), parity.reshape(-1, 1), x.reshape(-1, 1)
    out_par, part, u_lo, v = np.meshgrid(
        np.arange(per_row), np.arange(2), np.arange(fold), np.arange(half), indexing="ij"
    )
    out_par, part, u_lo, v = (t.reshape(1, -1) for t in (out_par, part, u_lo, v))
    turns = (v * x + outer * u_lo * y_hi) % side
    angle = 2.0 * np.pi * turns / side
    table = np.where(part == 0, np.cos(angle), -np.sin(angle)) / side
    table = np.where(parity == out_par, table, 0.0).astype(np.float32)
    high = table.astype(BF16)
    low = (table - high.astype(np.float32)).astype(BF16)
    lane_u = np.arange(LANES) // half
    turn = (np.arange(outer)[:, None] * lane_u[None, :]) % side
    angle = 2.0 * np.pi * turn / side
    twiddle = np.stack([np.cos(angle), np.sin(angle)], 1).astype(np.float32)
    turn = 2.0 * np.pi * np.arange(side) / side
    wave = np.concatenate([np.cos(turn), np.sin(turn)]).astype(np.float32)
    return high, low, twiddle.reshape(2 * outer, LANES), np.tile(wave[None], (8, 1))


def butterflies(real, imag):
    count = len(real)
    if count == 1:
        return real, imag
    even_r, even_i = butterflies(real[0::2], imag[0::2])
    odd_r, odd_i = butterflies(real[1::2], imag[1::2])
    top_r, top_i, low_r, low_i = [], [], [], []
    for k in range(count // 2):
        c = math.cos(2.0 * math.pi * k / count)
        s = math.sin(2.0 * math.pi * k / count)
        r, i = odd_r[k], odd_i[k]
        if k == 0:
            tr, ti = r, i
        elif 4 * k == count:
            tr, ti = i, -r
        elif 8 * k == count:
            tr, ti = (r + i) * c, (i - r) * c
        elif 8 * k == 3 * count:
            tr, ti = (i - r) * s, -(r + i) * s
        else:
            tr, ti = r * c + i * s, i * c - r * s
        top_r.append(even_r[k] + tr)
        top_i.append(even_i[k] + ti)
        low_r.append(even_r[k] - tr)
        low_i.append(even_i[k] - ti)
    return top_r + low_r, top_i + low_i


def split(value):
    high = value.astype(BF16)
    return high, (value - high.astype(F32)).astype(BF16)


def spectra_body(
    ids, images, high, low, twiddle, wave, offsets, ctf, noise,
    rotated, square_high, square_low, power_high, power_low, data_power,
    stacked, partial, rows, w_real, w_imag, cosine, sine, inverse, total,
):
    count, pixels = images.shape
    side = math.isqrt(pixels)
    half = side // 2
    fold = LANES // half
    outer = side // fold
    per_row = LANES // side
    groups = outer // per_row
    shifts = offsets.shape[0]
    columns = noise.shape[1] // LANES
    width = noise.shape[1]

    for m in range(groups):
        for y in range(fold):
            source = (m + groups * y) * LANES
            stacked[m * count:(m + 1) * count, y * LANES:(y + 1) * LANES] = images[:, source:source + LANES]
    partial[...] = jnp.dot(stacked[...], high[...], preferred_element_type=F32)
    partial[...] += jnp.dot(stacked[...], low[...], preferred_element_type=F32)

    inverse[...] = 1.0 / noise[...]

    def fetch(p, carry):
        rows[pl.ds(p, 1), :] = ctf[pl.ds(ids[p], 1), :]
        return carry

    lax.fori_loop(0, count, fetch, 0, unroll=8)

    lane = lax.broadcasted_iota(jnp.int32, (shifts, LANES), 1)
    step_u = offsets[:, 0:1]
    step_v = offsets[:, 1:2]
    for column in range(columns):
        u = lane // half + fold * column
        turn = (u * step_u + (lane % half) * step_v) & (side - 1)
        at = slice(column * LANES, (column + 1) * LANES)
        cosine[:, at] = jnp.take_along_axis(wave[...], turn, axis=1)
        sine[:, at] = jnp.take_along_axis(wave[...], turn + side, axis=1)

    def transform(block, carry):
        base = block * 8
        real, imag = [], []
        for y in range(outer):
            m, parity = y // per_row, y % per_row
            row = pl.ds(m * count + base, 8)
            r = partial[row, (2 * parity) * LANES:(2 * parity + 1) * LANES]
            i = partial[row, (2 * parity + 1) * LANES:(2 * parity + 2) * LANES]
            if y:
                c = twiddle[2 * y:2 * y + 1, :]
                s = twiddle[2 * y + 1:2 * y + 2, :]
                r, i = r * c + i * s, i * c - r * s
            real.append(r)
            imag.append(i)
        real, imag = butterflies(real, imag)
        here = pl.ds(base, 8)
        energy = jnp.zeros((8, LANES), F32)
        for column in range(columns):
            at = slice(column * LANES, (column + 1) * LANES)
            inv = inverse[:, at]
            whiten = rows[here, at] * inv
            r, i = real[column], imag[column]
            energy += (r * r + i * i) * inv
            w_real[here, at] = (r * whiten).astype(BF16).astype(F32)
            w_imag[here, at] = (i * whiten).astype(BF16).astype(F32)
        total[here, :] = energy
        return carry

    lax.fori_loop(0, count // 8, transform, 0)
    data_power[...] = jnp.broadcast_to(jnp.sum(total[...], axis=1, keepdims=True), data_power.shape)

    def rotate(column, carry):
        at = pl.ds(pl.multiple_of(column * LANES, LANES), LANES)
        far = pl.ds(pl.multiple_of(width + column * LANES, LANES), LANES)
        c0 = rows[:, at]
        sq = c0 * c0
        square_high[:, at], square_low[:, at] = split(sq)
        power_high[:, at], power_low[:, at] = split(sq * inverse[:, at])
        wr, wi = w_real[:, at], w_imag[:, at]
        for s in range(shifts):
            c, n = cosine[s:s + 1, at], sine[s:s + 1, at]
            rotated[s * count:(s + 1) * count, at] = (wr * c - wi * n).astype(BF16)
            rotated[s * count:(s + 1) * count, far] = (wi * c + wr * n).astype(BF16)
        return carry

    lax.fori_loop(0, columns, rotate, 0)


def spectra(group_ids, particles, shift_offsets, ctf_table, noise_power):
    count, pixels = particles.shape
    side = math.isqrt(pixels)
    width = noise_power.shape[0]
    shifts = shift_offsets.shape[0]
    high, low, twiddle, wave = dft_tables(side)
    vmem = pl.BlockSpec(memory_space=pltpu.VMEM)
    shape = jax.ShapeDtypeStruct
    plane = shape((count, width), BF16)
    k = high.shape[0]
    groups = pixels // k
    return pl.pallas_call(
        spectra_body,
        out_shape=(shape((shifts * count, 2 * width), BF16), plane, plane, plane, plane, shape((count, LANES), F32)),
        in_specs=[pl.BlockSpec(memory_space=pltpu.SMEM)] + [vmem] * 8,
        out_specs=(vmem,) * 6,
        scratch_shapes=[
            pltpu.VMEM((groups * count, k), BF16),
            pltpu.VMEM((groups * count, high.shape[1]), F32),
            pltpu.VMEM((count, width), F32),
            pltpu.VMEM((count, width), F32),
            pltpu.VMEM((count, width), F32),
            pltpu.VMEM((shifts, width), F32),
            pltpu.VMEM((shifts, width), F32),
            pltpu.VMEM((1, width), F32),
            pltpu.VMEM((count, LANES), F32),
        ],
        name="spectra",
    )(
        group_ids, particles, jnp.asarray(high), jnp.asarray(low), jnp.asarray(twiddle), jnp.asarray(wave),
        shift_offsets, ctf_table, noise_power.reshape(1, width),
    )


def dot_rows(a, b):
    return lax.dot_general(a, b, (((1,), (1,)), ((), ())), preferred_element_type=F32)


def dot_columns(a, b):
    return lax.dot_general(a, b, (((0,), (0,)), ((), ())), preferred_element_type=F32)


def classes_body(digit_bits, classes, *refs):
    others = classes - 1
    place, slots, priors = refs[:3]
    rotated, square_high, square_low, power_high, power_low, data_power, own = refs[3:10]
    mine = refs[10:10 + others]
    theirs = refs[10 + others:10 + 2 * others]
    keep, send, stack, soft, sums, extra = refs[10 + 2 * others:]
    rotations = own.shape[1]
    count = data_power.shape[0]
    shifts = rotated.shape[0] // count
    width = power_high.shape[1]
    lanes = classes * SLOT
    g, h = place[0], place[1]

    here = pl.ds(pl.multiple_of(h * width, width), width)
    there = pl.ds(pl.multiple_of((1 - h) * width, width), width)
    stack[...] = jnp.zeros_like(stack)
    stack[0:rotations, :] = own[0]
    for d in range(1, classes):
        rows = slice(d * SLOT, d * SLOT + rotations)
        stack[rows, here] = mine[d - 1][...]
        stack[rows, there] = theirs[d - 1][...]

    real, imag = stack[:, :width].astype(F32), stack[:, width:].astype(F32)
    amp_high, amp_low = split(real * real + imag * imag)
    own_power = (
        dot_rows(power_high[...], amp_high) + dot_rows(power_high[...], amp_low) + dot_rows(power_low[...], amp_high)
    )
    lane = lax.broadcasted_iota(jnp.int32, (1, lanes), 1)
    prior = jnp.zeros((1, lanes), F32)
    for d in range(classes):
        slot = lax.rem(g - d + classes, classes)
        prior = jnp.where(lane // SLOT == d, priors[slots[slot]], prior)
    prior = jnp.where(lane % SLOT < rotations, prior, -1e30)
    inter = dot_rows(rotated[...], stack[...])
    logits = []
    top = None
    for s in range(shifts):
        l = inter[s * count:(s + 1) * count] - 0.5 * own_power
        l = (l - 0.5 * data_power[:, 0:1]) + prior
        logits.append(l)
        top = l if top is None else jnp.maximum(top, l)
    row_max = jnp.max(top, axis=1, keepdims=True)
    raised = [jnp.exp(l - row_max) for l in logits]
    norm = jnp.sum(functools.reduce(jnp.add, raised), axis=1, keepdims=True)
    weight = jnp.zeros((count, lanes), F32)
    for s in range(shifts):
        w = raised[s] / norm
        weight += w
        soft[s * count:(s + 1) * count, :] = w.astype(BF16)
    evidence = jnp.sum(row_max + jnp.log(norm), axis=0, keepdims=True)

    sums[...] = dot_columns(soft[...], rotated[...])

    wide = lax.broadcasted_iota(jnp.int32, (count, LANES), 1)
    by_class = jnp.zeros((count, LANES), F32)
    for d in range(classes):
        part = jnp.sum(jnp.where(lane // SLOT == d, weight, 0.0), axis=1, keepdims=True)
        by_class = jnp.where(wide == d, part, by_class)
    class_high, class_low = split(by_class)
    extra[...] = (
        dot_columns(class_high, square_high[...])
        + dot_columns(class_high, square_low[...])
        + dot_columns(class_low, square_high[...])
    )

    column = lax.broadcasted_iota(jnp.int32, (1, width), 1)
    number = jnp.round(jnp.broadcast_to(evidence, (1, width)) * float(2**FIXED)).astype(jnp.int32)
    digit = lax.shift_right_logical(jnp.abs(number), jnp.minimum(column * digit_bits, 31))
    digit = jnp.where(column * digit_bits < 31, digit & (2**digit_bits - 1), 0)
    digit = jnp.where(number < 0, -digit, digit).astype(F32)

    empty = jnp.zeros((SLOT - rotations - 2, width), F32)
    for d in range(classes):
        rows = slice(d * SLOT, d * SLOT + rotations)
        tail = jnp.concatenate([extra[d:d + 1, :], digit, empty], axis=0)
        keep[d, 0:rotations, :] = sums[rows, here]
        keep[d, rotations:SLOT, :] = tail
        send[d, :, :] = jnp.concatenate([sums[rows, there], tail], axis=0).astype(BF16)


def classes_call(place, slot_class, log_prior, spectra_out, own, mine, theirs, digit_bits):
    classes = len(mine) + 1
    rotated, *_, data_power = spectra_out
    rows, full = rotated.shape
    width = full // 2
    lanes = classes * SLOT
    vmem = pl.BlockSpec(memory_space=pltpu.VMEM)
    smem = pl.BlockSpec(memory_space=pltpu.SMEM)
    shape = jax.ShapeDtypeStruct
    return pl.pallas_call(
        functools.partial(classes_body, digit_bits, classes),
        out_shape=(shape((classes, SLOT, width), F32), shape((classes, SLOT, width), BF16)),
        in_specs=[smem] * 3 + [vmem] * (7 + 2 * len(mine)),
        out_specs=(vmem, vmem),
        scratch_shapes=[
            pltpu.VMEM((lanes, full), BF16),
            pltpu.VMEM((rows, lanes), BF16),
            pltpu.VMEM((lanes, full), F32),
            pltpu.VMEM((LANES, width), F32),
        ],
        name="classes",
    )(place, slot_class, log_prior, *spectra_out, own, *mine, *theirs)


def tree(parts):
    while len(parts) > 1:
        middle = len(parts) // 2
        parts = [parts[j] + parts[j + middle] for j in range(middle)]
    return parts[0]


def shards(
    particles, references, slot_class, log_prior, shift_offsets, group_ids, ctf_table, noise_power
):
    rings = lax.axis_size("gx")
    spread = lax.axis_size("gy")
    chips = spread // 2
    count = particles.shape[0]
    width = noise_power.shape[0]
    rotations = references.shape[1]
    g = lax.axis_index("gx")
    q = lax.axis_index("gy")
    digit_bits = max(1, 8 - (rings * spread - 1).bit_length())

    def parity(number):
        return bin(number).count("1") & 1

    chip = q // 2
    h = (q & 1) ^ (g & 1)
    for bit in range((chips - 1).bit_length()):
        h = h ^ ((chip >> bit) & 1)

    def move(value, rule):
        pairs = []
        for z in range(rings):
            for c in range(chips):
                for core in range(2):
                    z2, c2, core2 = rule(z, c, core)
                    pairs.append((z * spread + 2 * c + core, z2 * spread + 2 * c2 + core2))
        return lax.ppermute(value, ("gx", "gy"), pairs)

    def shift(d):
        return lambda z, c, core: ((z + d) % rings, c, core ^ (d & 1))

    def swap(z, c, core):
        return z, c, core ^ 1

    def hop(bit):
        return lambda z, c, core: (z, c ^ (1 << bit), core ^ 1)

    half_stack = lax.dynamic_slice_in_dim(references[0], h * width, width, 1)
    mine = [move(half_stack, shift(d)) for d in range(1, rings)]
    theirs = [move(value, swap) for value in mine]
    spectra_out = spectra(group_ids, particles, shift_offsets, ctf_table, noise_power)
    place = jnp.stack([g, h]).astype(jnp.int32)
    keep, send = classes_call(place, slot_class, log_prior, spectra_out, references, mine, theirs, digit_bits)

    pair = keep + move(send, swap).astype(F32)
    gathered = [pair[0]]
    for d in range(1, rings):
        gathered.append(move(pair[d].astype(BF16), shift(rings - d)).astype(F32))
    owned = tree(gathered)
    for bit in range((chips - 1).bit_length()):
        low = owned.astype(BF16)
        owned = lax.reduce_precision(owned, 8, 7) + move(low, hop(bit)).astype(F32)

    other = move(owned, swap)
    first = jnp.where(h == 0, owned, other)
    second = jnp.where(h == 0, other, owned)
    class_sums = jnp.concatenate([first[:rotations], second[:rotations]], axis=1)[None]
    ctf_power = first[rotations][None]
    scale = np.zeros((LANES,), np.float64)
    for j in range(-(-31 // digit_bits)):
        scale[j] = 2.0 ** (j * digit_bits - FIXED)
    scale = scale / (count * rings * spread * width)
    log_evidence = jnp.sum(first[rotations + 1, :LANES] * jnp.asarray(scale, F32))
    return class_sums, ctf_power, log_evidence


def solution(mesh):
    return jax.shard_map(
        shards,
        mesh=mesh,
        in_specs=(
            P(("gx", "gy"), None),
            P("gx", None, None),
            P(),
            P(),
            P(),
            P(("gx", "gy")),
            P(),
            P(),
        ),
        out_specs=(P("gx", None, None), P("gx", None), P()),
        check_vma=False,
    )
```

time: 208 us -> 56.9 us (0.27)
  blocking collectives: 60.6 us -> 0 us
  waiting for transfers between devices: 51.9 us -> 19.2 us
  matrix products: 27.2 us -> 0 us
  other arithmetic: 25.1 us -> 2.46 us
  Pallas kernels: 0 us -> 16.2 us
  between operations: 16 us -> 0.77 us
  starting transfers between devices: 0.08 us -> 13.7 us
  local copies, waits for them, and re-layouts: 17.6 us -> 4.32 us
  loops' own time: 8.13 us -> 0 us
    psum x1 -> x0, waiting for transfers between devices: 51.8 us -> none  [shards(): class_sums = lax.psum(owned, 'gy')]
    psum x1 -> x0, blocking collectives: 42.4 us -> none  [shards(): lax.psum((group_weights, jnp.sum(evidence)), ('gx', 'gy'))]
    dot_general x22 -> x0, matrix products: 27.2 us -> none  [the longest x1 4.7 us: spectra(): jnp.einsum('uy,pyw->puw', jnp.sin(row_turns), partial_x, precision=lax.Pr...]
    ppermute x0 -> x13, waiting for transfers between devices: none -> 19.2 us  [move(): return lax.ppermute(value, ('gx', 'gy'), pairs)]
    all_gather x1 -> x0, blocking collectives: 18.2 us -> none  [shards(): piece = lax.all_gather(references, 'gx', axis=0, tiled=True)]
    pallas_call x0 -> x2, Pallas kernels: none -> 16.2 us  [the longest x1 8.13 us: spectra(): pl.pallas_call(spectra_body, out_shape=(shape((shifts * count, 2 * width)...]
    ppermute x0 -> x13, starting transfers between devices: none -> 13.7 us  [move(): return lax.ppermute(value, ('gx', 'gy'), pairs)]
    cos x9 -> x0, other arithmetic: 8.68 us -> none  [the longest x8 8.53 us: phase_tables(): return (jnp.cos(angles), jnp.sin(angles))]
  transfers between devices with their start and end apart: 2 -> 13, of which waited for: 1 -> 8; matrix products, arithmetic and copies ran while one was open for 1% -> 3% of each run, Pallas kernels for 0% -> 14%
where the time goes in v1:
time: 56.9 us; the launch traced here: 56.6 us
  waiting for transfers between devices  19.2 us (34%)
  Pallas kernels  16.2 us (28%)
  starting transfers between devices  13.7 us (24%)
  local copies, waits for them, and re-layouts  4.32 us (8%)
  other arithmetic  2.46 us (4%)
  between operations  0.77 us (1%)
    ppermute x13, waiting for transfers between devices, move(): return lax.ppermute(value, ('gx', 'gy'), pairs)  19.2 us
    ppermute x13, starting transfers between devices, move(): return lax.ppermute(value, ('gx', 'gy'), pairs)  13.7 us
    pallas_call x1, Pallas kernels, spectra(): pl.pallas_call(spectra_body, out_shape=(shape((shifts * count, 2 * width)...  8.13 us
    pallas_call x1, Pallas kernels, classes_call(): pl.pallas_call(functools.partial(classes_body, digit_bits, classes), out_...  8.11 us
    unnamed x16, local copies, waits for them, and re-layouts  2.85 us
  transfers between devices with their start and end apart: 13, of which 8 were waited for; matrix products, arithmetic and copies ran while one was open for 3% of the time, Pallas kernels for 14%

profile of v1, /device:TPU:0, one launch (start us, length us, event | category | flops | bytes accessed | tf_op | source)
XLA Modules:
  0.0 56.6 jit_solution(4791372626992624211)
XLA Ops:
  0.7 0.8 %dynamic-slice_bitcast_fusion = bf16[12,2048]{1,0:T(8,128)(2,1)S(1)} fusion(bf16[1,12,4096]{2,1,0:T(8,128)(2,1)} %refs_9_.1, s32[]{:T(128)S(6)} %select_n.22), kind=kLoop, calls=%fused_computation.12 | loop fusion | bytes 98308 | tf_op jit(solution)/shard_map/dynamic_slice | solution.py:360
  1.5 4.5 %collective-permute-start.2 = (bf16[12,2048]{1,0:T(8,128)(2,1)S(1)}, bf16[12,2048]{1,0:T(8,128)(2,1)S(1)}, u32[]{:S(2)}, u32[]{:S(2)}) collective-permute-start(bf16[12,2048]{1,0:T(8,128)(2,1)S(1)} %dynamic-slice_bitcast_fusion), channel_id=1, source_target_pairs={{0,25},{1,24},{2,27},{3,26},{4,29},{5,28},{6,31},{7,30},{8,1},{9,0... | collective-permute-start | bytes 147464 | tf_op jit(solution)/shard_map/ppermute | solution.py:349
  6.0 1.0 %collective-permute-start = (bf16[12,2048]{1,0:T(8,128)(2,1)S(1)}, bf16[12,2048]{1,0:T(8,128)(2,1)S(1)}, u32[]{:S(2)}, u32[]{:S(2)}) collective-permute-start(bf16[12,2048]{1,0:T(8,128)(2,1)S(1)} %dynamic-slice_bitcast_fusion), channel_id=1, source_target_pairs={{0,9},{1,8},{2,11},{3,10},{4,13},{5,12},{6,15},{7,14},{8,17},{9,16... | collective-permute-start | bytes 147464 | tf_op jit(solution)/shard_map/ppermute | solution.py:349
  7.0 1.5 %collective-permute-done.2.refs_12_ = bf16[12,2048]{1,0:T(8,128)(2,1)S(1)} collective-permute-done((bf16[12,2048]{1,0:T(8,128)(2,1)S(1)}, bf16[12,2048]{1,0:T(8,128)(2,1)S(1)}, u32[]{:S(2)}, u32[]{:S(2)}) %collective-permute-start.2) | collective-permute-done | bytes 49184 | tf_op jit(solution)/shard_map/ppermute | solution.py:349
  8.6 0.1 collective-permute-start.5
  8.6 5.0 %collective-permute-done.1.refs_11_ = bf16[12,2048]{1,0:T(8,128)(2,1)S(1)} collective-permute-done((bf16[12,2048]{1,0:T(8,128)(2,1)S(1)}, bf16[12,2048]{1,0:T(8,128)(2,1)S(1)}, u32[]{:S(2)}, u32[]{:S(2)}) %collective-permute-start.1) | collective-permute-done | bytes 49184 | tf_op jit(solution)/shard_map/ppermute | solution.py:349
  13.6 0.1 collective-permute-start.4
  13.7 0.4 collective-permute-start.3
  14.1 0.6 %pad_add_fusion.refs_0_ = s32[2]{0:T(128)} fusion(s32[1]{0:T(128)} %bitcast.1, s32[1]{0:T(128)} %bitcast), kind=kLoop, calls=%fused_computation.16 | loop fusion | flops 2 | bytes 16 | tf_op jit(solution)/shard_map/stack | solution.py:364
  14.7 1.3 %copy.16.offsets = s32[8,2]{1,0:T(8,128)} copy(s32[8,2]{0,1:T(2,128)} %param.17) | data formatting | bytes 128 | tf_op args[4]
  16.1 8.1 %spectra.1 = (bf16[512,4096]{1,0:T(8,128)(2,1)}, bf16[64,2048]{1,0:T(8,128)(2,1)}, bf16[64,2048]{1,0:T(8,128)(2,1)}, bf16[64,2048]{1,0:T(8,128)(2,1)}, bf16[64,2048]{1,0:T(8,128)(2,1)}, /*index=5*/f32[64,128]{1,0:T(8,128)}) custom-call(s32[64]{0:T(128)} %ids.1, bf16[64,4096]{1,0:T(8,128)(2,1)} %images.1, bf16[512,512]{1,0:T(8,128)(2,1)} %constant.41.clone.high, ...), custom_call_target="tpu_custom_call" | custom-call | tf_op jit(solution)/shard_map/spectra/pallas_call | solution.py:178
  24.3 0.5 copy-done.3
  24.8 0.0 copy-done.4
  24.9 0.0 copy-done.5
  24.9 8.1 %classes.1 = (f32[4,16,2048]{2,1,0:T(8,128)}, bf16[4,16,2048]{2,1,0:T(8,128)(2,1)}) custom-call(s32[2]{0:T(128)} %pad_add_fusion.refs_0_, s32[4]{0:T(128)} %refs_1_.1, f32[4]{0:T(128)} %refs_2_.1, bf16[512,4096]{1,0:T(8,128)(2,1)} %get-tuple-element.11.refs_3_, bf16[64,2048]{1,0:T(8,128)(2,1)} %get-tuple-element.12.refs_4_, ...), custom_call_target="tpu_custom_call" | custom-call | tf_op jit(solution)/shard_map/classes/pallas_call | solution.py:299
  33.0 0.1 collective-permute-start.6
  33.1 1.7 %collective-permute-done.6 = bf16[4,16,2048]{2,1,0:T(8,128)(2,1)S(1)} collective-permute-done((bf16[4,16,2048]{2,1,0:T(8,128)(2,1)}, bf16[4,16,2048]{2,1,0:T(8,128)(2,1)S(1)}, u32[]{:S(2)}, u32[]{:S(2)}) %collective-permute-start.6) | collective-permute-done | bytes 262176 | tf_op jit(solution)/shard_map/ppermute | solution.py:349
  34.8 1.1 %fusion.6 = (bf16[4,16,2048]{2,1,0:T(8,128)(2,1)S(1)}, f32[4,16,2048]{2,1,0:T(8,128)S(1)}) fusion(f32[4,16,2048]{2,1,0:T(8,128)} %get-tuple-element.17, bf16[4,16,2048]{2,1,0:T(8,128)(2,1)S(1)} %collective-permute-done.6), kind=kLoop, calls=%fused_computation.18 | loop fusion | flops 393216 | bytes 1572864 | tf_op jit(solution)/shard_map/convert.2
  35.9 1.1 %collective-permute-start.7 = (bf16[16,2048]{1,0:T(8,128)(2,1)S(1)}, bf16[16,2048]{1,0:T(8,128)(2,1)S(1)}, u32[]{:S(2)}, u32[]{:S(2)}) collective-permute-start(bf16[16,2048]{1,0:T(8,128)(2,1)S(1)} %get-tuple-element.26), channel_id=1, source_target_pairs={{0,16},{1,17},{2,18},{3,19},{4,20},{5,21},{6,22},{7,23},{8,24},{9,... | collective-permute-start | bytes 196616 | tf_op jit(solution)/shard_map/ppermute | solution.py:349
  37.0 0.6 %collective-permute-start.9 = (bf16[16,2048]{1,0:T(8,128)(2,1)S(1)}, bf16[16,2048]{1,0:T(8,128)(2,1)S(1)}, u32[]{:S(2)}, u32[]{:S(2)}) collective-permute-start(bf16[16,2048]{1,0:T(8,128)(2,1)S(1)} %get-tuple-element.27), channel_id=1, source_target_pairs={{0,9},{1,8},{2,11},{3,10},{4,13},{5,12},{6,15},{7,14},{8,17},{9,16... | collective-permute-start | bytes 196616 | tf_op jit(solution)/shard_map/ppermute | solution.py:349
  37.7 2.9 %collective-permute-start.8 = (bf16[16,2048]{1,0:T(8,128)(2,1)S(1)}, bf16[16,2048]{1,0:T(8,128)(2,1)S(1)}, u32[]{:S(2)}, u32[]{:S(2)}) collective-permute-start(bf16[16,2048]{1,0:T(8,128)(2,1)S(1)} %get-tuple-element.28), channel_id=1, source_target_pairs={{0,25},{1,24},{2,27},{3,26},{4,29},{5,28},{6,31},{7,30},{8,1},{9,0... | collective-permute-start | bytes 196616 | tf_op jit(solution)/shard_map/ppermute | solution.py:349
  40.6 2.8 %collective-permute-done.7 = bf16[16,2048]{1,0:T(8,128)(2,1)S(1)} collective-permute-done((bf16[16,2048]{1,0:T(8,128)(2,1)S(1)}, bf16[16,2048]{1,0:T(8,128)(2,1)S(1)}, u32[]{:S(2)}, u32[]{:S(2)}) %collective-permute-start.7) | collective-permute-done | bytes 65568 | tf_op jit(solution)/shard_map/ppermute | solution.py:349
  43.3 1.3 %collective-permute-done.8 = bf16[16,2048]{1,0:T(8,128)(2,1)S(1)} collective-permute-done((bf16[16,2048]{1,0:T(8,128)(2,1)S(1)}, bf16[16,2048]{1,0:T(8,128)(2,1)S(1)}, u32[]{:S(2)}, u32[]{:S(2)}) %collective-permute-start.8) | collective-permute-done | bytes 65568 | tf_op jit(solution)/shard_map/ppermute | solution.py:349
  44.7 1.3 %collective-permute-start.10 = (bf16[16,2048]{1,0:T(8,128)(2,1)S(1)}, bf16[16,2048]{1,0:T(8,128)(2,1)S(1)}, u32[]{:S(2)}, u32[]{:S(2)}) collective-permute-start(bf16[16,2048]{1,0:T(8,128)(2,1)S(1)} %get-tuple-element.22), channel_id=1, source_target_pairs={{0,3},{1,2},{2,1},{3,0},{4,7},{5,6},{6,5},{7,4},{8,11},{9,10},{10,... | collective-permute-start | bytes 196616 | tf_op jit(solution)/shard_map/ppermute | solution.py:349
  46.0 2.9 %collective-permute-done.10 = bf16[16,2048]{1,0:T(8,128)(2,1)S(1)} collective-permute-done((bf16[16,2048]{1,0:T(8,128)(2,1)S(1)}, bf16[16,2048]{1,0:T(8,128)(2,1)S(1)}, u32[]{:S(2)}, u32[]{:S(2)}) %collective-permute-start.10) | collective-permute-done | bytes 65568 | tf_op jit(solution)/shard_map/ppermute | solution.py:349
  48.9 1.3 %collective-permute-start.11 = (bf16[16,2048]{1,0:T(8,128)(2,1)S(1)}, bf16[16,2048]{1,0:T(8,128)(2,1)S(1)}, u32[]{:S(2)}, u32[]{:S(2)}) collective-permute-start(bf16[16,2048]{1,0:T(8,128)(2,1)S(1)} %fusion.2), channel_id=1, source_target_pairs={{0,5},{1,4},{2,7},{3,6},{4,1},{5,0},{6,3},{7,2},{8,13},{9,12},{10,... | collective-permute-start | bytes 196616 | tf_op jit(solution)/shard_map/ppermute | solution.py:349
  50.2 2.9 %collective-permute-done.11 = bf16[16,2048]{1,0:T(8,128)(2,1)S(1)} collective-permute-done((bf16[16,2048]{1,0:T(8,128)(2,1)S(1)}, bf16[16,2048]{1,0:T(8,128)(2,1)S(1)}, u32[]{:S(2)}, u32[]{:S(2)}) %collective-permute-start.11) | collective-permute-done | bytes 65568 | tf_op jit(solution)/shard_map/ppermute | solution.py:349
  53.0 0.2 collective-permute-start.12
  53.2 1.2 %collective-permute-done.12 = f32[16,2048]{1,0:T(8,128)S(1)} collective-permute-done((f32[16,2048]{1,0:T(8,128)S(1)}, f32[16,2048]{1,0:T(8,128)S(1)}, u32[]{:S(2)}, u32[]{:S(2)}) %collective-permute-start.12) | collective-permute-done | bytes 131104 | tf_op jit(solution)/shard_map/ppermute | solution.py:349
  54.5 0.6 %slice.42 = f32[1,2048]{1,0:T(1,128)} slice(f32[16,2048]{1,0:T(8,128)S(1)} %broadcast_select_fusion), slice={[12:13], [0:2048]} | slice | bytes 16384 | tf_op jit(solution)/shard_map/slice | solution.py:380
  55.1 0.6 %fusion.3 = f32[]{:T(128)} fusion(f32[1,128]{1,0:T(1,128)S(1)} %copy-done.6, f32[16,2048]{1,0:T(8,128)S(1)} %broadcast_select_fusion), kind=kLoop, calls=%fused_computation.15 | loop fusion | flops 255 | bytes 1028 | tf_op jit(solution)/shard_map/reduce_sum | solution.py:385
  55.7 0.9 %copy.17 = f32[1,12,4096]{2,0,1:T(1,128)} copy(f32[1,12,4096]{2,1,0:T(8,128)S(1)} %maximum_bitcast_fusion) | data formatting | bytes 393216
  (24 shorter events, 0.2 us)
Async XLA Ops:
  1.5 7.0 %collective-permute-start.2 = (bf16[12,2048]{1,0:T(8,128)(2,1)S(1)}, bf16[12,2048]{1,0:T(8,128)(2,1)S(1)}, u32[]{:S(2)}, u32[]{:S(2)}) collective-permute-start(bf16[12,2048]{1,0:T(8,128)(2,1)S(1)} %dynamic-slice_bitcast_fusion), channel_id=1, source_target_pairs={{0,25},{1,24},{2,27},{3,26},{4,29},{5,28},{6,31},{7,30},{8,1},{9,0... | collective-permute-start | bytes 147464 | tf_op jit(solution)/shard_map/ppermute | solution.py:349
  6.0 7.6 %collective-permute-start.1 = (bf16[12,2048]{1,0:T(8,128)(2,1)S(1)}, bf16[12,2048]{1,0:T(8,128)(2,1)S(1)}, u32[]{:S(2)}, u32[]{:S(2)}) collective-permute-start(bf16[12,2048]{1,0:T(8,128)(2,1)S(1)} %dynamic-slice_bitcast_fusion), channel_id=1, source_target_pairs={{0,16},{1,17},{2,18},{3,19},{4,20},{5,21},{6,22},{7,23},{8,24},{9,... | collective-permute-start | bytes 147464 | tf_op jit(solution)/shard_map/ppermute | solution.py:349
  6.0 7.7 %collective-permute-start = (bf16[12,2048]{1,0:T(8,128)(2,1)S(1)}, bf16[12,2048]{1,0:T(8,128)(2,1)S(1)}, u32[]{:S(2)}, u32[]{:S(2)}) collective-permute-start(bf16[12,2048]{1,0:T(8,128)(2,1)S(1)} %dynamic-slice_bitcast_fusion), channel_id=1, source_target_pairs={{0,9},{1,8},{2,11},{3,10},{4,13},{5,12},{6,15},{7,14},{8,17},{9,16... | collective-permute-start | bytes 147464 | tf_op jit(solution)/shard_map/ppermute | solution.py:349
  8.5 15.7 %copy-start = (bf16[12,2048]{1,0:T(8,128)(2,1)}, bf16[12,2048]{1,0:T(8,128)(2,1)S(1)}, u32[]{:S(2)}) copy-start(bf16[12,2048]{1,0:T(8,128)(2,1)S(1)} %collective-permute-done.2.refs_12_) | copy-start | bytes 147460
  8.6 15.7 %collective-permute-start.5 = (bf16[12,2048]{1,0:T(8,128)(2,1)S(1)}, bf16[12,2048]{1,0:T(8,128)(2,1)S(1)}, u32[]{:S(2)}, u32[]{:S(2)}) collective-permute-start(bf16[12,2048]{1,0:T(8,128)(2,1)S(1)} %collective-permute-done.2.refs_12_), channel_id=1, source_target_pairs={{0,1},{1,0},{2,3},{3,2},{4,5},{5,4},{6,7},{7,6},{8,9},{9,8},{10,11... | collective-permute-start | bytes 147464 | tf_op jit(solution)/shard_map/ppermute | solution.py:349
  13.6 10.7 %copy-start.1 = (bf16[12,2048]{1,0:T(8,128)(2,1)}, bf16[12,2048]{1,0:T(8,128)(2,1)S(1)}, u32[]{:S(2)}) copy-start(bf16[12,2048]{1,0:T(8,128)(2,1)S(1)} %collective-permute-done.1.refs_11_) | copy-start | bytes 147460
  13.6 10.6 %collective-permute-start.4 = (bf16[12,2048]{1,0:T(8,128)(2,1)S(1)}, bf16[12,2048]{1,0:T(8,128)(2,1)S(1)}, u32[]{:S(2)}, u32[]{:S(2)}) collective-permute-start(bf16[12,2048]{1,0:T(8,128)(2,1)S(1)} %collective-permute-done.1.refs_11_), channel_id=1, source_target_pairs={{0,1},{1,0},{2,3},{3,2},{4,5},{5,4},{6,7},{7,6},{8,9},{9,8},{10,11... | collective-permute-start | bytes 147464 | tf_op jit(solution)/shard_map/ppermute | solution.py:349
  13.7 10.6 %copy-start.2 = (bf16[12,2048]{1,0:T(8,128)(2,1)}, bf16[12,2048]{1,0:T(8,128)(2,1)S(1)}, u32[]{:S(2)}) copy-start(bf16[12,2048]{1,0:T(8,128)(2,1)S(1)} %collective-permute-done.refs_10_) | copy-start | bytes 147460
  13.7 10.5 %collective-permute-start.3 = (bf16[12,2048]{1,0:T(8,128)(2,1)S(1)}, bf16[12,2048]{1,0:T(8,128)(2,1)S(1)}, u32[]{:S(2)}, u32[]{:S(2)}) collective-permute-start(bf16[12,2048]{1,0:T(8,128)(2,1)S(1)} %collective-permute-done.refs_10_), channel_id=1, source_target_pairs={{0,1},{1,0},{2,3},{3,2},{4,5},{5,4},{6,7},{7,6},{8,9},{9,8},{10,11... | collective-permute-start | bytes 147464 | tf_op jit(solution)/shard_map/ppermute | solution.py:349
  24.2 0.6 %copy-start.3 = (bf16[12,2048]{1,0:T(8,128)(2,1)}, bf16[12,2048]{1,0:T(8,128)(2,1)S(1)}, u32[]{:S(2)}) copy-start(bf16[12,2048]{1,0:T(8,128)(2,1)S(1)} %collective-permute-done.5.refs_15_) | copy-start | bytes 147460
  24.2 0.6 %copy-start.4 = (bf16[12,2048]{1,0:T(8,128)(2,1)}, bf16[12,2048]{1,0:T(8,128)(2,1)S(1)}, u32[]{:S(2)}) copy-start(bf16[12,2048]{1,0:T(8,128)(2,1)S(1)} %collective-permute-done.4.refs_14_) | copy-start | bytes 147460
  24.3 0.6 %copy-start.5 = (bf16[12,2048]{1,0:T(8,128)(2,1)}, bf16[12,2048]{1,0:T(8,128)(2,1)S(1)}, u32[]{:S(2)}) copy-start(bf16[12,2048]{1,0:T(8,128)(2,1)S(1)} %collective-permute-done.3.refs_13_) | copy-start | bytes 147460
  24.9 30.2 %copy-start.6 = (f32[1,128]{1,0:T(1,128)S(1)}, f32[1,128]{1,0:T(1,128)}, u32[]{:S(2)}) copy-start(f32[1,128]{1,0:T(1,128)} %constant.47) | copy-start | bytes 1540
  33.0 1.7 %collective-permute-start.6 = (bf16[4,16,2048]{2,1,0:T(8,128)(2,1)}, bf16[4,16,2048]{2,1,0:T(8,128)(2,1)S(1)}, u32[]{:S(2)}, u32[]{:S(2)}) collective-permute-start(bf16[4,16,2048]{2,1,0:T(8,128)(2,1)} %get-tuple-element.18), channel_id=1, source_target_pairs={{0,1},{1,0},{2,3},{3,2},{4,5},{5,4},{6,7},{7,6},{8,9},{9,8},{10,11... | collective-permute-start | bytes 786440 | tf_op jit(solution)/shard_map/ppermute | solution.py:349
  35.9 7.4 %collective-permute-start.7 = (bf16[16,2048]{1,0:T(8,128)(2,1)S(1)}, bf16[16,2048]{1,0:T(8,128)(2,1)S(1)}, u32[]{:S(2)}, u32[]{:S(2)}) collective-permute-start(bf16[16,2048]{1,0:T(8,128)(2,1)S(1)} %get-tuple-element.26), channel_id=1, source_target_pairs={{0,16},{1,17},{2,18},{3,19},{4,20},{5,21},{6,22},{7,23},{8,24},{9,... | collective-permute-start | bytes 196616 | tf_op jit(solution)/shard_map/ppermute | solution.py:349
  37.0 6.3 %collective-permute-start.9 = (bf16[16,2048]{1,0:T(8,128)(2,1)S(1)}, bf16[16,2048]{1,0:T(8,128)(2,1)S(1)}, u32[]{:S(2)}, u32[]{:S(2)}) collective-permute-start(bf16[16,2048]{1,0:T(8,128)(2,1)S(1)} %get-tuple-element.27), channel_id=1, source_target_pairs={{0,9},{1,8},{2,11},{3,10},{4,13},{5,12},{6,15},{7,14},{8,17},{9,16... | collective-permute-start | bytes 196616 | tf_op jit(solution)/shard_map/ppermute | solution.py:349
  37.7 7.0 %collective-permute-start.8 = (bf16[16,2048]{1,0:T(8,128)(2,1)S(1)}, bf16[16,2048]{1,0:T(8,128)(2,1)S(1)}, u32[]{:S(2)}, u32[]{:S(2)}) collective-permute-start(bf16[16,2048]{1,0:T(8,128)(2,1)S(1)} %get-tuple-element.28), channel_id=1, source_target_pairs={{0,25},{1,24},{2,27},{3,26},{4,29},{5,28},{6,31},{7,30},{8,1},{9,0... | collective-permute-start | bytes 196616 | tf_op jit(solution)/shard_map/ppermute | solution.py:349
  44.7 4.2 %collective-permute-start.10 = (bf16[16,2048]{1,0:T(8,128)(2,1)S(1)}, bf16[16,2048]{1,0:T(8,128)(2,1)S(1)}, u32[]{:S(2)}, u32[]{:S(2)}) collective-permute-start(bf16[16,2048]{1,0:T(8,128)(2,1)S(1)} %get-tuple-element.22), channel_id=1, source_target_pairs={{0,3},{1,2},{2,1},{3,0},{4,7},{5,6},{6,5},{7,4},{8,11},{9,10},{10,... | collective-permute-start | bytes 196616 | tf_op jit(solution)/shard_map/ppermute | solution.py:349
  48.9 4.2 %collective-permute-start.11 = (bf16[16,2048]{1,0:T(8,128)(2,1)S(1)}, bf16[16,2048]{1,0:T(8,128)(2,1)S(1)}, u32[]{:S(2)}, u32[]{:S(2)}) collective-permute-start(bf16[16,2048]{1,0:T(8,128)(2,1)S(1)} %fusion.2), channel_id=1, source_target_pairs={{0,5},{1,4},{2,7},{3,6},{4,1},{5,0},{6,3},{7,2},{8,13},{9,12},{10,... | collective-permute-start | bytes 196616 | tf_op jit(solution)/shard_map/ppermute | solution.py:349
  53.0 1.4 %collective-permute-start.12 = (f32[16,2048]{1,0:T(8,128)S(1)}, f32[16,2048]{1,0:T(8,128)S(1)}, u32[]{:S(2)}, u32[]{:S(2)}) collective-permute-start(f32[16,2048]{1,0:T(8,128)S(1)} %convert_add_fusion.1), channel_id=1, source_target_pairs={{0,1},{1,0},{2,3},{3,2},{4,5},{5,4},{6,7},{7,6},{8,9},{9,8},{10,11... | collective-permute-start | bytes 393224 | tf_op jit(solution)/shard_map/ppermute | solution.py:349

commit v2 on v1

--- a/solution.py
+++ b/solution.py
@@ -76,10 +76,20 @@
 
 
 def spectra_body(
+    ids_far, images_far, high_far, low_far, twiddle_far, wave_far, offsets_far, ctf_far, noise_far,
+    rotated, square_high, square_low, power_high, power_low, data_power,
     ids, images, high, low, twiddle, wave, offsets, ctf, noise,
-    rotated, square_high, square_low, power_high, power_low, data_power,
-    stacked, partial, rows, w_real, w_imag, cosine, sine, inverse, total,
+    stacked, partial, rows, w_real, w_imag, cosine, sine, inverse, total, arrived,
 ):
+    copies = [
+        pltpu.make_async_copy(far, near, arrived.at[j])
+        for j, (far, near) in enumerate((
+            (images_far, images), (high_far, high), (low_far, low), (offsets_far, offsets), (wave_far, wave),
+            (noise_far, noise), (ids_far, ids), (ctf_far, ctf), (twiddle_far, twiddle),
+        ))
+    ]
+    for copy in copies:
+        copy.start()
     count, pixels = images.shape
     side = math.isqrt(pixels)
     half = side // 2
@@ -87,10 +97,12 @@
     outer = side // fold
     per_row = LANES // side
     groups = outer // per_row
-    shifts = offsets.shape[0]
+    shifts = offsets.shape[1]
     columns = noise.shape[1] // LANES
     width = noise.shape[1]
 
+    for copy in copies[:6]:
+        copy.wait()
     for m in range(groups):
         for y in range(fold):
             source = (m + groups * y) * LANES
@@ -99,6 +111,8 @@
     partial[...] += jnp.dot(stacked[...], low[...], preferred_element_type=F32)
 
     inverse[...] = 1.0 / noise[...]
+    for copy in copies[6:]:
+        copy.wait()
 
     def fetch(p, carry):
         rows[pl.ds(p, 1), :] = ctf[pl.ds(ids[p], 1), :]
@@ -107,8 +121,12 @@
     lax.fori_loop(0, count, fetch, 0, unroll=8)
 
     lane = lax.broadcasted_iota(jnp.int32, (shifts, LANES), 1)
-    step_u = offsets[:, 0:1]
-    step_v = offsets[:, 1:2]
+    shift = lax.broadcasted_iota(jnp.int32, (shifts, LANES), 0)
+    step_u = jnp.zeros((shifts, LANES), jnp.int32)
+    step_v = jnp.zeros((shifts, LANES), jnp.int32)
+    for s in range(shifts):
+        step_u = jnp.where(shift == s, offsets[0, s], step_u)
+        step_v = jnp.where(shift == s, offsets[1, s], step_v)
     for column in range(columns):
         u = lane // half + fold * column
         turn = (u * step_u + (lane % half) * step_v) & (side - 1)
@@ -171,16 +189,27 @@
     shifts = shift_offsets.shape[0]
     high, low, twiddle, wave = dft_tables(side)
     vmem = pl.BlockSpec(memory_space=pltpu.VMEM)
-    shape = jax.ShapeDtypeStruct
+    far = pl.BlockSpec(memory_space=pltpu.HBM)
+    shape = pltpu.VMEM
     plane = shape((count, width), BF16)
     k = high.shape[0]
     groups = pixels // k
     return pl.pallas_call(
         spectra_body,
         out_shape=(shape((shifts * count, 2 * width), BF16), plane, plane, plane, plane, shape((count, LANES), F32)),
-        in_specs=[pl.BlockSpec(memory_space=pltpu.SMEM)] + [vmem] * 8,
+        cost_estimate=pl.CostEstimate(flops=2**32, transcendentals=0, bytes_accessed=2**23),
+        in_specs=[far] * 9,
         out_specs=(vmem,) * 6,
         scratch_shapes=[
+            pltpu.SMEM(group_ids.shape, jnp.int32),
+            pltpu.VMEM(particles.shape, particles.dtype),
+            pltpu.VMEM(high.shape, BF16),
+            pltpu.VMEM(low.shape, BF16),
+            pltpu.VMEM(twiddle.shape, F32),
+            pltpu.VMEM(wave.shape, F32),
+            pltpu.SMEM(shift_offsets.shape[::-1], jnp.int32),
+            pltpu.VMEM(ctf_table.shape, F32),
+            pltpu.VMEM((1, width), F32),
             pltpu.VMEM((groups * count, k), BF16),
             pltpu.VMEM((groups * count, high.shape[1]), F32),
             pltpu.VMEM((count, width), F32),
@@ -190,12 +219,17 @@
             pltpu.VMEM((shifts, width), F32),
             pltpu.VMEM((1, width), F32),
             pltpu.VMEM((count, LANES), F32),
+            pltpu.SemaphoreType.DMA((9,)),
         ],
+        compiler_params=pltpu.CompilerParams(vmem_limit_bytes=24 * 2**20),
         name="spectra",
-    )(
-        group_ids, particles, jnp.asarray(high), jnp.asarray(low), jnp.asarray(twiddle), jnp.asarray(wave),
-        shift_offsets, ctf_table, noise_power.reshape(1, width),
-    )
+    )(*(
+        pltpu.with_memory_space_constraint(x, pltpu.HBM)
+        for x in (
+            group_ids, particles, jnp.asarray(high), jnp.asarray(low), jnp.asarray(twiddle), jnp.asarray(wave),
+            shift_offsets.T, ctf_table, noise_power.reshape(1, width),
+        )
+    ))
 
 
 def dot_rows(a, b):
@@ -208,17 +242,17 @@
 
 def classes_body(digit_bits, classes, *refs):
     others = classes - 1
-    place, slots, priors = refs[:3]
-    rotated, square_high, square_low, power_high, power_low, data_power, own = refs[3:10]
-    mine = refs[10:10 + others]
-    theirs = refs[10 + others:10 + 2 * others]
-    keep, send, stack, soft, sums, extra = refs[10 + 2 * others:]
+    ring, side, slots, priors = refs[:4]
+    rotated, square_high, square_low, power_high, power_low, data_power, own = refs[4:11]
+    mine = refs[11:11 + others]
+    theirs = refs[11 + others:11 + 2 * others]
+    keep, send, stack, soft, sums, extra = refs[11 + 2 * others:]
     rotations = own.shape[1]
     count = data_power.shape[0]
     shifts = rotated.shape[0] // count
     width = power_high.shape[1]
     lanes = classes * SLOT
-    g, h = place[0], place[1]
+    g, h = ring[0], side[0]
 
     here = pl.ds(pl.multiple_of(h * width, width), width)
     there = pl.ds(pl.multiple_of((1 - h) * width, width), width)
@@ -287,7 +321,7 @@
         send[d, :, :] = jnp.concatenate([sums[rows, there], tail], axis=0).astype(BF16)
 
 
-def classes_call(place, slot_class, log_prior, spectra_out, own, mine, theirs, digit_bits):
+def classes_call(ring, side, slot_class, log_prior, spectra_out, own, mine, theirs, digit_bits):
     classes = len(mine) + 1
     rotated, *_, data_power = spectra_out
     rows, full = rotated.shape
@@ -295,11 +329,12 @@
     lanes = classes * SLOT
     vmem = pl.BlockSpec(memory_space=pltpu.VMEM)
     smem = pl.BlockSpec(memory_space=pltpu.SMEM)
-    shape = jax.ShapeDtypeStruct
+    shape = pltpu.VMEM
+    spectra_out = [pltpu.with_memory_space_constraint(x, pltpu.VMEM) for x in spectra_out]
     return pl.pallas_call(
         functools.partial(classes_body, digit_bits, classes),
         out_shape=(shape((classes, SLOT, width), F32), shape((classes, SLOT, width), BF16)),
-        in_specs=[smem] * 3 + [vmem] * (7 + 2 * len(mine)),
+        in_specs=[smem] * 4 + [vmem] * (7 + 2 * len(mine)),
         out_specs=(vmem, vmem),
         scratch_shapes=[
             pltpu.VMEM((lanes, full), BF16),
@@ -307,8 +342,36 @@
             pltpu.VMEM((lanes, full), F32),
             pltpu.VMEM((LANES, width), F32),
         ],
+        compiler_params=pltpu.CompilerParams(vmem_limit_bytes=24 * 2**20),
         name="classes",
-    )(place, slot_class, log_prior, *spectra_out, own, *mine, *theirs)
+    )(ring, side, slot_class, log_prior, *spectra_out, own, *mine, *theirs)
+
+
+def finish_body(side, owned, other, scale, sums, ctf_power, log_evidence):
+    rotations, _, full = sums.shape
+    width = full // 2
+    h = side[0]
+    here = pl.ds(pl.multiple_of(h * width, width), width)
+    there = pl.ds(pl.multiple_of((1 - h) * width, width), width)
+    sums[:, 0, here] = owned[:rotations, :]
+    sums[:, 0, there] = other[:rotations, :]
+    tail = jnp.where(h == 0, owned[rotations:, :], other[rotations:, :])
+    ctf_power[...] = tail[0:1, :]
+    log_evidence[...] = jnp.sum(tail[1:2, :LANES] * scale[...], axis=1, keepdims=True)
+
+
+def finish(side, owned, other, rotations, scale):
+    width = owned.shape[1]
+    vmem = pl.BlockSpec(memory_space=pltpu.VMEM)
+    shape = jax.ShapeDtypeStruct
+    return pl.pallas_call(
+        finish_body,
+        out_shape=(shape((rotations, 1, 2 * width), F32), shape((1, width), F32), shape((1, 1), F32)),
+        in_specs=[pl.BlockSpec(memory_space=pltpu.SMEM)] + [vmem] * 3,
+        out_specs=(vmem,) * 3,
+        compiler_params=pltpu.CompilerParams(vmem_limit_bytes=8 * 2**20),
+        name="finish",
+    )(side, owned, other, scale)
 
 
 def tree(parts):
@@ -359,10 +422,11 @@
 
     half_stack = lax.dynamic_slice_in_dim(references[0], h * width, width, 1)
     mine = [move(half_stack, shift(d)) for d in range(1, rings)]
+    spectra_out = spectra(group_ids, particles, shift_offsets, ctf_table, noise_power)
+    mine, spectra_out = lax.optimization_barrier((mine, spectra_out))
     theirs = [move(value, swap) for value in mine]
-    spectra_out = spectra(group_ids, particles, shift_offsets, ctf_table, noise_power)
-    place = jnp.stack([g, h]).astype(jnp.int32)
-    keep, send = classes_call(place, slot_class, log_prior, spectra_out, references, mine, theirs, digit_bits)
+    ring, side = g.reshape(1), h.reshape(1)
+    keep, send = classes_call(ring, side, slot_class, log_prior, spectra_out, references, mine, theirs, digit_bits)
 
     pair = keep + move(send, swap).astype(F32)
     gathered = [pair[0]]
@@ -374,16 +438,12 @@
         owned = lax.reduce_precision(owned, 8, 7) + move(low, hop(bit)).astype(F32)
 
     other = move(owned, swap)
-    first = jnp.where(h == 0, owned, other)
-    second = jnp.where(h == 0, other, owned)
-    class_sums = jnp.concatenate([first[:rotations], second[:rotations]], axis=1)[None]
-    ctf_power = first[rotations][None]
-    scale = np.zeros((LANES,), np.float64)
+    scale = np.zeros((1, LANES), np.float64)
     for j in range(-(-31 // digit_bits)):
-        scale[j] = 2.0 ** (j * digit_bits - FIXED)
+        scale[0, j] = 2.0 ** (j * digit_bits - FIXED)
     scale = scale / (count * rings * spread * width)
-    log_evidence = jnp.sum(first[rotations + 1, :LANES] * jnp.asarray(scale, F32))
-    return class_sums, ctf_power, log_evidence
+    sums, ctf_power, log_evidence = finish(side, owned, other, rotations, jnp.asarray(scale, F32))
+    return sums.reshape(1, rotations, 2 * width), ctf_power, log_evidence.reshape(())
 
 
 def solution(mesh):

time: 56.9 us -> 41.6 us (0.73)
  waiting for transfers between devices: 19.2 us -> 14.2 us
  Pallas kernels: 16.2 us -> 11.4 us
  local copies, waits for them, and re-layouts: 4.32 us -> 0.88 us
  other arithmetic: 2.46 us -> 0.15 us
    ppermute x13, waiting for transfers between devices: 19.2 us -> 14.2 us  [move(): return lax.ppermute(value, ('gx', 'gy'), pairs)]
    pallas_call x1, Pallas kernels: 8.11 us -> 5.21 us  [classes_call(): pl.pallas_call(functools.partial(classes_body, digit_bits, classes), out_...]
    unnamed x16 -> x8, local copies, waits for them, and re-layouts: 2.85 us -> 0.02 us
    pallas_call x1, Pallas kernels: 8.13 us -> 5.53 us  [spectra(): pl.pallas_call(spectra_body, out_shape=(shape((shifts * count, 2 * width)...]
    another operation x2 -> x1, other arithmetic: 1.73 us -> 0.07 us
    pallas_call x0 -> x1, Pallas kernels: none -> 0.71 us  [finish(): pl.pallas_call(finish_body, out_shape=(shape((rotations, 1, 2 * width), F...]
    slice x1 -> x0, local copies, waits for them, and re-layouts: 0.61 us -> none  [shards(): ctf_power = first[rotations][None]]
    reduce_sum x1 -> x0, other arithmetic: 0.6 us -> none  [shards(): jnp.sum(first[rotations + 1, :LANES] * jnp.asarray(scale, F32))]
  transfers between devices with their start and end apart: 13 -> 13, of which waited for: 8 -> 9; matrix products, arithmetic and copies ran while one was open for 3% -> 0% of each run, Pallas kernels for 14% -> 13%
where the time goes in v2:
time: 41.6 us; the launch traced here: 41.4 us
  waiting for transfers between devices  14.2 us (34%)
  starting transfers between devices  14 us (34%)
  Pallas kernels  11.4 us (27%)
  local copies, waits for them, and re-layouts  0.88 us (2%)
  between operations  0.73 us (2%)
    ppermute x13, waiting for transfers between devices, move(): return lax.ppermute(value, ('gx', 'gy'), pairs)  14.2 us
    ppermute x13, starting transfers between devices, move(): return lax.ppermute(value, ('gx', 'gy'), pairs)  14 us
    pallas_call x1, Pallas kernels, spectra(): pl.pallas_call(spectra_body, out_shape=(shape((shifts * count, 2 * width)...  5.53 us
    pallas_call x1, Pallas kernels, classes_call(): pl.pallas_call(functools.partial(classes_body, digit_bits, classes), out_...  5.21 us
    dynamic_slice x1, local copies, waits for them, and re-layouts, shards(): half_stack = lax.dynamic_slice_in_dim(references[0], h * width, width, 1)  0.85 us
  transfers between devices with their start and end apart: 13, of which 9 were waited for; matrix products, arithmetic and copies ran while one was open for 0% of the time, Pallas kernels for 13%

profile of v2, /device:TPU:0, one launch (start us, length us, event | category | flops | bytes accessed | tf_op | source)
XLA Modules:
  0.0 41.4 jit_solution(9739697610898693280)
XLA Ops:
  0.7 0.8 %dynamic-slice_bitcast_fusion = bf16[12,2048]{1,0:T(8,128)(2,1)S(1)} fusion(bf16[1,12,4096]{2,1,0:T(8,128)(2,1)} %refs_10_.1, s32[]{:T(128)S(6)} %select_n.9), kind=kLoop, calls=%fused_computation.10 | loop fusion | bytes 98308 | tf_op jit(solution)/shard_map/dynamic_slice | solution.py:423
  1.5 4.5 %collective-permute-start.2 = (bf16[12,2048]{1,0:T(8,128)(2,1)S(1)}, bf16[12,2048]{1,0:T(8,128)(2,1)S(1)}, u32[]{:S(2)}, u32[]{:S(2)}) collective-permute-start(bf16[12,2048]{1,0:T(8,128)(2,1)S(1)} %dynamic-slice_bitcast_fusion), channel_id=1, source_target_pairs={{0,25},{1,24},{2,27},{3,26},{4,29},{5,28},{6,31},{7,30},{8,1},{9,0... | collective-permute-start | bytes 147464 | tf_op jit(solution)/shard_map/ppermute | solution.py:412
  6.0 0.0 collective-permute-start.1
  6.0 1.0 %collective-permute-start = (bf16[12,2048]{1,0:T(8,128)(2,1)S(1)}, bf16[12,2048]{1,0:T(8,128)(2,1)S(1)}, u32[]{:S(2)}, u32[]{:S(2)}) collective-permute-start(bf16[12,2048]{1,0:T(8,128)(2,1)S(1)} %dynamic-slice_bitcast_fusion), channel_id=1, source_target_pairs={{0,9},{1,8},{2,11},{3,10},{4,13},{5,12},{6,15},{7,14},{8,17},{9,16... | collective-permute-start | bytes 147464 | tf_op jit(solution)/shard_map/ppermute | solution.py:412
  7.0 5.5 %spectra.1 = (bf16[512,4096]{1,0:T(8,128)(2,1)S(1)}, bf16[64,2048]{1,0:T(8,128)(2,1)S(1)}, bf16[64,2048]{1,0:T(8,128)(2,1)S(1)}, bf16[64,2048]{1,0:T(8,128)(2,1)...) custom-call(s32[64]{0:T(128)} %ids_far.1, bf16[64,4096]{1,0:T(8,128)(2,1)} %images_far.1, ...), custom_call_target="tpu_custom_call" | custom-call | flops 4294967296 | bytes 8388608 | tf_op jit(solution)/shard_map/spectra/pallas_call | solution.py:197
  12.6 0.0 collective-permute-done.2.refs_13_
  12.6 1.0 %collective-permute-done.1.refs_12_ = bf16[12,2048]{1,0:T(8,128)(2,1)S(1)} collective-permute-done((bf16[12,2048]{1,0:T(8,128)(2,1)S(1)}, bf16[12,2048]{1,0:T(8,128)(2,1)S(1)}, u32[]{:S(2)}, u32[]{:S(2)}) %collective-permute-start.1) | collective-permute-done | bytes 49184 | tf_op jit(solution)/shard_map/ppermute | solution.py:412
  13.6 0.0 collective-permute-done.refs_11_
  13.6 0.1 collective-permute-start.3
  13.7 0.4 %collective-permute-start.4 = (bf16[12,2048]{1,0:T(8,128)(2,1)S(1)}, bf16[12,2048]{1,0:T(8,128)(2,1)S(1)}, u32[]{:S(2)}, u32[]{:S(2)}) collective-permute-start(bf16[12,2048]{1,0:T(8,128)(2,1)S(1)} %collective-permute-done.1.refs_12_), channel_id=1, source_target_pairs={{0,1},{1,0},{2,3},{3,2},{4,5},{5,4},{6,7},{7,6},{8,9},{9,8},{10,11... | collective-permute-start | bytes 147464 | tf_op jit(solution)/shard_map/ppermute | solution.py:412
  14.1 0.1 collective-permute-start.5
  14.2 0.7 %collective-permute-done.3.refs_14_ = bf16[12,2048]{1,0:T(8,128)(2,1)S(1)} collective-permute-done((bf16[12,2048]{1,0:T(8,128)(2,1)S(1)}, bf16[12,2048]{1,0:T(8,128)(2,1)S(1)}, u32[]{:S(2)}, u32[]{:S(2)}) %collective-permute-start.3) | collective-permute-done | bytes 49184 | tf_op jit(solution)/shard_map/ppermute | solution.py:412
  14.9 0.2 collective-permute-done.4.refs_15_
  15.0 0.4 collective-permute-done.5.refs_16_
  15.4 0.0 copy-start.1
  15.4 5.2 %classes.1 = (f32[4,16,2048]{2,1,0:T(8,128)S(1)}, bf16[4,16,2048]{2,1,0:T(8,128)(2,1)S(1)}) custom-call(s32[1]{0:T(128)} %bitcast.1.refs_0_, s32[1]{0:T(128)} %bitcast.refs_1_.side, s32[4]{0:T(128)S(1)} %copy-done.2, f32[4]{0:T(128)S(1)} %copy-done.3, bf16[512,4096]{1,0:T(8,128)(2,1)S(1)} %get-tuple-element.29.refs_4_, ...), custom_call_target="tpu_custom_call" | custom-call | tf_op jit(solution)/shard_map/classes/pallas_call | solution.py:334
  20.6 0.2 collective-permute-start.6
  20.8 1.4 %collective-permute-done.6 = bf16[4,16,2048]{2,1,0:T(8,128)(2,1)S(1)} collective-permute-done((bf16[4,16,2048]{2,1,0:T(8,128)(2,1)S(1)}, bf16[4,16,2048]{2,1,0:T(8,128)(2,1)S(1)}, u32[]{:S(2)}, u32[]{:S(2)}) %collective-permute-start.6) | collective-permute-done | bytes 262176 | tf_op jit(solution)/shard_map/ppermute | solution.py:412
  22.2 0.1 fusion.5
  22.3 1.4 %collective-permute-start.7 = (bf16[16,2048]{1,0:T(8,128)(2,1)S(1)}, bf16[16,2048]{1,0:T(8,128)(2,1)S(1)}, u32[]{:S(2)}, u32[]{:S(2)}) collective-permute-start(bf16[16,2048]{1,0:T(8,128)(2,1)S(1)} %get-tuple-element.47), channel_id=1, source_target_pairs={{0,16},{1,17},{2,18},{3,19},{4,20},{5,21},{6,22},{7,23},{8,24},{9,... | collective-permute-start | bytes 196616 | tf_op jit(solution)/shard_map/ppermute | solution.py:412
  23.7 0.9 %collective-permute-start.9 = (bf16[16,2048]{1,0:T(8,128)(2,1)S(1)}, bf16[16,2048]{1,0:T(8,128)(2,1)S(1)}, u32[]{:S(2)}, u32[]{:S(2)}) collective-permute-start(bf16[16,2048]{1,0:T(8,128)(2,1)S(1)} %get-tuple-element.48), channel_id=1, source_target_pairs={{0,9},{1,8},{2,11},{3,10},{4,13},{5,12},{6,15},{7,14},{8,17},{9,16... | collective-permute-start | bytes 196616 | tf_op jit(solution)/shard_map/ppermute | solution.py:412
  24.6 2.7 %collective-permute-start.8 = (bf16[16,2048]{1,0:T(8,128)(2,1)S(1)}, bf16[16,2048]{1,0:T(8,128)(2,1)S(1)}, u32[]{:S(2)}, u32[]{:S(2)}) collective-permute-start(bf16[16,2048]{1,0:T(8,128)(2,1)S(1)} %get-tuple-element.49), channel_id=1, source_target_pairs={{0,25},{1,24},{2,27},{3,26},{4,29},{5,28},{6,31},{7,30},{8,1},{9,0... | collective-permute-start | bytes 196616 | tf_op jit(solution)/shard_map/ppermute | solution.py:412
  27.3 3.6 %collective-permute-done.7 = bf16[16,2048]{1,0:T(8,128)(2,1)S(1)} collective-permute-done((bf16[16,2048]{1,0:T(8,128)(2,1)S(1)}, bf16[16,2048]{1,0:T(8,128)(2,1)S(1)}, u32[]{:S(2)}, u32[]{:S(2)}) %collective-permute-start.7) | collective-permute-done | bytes 65568 | tf_op jit(solution)/shard_map/ppermute | solution.py:412
  30.8 0.0 collective-permute-done.9
  30.8 0.0 collective-permute-done.8
  30.9 1.3 %collective-permute-start.10 = (bf16[16,2048]{1,0:T(8,128)(2,1)S(1)}, bf16[16,2048]{1,0:T(8,128)(2,1)S(1)}, u32[]{:S(2)}, u32[]{:S(2)}) collective-permute-start(bf16[16,2048]{1,0:T(8,128)(2,1)S(1)} %get-tuple-element.43), channel_id=1, source_target_pairs={{0,3},{1,2},{2,1},{3,0},{4,7},{5,6},{6,5},{7,4},{8,11},{9,10},{10,... | collective-permute-start | bytes 196616 | tf_op jit(solution)/shard_map/ppermute | solution.py:412
  32.2 2.9 %collective-permute-done.10 = bf16[16,2048]{1,0:T(8,128)(2,1)S(1)} collective-permute-done((bf16[16,2048]{1,0:T(8,128)(2,1)S(1)}, bf16[16,2048]{1,0:T(8,128)(2,1)S(1)}, u32[]{:S(2)}, u32[]{:S(2)}) %collective-permute-start.10) | collective-permute-done | bytes 65568 | tf_op jit(solution)/shard_map/ppermute | solution.py:412
  35.1 1.3 %collective-permute-start.11 = (bf16[16,2048]{1,0:T(8,128)(2,1)S(1)}, bf16[16,2048]{1,0:T(8,128)(2,1)S(1)}, u32[]{:S(2)}, u32[]{:S(2)}) collective-permute-start(bf16[16,2048]{1,0:T(8,128)(2,1)S(1)} %fusion.2), channel_id=1, source_target_pairs={{0,5},{1,4},{2,7},{3,6},{4,1},{5,0},{6,3},{7,2},{8,13},{9,12},{10,... | collective-permute-start | bytes 196616 | tf_op jit(solution)/shard_map/ppermute | solution.py:412
  36.4 2.9 %collective-permute-done.11 = bf16[16,2048]{1,0:T(8,128)(2,1)S(1)} collective-permute-done((bf16[16,2048]{1,0:T(8,128)(2,1)S(1)}, bf16[16,2048]{1,0:T(8,128)(2,1)S(1)}, u32[]{:S(2)}, u32[]{:S(2)}) %collective-permute-start.11) | collective-permute-done | bytes 65568 | tf_op jit(solution)/shard_map/ppermute | solution.py:412
  39.3 0.2 collective-permute-start.12
  39.5 1.2 %collective-permute-done.12.other = f32[16,2048]{1,0:T(8,128)S(1)} collective-permute-done((f32[16,2048]{1,0:T(8,128)S(1)}, f32[16,2048]{1,0:T(8,128)S(1)}, u32[]{:S(2)}, u32[]{:S(2)}) %collective-permute-start.12) | collective-permute-done | bytes 131104 | tf_op jit(solution)/shard_map/ppermute | solution.py:412
  40.7 0.7 %finish.1 = (f32[12,1,4096]{2,1,0:T(1,128)}, f32[1,2048]{1,0:T(1,128)}, f32[1,1]{1,0:T(1,128)}) custom-call(s32[1]{0:T(128)} %bitcast.refs_1_.side, f32[16,2048]{1,0:T(8,128)S(1)} %convert_add_fusion.1.owned, f32[16,2048]{1,0:T(8,128)S(1)} %collective-permute-done.12.other, f32[1,128]{1,0:T(1,128)S(1)} %copy-done.1), custom_call_target="tpu_custom_call" | custom-call | tf_op jit(solution)/shard_map/finish/pallas_call | solution.py:367
  (11 shorter events, 0.1 us)
Async XLA Ops:
  1.5 11.1 %collective-permute-start.2 = (bf16[12,2048]{1,0:T(8,128)(2,1)S(1)}, bf16[12,2048]{1,0:T(8,128)(2,1)S(1)}, u32[]{:S(2)}, u32[]{:S(2)}) collective-permute-start(bf16[12,2048]{1,0:T(8,128)(2,1)S(1)} %dynamic-slice_bitcast_fusion), channel_id=1, source_target_pairs={{0,25},{1,24},{2,27},{3,26},{4,29},{5,28},{6,31},{7,30},{8,1},{9,0... | collective-permute-start | bytes 147464 | tf_op jit(solution)/shard_map/ppermute | solution.py:412
  6.0 7.6 %collective-permute-start.1 = (bf16[12,2048]{1,0:T(8,128)(2,1)S(1)}, bf16[12,2048]{1,0:T(8,128)(2,1)S(1)}, u32[]{:S(2)}, u32[]{:S(2)}) collective-permute-start(bf16[12,2048]{1,0:T(8,128)(2,1)S(1)} %dynamic-slice_bitcast_fusion), channel_id=1, source_target_pairs={{0,16},{1,17},{2,18},{3,19},{4,20},{5,21},{6,22},{7,23},{8,24},{9,... | collective-permute-start | bytes 147464 | tf_op jit(solution)/shard_map/ppermute | solution.py:412
  6.0 7.6 %collective-permute-start = (bf16[12,2048]{1,0:T(8,128)(2,1)S(1)}, bf16[12,2048]{1,0:T(8,128)(2,1)S(1)}, u32[]{:S(2)}, u32[]{:S(2)}) collective-permute-start(bf16[12,2048]{1,0:T(8,128)(2,1)S(1)} %dynamic-slice_bitcast_fusion), channel_id=1, source_target_pairs={{0,9},{1,8},{2,11},{3,10},{4,13},{5,12},{6,15},{7,14},{8,17},{9,16... | collective-permute-start | bytes 147464 | tf_op jit(solution)/shard_map/ppermute | solution.py:412
  7.0 8.3 %copy-start = (bf16[1,12,4096]{2,1,0:T(8,128)(2,1)S(1)}, bf16[1,12,4096]{2,1,0:T(8,128)(2,1)}, u32[]{:S(2)}) copy-start(bf16[1,12,4096]{2,1,0:T(8,128)(2,1)} %refs_10_.1) | copy-start | bytes 294916
  7.0 8.3 %copy-start.2 = (s32[4]{0:T(128)S(1)}, s32[4]{0:T(128)}, u32[]{:S(2)}) copy-start(s32[4]{0:T(128)} %refs_2_.1) | copy-start | bytes 52
  7.0 8.3 %copy-start.3 = (f32[4]{0:T(128)S(1)}, f32[4]{0:T(128)}, u32[]{:S(2)}) copy-start(f32[4]{0:T(128)} %refs_3_.1) | copy-start | bytes 52
  13.6 1.3 %collective-permute-start.3 = (bf16[12,2048]{1,0:T(8,128)(2,1)S(1)}, bf16[12,2048]{1,0:T(8,128)(2,1)S(1)}, u32[]{:S(2)}, u32[]{:S(2)}) collective-permute-start(bf16[12,2048]{1,0:T(8,128)(2,1)S(1)} %collective-permute-done.refs_11_), channel_id=1, source_target_pairs={{0,1},{1,0},{2,3},{3,2},{4,5},{5,4},{6,7},{7,6},{8,9},{9,8},{10,11... | collective-permute-start | bytes 147464 | tf_op jit(solution)/shard_map/ppermute | solution.py:412
  13.7 1.3 %collective-permute-start.4 = (bf16[12,2048]{1,0:T(8,128)(2,1)S(1)}, bf16[12,2048]{1,0:T(8,128)(2,1)S(1)}, u32[]{:S(2)}, u32[]{:S(2)}) collective-permute-start(bf16[12,2048]{1,0:T(8,128)(2,1)S(1)} %collective-permute-done.1.refs_12_), channel_id=1, source_target_pairs={{0,1},{1,0},{2,3},{3,2},{4,5},{5,4},{6,7},{7,6},{8,9},{9,8},{10,11... | collective-permute-start | bytes 147464 | tf_op jit(solution)/shard_map/ppermute | solution.py:412
  14.1 1.3 %collective-permute-start.5 = (bf16[12,2048]{1,0:T(8,128)(2,1)S(1)}, bf16[12,2048]{1,0:T(8,128)(2,1)S(1)}, u32[]{:S(2)}, u32[]{:S(2)}) collective-permute-start(bf16[12,2048]{1,0:T(8,128)(2,1)S(1)} %collective-permute-done.2.refs_13_), channel_id=1, source_target_pairs={{0,1},{1,0},{2,3},{3,2},{4,5},{5,4},{6,7},{7,6},{8,9},{9,8},{10,11... | collective-permute-start | bytes 147464 | tf_op jit(solution)/shard_map/ppermute | solution.py:412
  15.4 25.3 %copy-start.1 = (f32[1,128]{1,0:T(1,128)S(1)}, f32[1,128]{1,0:T(1,128)}, u32[]{:S(2)}) copy-start(f32[1,128]{1,0:T(1,128)} %constant.43.clone.scale) | copy-start | bytes 1540
  20.6 1.6 %collective-permute-start.6 = (bf16[4,16,2048]{2,1,0:T(8,128)(2,1)S(1)}, bf16[4,16,2048]{2,1,0:T(8,128)(2,1)S(1)}, u32[]{:S(2)}, u32[]{:S(2)}) collective-permute-start(bf16[4,16,2048]{2,1,0:T(8,128)(2,1)S(1)} %get-tuple-element.39), channel_id=1, source_target_pairs={{0,1},{1,0},{2,3},{3,2},{4,5},{5,4},{6,7},{7,6},{8,9},{9,8},{10,11... | collective-permute-start | bytes 786440 | tf_op jit(solution)/shard_map/ppermute | solution.py:412
  22.3 8.5 %collective-permute-start.7 = (bf16[16,2048]{1,0:T(8,128)(2,1)S(1)}, bf16[16,2048]{1,0:T(8,128)(2,1)S(1)}, u32[]{:S(2)}, u32[]{:S(2)}) collective-permute-start(bf16[16,2048]{1,0:T(8,128)(2,1)S(1)} %get-tuple-element.47), channel_id=1, source_target_pairs={{0,16},{1,17},{2,18},{3,19},{4,20},{5,21},{6,22},{7,23},{8,24},{9,... | collective-permute-start | bytes 196616 | tf_op jit(solution)/shard_map/ppermute | solution.py:412
  23.7 7.1 %collective-permute-start.9 = (bf16[16,2048]{1,0:T(8,128)(2,1)S(1)}, bf16[16,2048]{1,0:T(8,128)(2,1)S(1)}, u32[]{:S(2)}, u32[]{:S(2)}) collective-permute-start(bf16[16,2048]{1,0:T(8,128)(2,1)S(1)} %get-tuple-element.48), channel_id=1, source_target_pairs={{0,9},{1,8},{2,11},{3,10},{4,13},{5,12},{6,15},{7,14},{8,17},{9,16... | collective-permute-start | bytes 196616 | tf_op jit(solution)/shard_map/ppermute | solution.py:412
  24.6 6.3 %collective-permute-start.8 = (bf16[16,2048]{1,0:T(8,128)(2,1)S(1)}, bf16[16,2048]{1,0:T(8,128)(2,1)S(1)}, u32[]{:S(2)}, u32[]{:S(2)}) collective-permute-start(bf16[16,2048]{1,0:T(8,128)(2,1)S(1)} %get-tuple-element.49), channel_id=1, source_target_pairs={{0,25},{1,24},{2,27},{3,26},{4,29},{5,28},{6,31},{7,30},{8,1},{9,0... | collective-permute-start | bytes 196616 | tf_op jit(solution)/shard_map/ppermute | solution.py:412
  30.9 4.2 %collective-permute-start.10 = (bf16[16,2048]{1,0:T(8,128)(2,1)S(1)}, bf16[16,2048]{1,0:T(8,128)(2,1)S(1)}, u32[]{:S(2)}, u32[]{:S(2)}) collective-permute-start(bf16[16,2048]{1,0:T(8,128)(2,1)S(1)} %get-tuple-element.43), channel_id=1, source_target_pairs={{0,3},{1,2},{2,1},{3,0},{4,7},{5,6},{6,5},{7,4},{8,11},{9,10},{10,... | collective-permute-start | bytes 196616 | tf_op jit(solution)/shard_map/ppermute | solution.py:412
  35.1 4.2 %collective-permute-start.11 = (bf16[16,2048]{1,0:T(8,128)(2,1)S(1)}, bf16[16,2048]{1,0:T(8,128)(2,1)S(1)}, u32[]{:S(2)}, u32[]{:S(2)}) collective-permute-start(bf16[16,2048]{1,0:T(8,128)(2,1)S(1)} %fusion.2), channel_id=1, source_target_pairs={{0,5},{1,4},{2,7},{3,6},{4,1},{5,0},{6,3},{7,2},{8,13},{9,12},{10,... | collective-permute-start | bytes 196616 | tf_op jit(solution)/shard_map/ppermute | solution.py:412
  39.3 1.4 %collective-permute-start.12 = (f32[16,2048]{1,0:T(8,128)S(1)}, f32[16,2048]{1,0:T(8,128)S(1)}, u32[]{:S(2)}, u32[]{:S(2)}) collective-permute-start(f32[16,2048]{1,0:T(8,128)S(1)} %convert_add_fusion.1.owned), channel_id=1, source_target_pairs={{0,1},{1,0},{2,3},{3,2},{4,5},{5,4},{6,7},{7,6},{8,9},{9,8},{10,11... | collective-permute-start | bytes 393224 | tf_op jit(solution)/shard_map/ppermute | solution.py:412

commit v3 on v2

--- a/solution.py
+++ b/solution.py
@@ -12,7 +12,7 @@
 F32 = jnp.float32
 BF16 = jnp.bfloat16
 LANES = 128
-SLOT = 16
+TOP = 8
 FIXED = 6
 
 
@@ -77,7 +77,7 @@
 
 def spectra_body(
     ids_far, images_far, high_far, low_far, twiddle_far, wave_far, offsets_far, ctf_far, noise_far,
-    rotated, square_high, square_low, power_high, power_low, data_power,
+    rotated, squares, powers, data_power,
     ids, images, high, low, twiddle, wave, offsets, ctf, noise,
     stacked, partial, rows, w_real, w_imag, cosine, sine, inverse, total, arrived,
 ):
@@ -163,20 +163,23 @@
         return carry
 
     lax.fori_loop(0, count // 8, transform, 0)
-    data_power[...] = jnp.broadcast_to(jnp.sum(total[...], axis=1, keepdims=True), data_power.shape)
+    energy = jnp.sum(jnp.transpose(total[...]), axis=0, keepdims=True)
+    data_power[...] = jnp.concatenate([energy] * (data_power.shape[1] // count), axis=1)
 
     def rotate(column, carry):
         at = pl.ds(pl.multiple_of(column * LANES, LANES), LANES)
-        far = pl.ds(pl.multiple_of(width + column * LANES, LANES), LANES)
-        c0 = rows[:, at]
-        sq = c0 * c0
-        square_high[:, at], square_low[:, at] = split(sq)
-        power_high[:, at], power_low[:, at] = split(sq * inverse[:, at])
+        square = rows[:, at] * rows[:, at]
+        high, low = split(square)
+        squares[column, 0:count, :] = high
+        squares[column, count:, :] = low
+        high, low = split(square * inverse[:, at])
+        powers[column, 0:count, :] = high
+        powers[column, count:, :] = low
         wr, wi = w_real[:, at], w_imag[:, at]
         for s in range(shifts):
             c, n = cosine[s:s + 1, at], sine[s:s + 1, at]
-            rotated[s * count:(s + 1) * count, at] = (wr * c - wi * n).astype(BF16)
-            rotated[s * count:(s + 1) * count, far] = (wi * c + wr * n).astype(BF16)
+            rotated[column, s * count:(s + 1) * count, :] = (wr * c - wi * n).astype(BF16)
+            rotated[columns + column, s * count:(s + 1) * count, :] = (wi * c + wr * n).astype(BF16)
         return carry
 
     lax.fori_loop(0, columns, rotate, 0)
@@ -191,15 +194,16 @@
     vmem = pl.BlockSpec(memory_space=pltpu.VMEM)
     far = pl.BlockSpec(memory_space=pltpu.HBM)
     shape = pltpu.VMEM
-    plane = shape((count, width), BF16)
+    columns = width // LANES
+    plane = shape((columns, 2 * count, LANES), BF16)
     k = high.shape[0]
     groups = pixels // k
     return pl.pallas_call(
         spectra_body,
-        out_shape=(shape((shifts * count, 2 * width), BF16), plane, plane, plane, plane, shape((count, LANES), F32)),
+        out_shape=(shape((2 * columns, shifts * count, LANES), BF16), plane, plane, shape((1, 2 * count), F32)),
         cost_estimate=pl.CostEstimate(flops=2**32, transcendentals=0, bytes_accessed=2**23),
         in_specs=[far] * 9,
-        out_specs=(vmem,) * 6,
+        out_specs=(vmem,) * 4,
         scratch_shapes=[
             pltpu.SMEM(group_ids.shape, jnp.int32),
             pltpu.VMEM(particles.shape, particles.dtype),
@@ -236,132 +240,201 @@
     return lax.dot_general(a, b, (((1,), (1,)), ((), ())), preferred_element_type=F32)
 
 
-def dot_columns(a, b):
-    return lax.dot_general(a, b, (((0,), (0,)), ((), ())), preferred_element_type=F32)
-
-
-def classes_body(digit_bits, classes, *refs):
-    others = classes - 1
-    ring, side, slots, priors = refs[:4]
-    rotated, square_high, square_low, power_high, power_low, data_power, own = refs[4:11]
-    mine = refs[11:11 + others]
-    theirs = refs[11 + others:11 + 2 * others]
-    keep, send, stack, soft, sums, extra = refs[11 + 2 * others:]
-    rotations = own.shape[1]
-    count = data_power.shape[0]
-    shifts = rotated.shape[0] // count
-    width = power_high.shape[1]
-    lanes = classes * SLOT
-    g, h = ring[0], side[0]
-
-    here = pl.ds(pl.multiple_of(h * width, width), width)
-    there = pl.ds(pl.multiple_of((1 - h) * width, width), width)
-    stack[...] = jnp.zeros_like(stack)
-    stack[0:rotations, :] = own[0]
-    for d in range(1, classes):
-        rows = slice(d * SLOT, d * SLOT + rotations)
-        stack[rows, here] = mine[d - 1][...]
-        stack[rows, there] = theirs[d - 1][...]
-
-    real, imag = stack[:, :width].astype(F32), stack[:, width:].astype(F32)
-    amp_high, amp_low = split(real * real + imag * imag)
-    own_power = (
-        dot_rows(power_high[...], amp_high) + dot_rows(power_high[...], amp_low) + dot_rows(power_low[...], amp_high)
-    )
-    lane = lax.broadcasted_iota(jnp.int32, (1, lanes), 1)
-    prior = jnp.zeros((1, lanes), F32)
+def side_by_side(planes, first, count):
+    return jnp.concatenate([planes[first + j] for j in range(count)], axis=1)
+
+
+def fold(value):
+    rest = value.shape[0] - TOP
+    pieces = TOP // rest
+    step = value.shape[1] // pieces
+    tail = jnp.concatenate([value[TOP:, j * step:(j + 1) * step] for j in range(pieces)], axis=0)
+    return jnp.concatenate([value[:TOP], tail], axis=1)
+
+
+def folded_width(rotations, width):
+    return width + (rotations - TOP) * width // TOP
+
+
+def pack_body(side, far, mine, theirs, near, arrived):
+    width = near.shape[2]
+    h = side[0]
+    copies = []
+    for j, half in enumerate((h, 1 - h)):
+        source = far.at[0, :, pl.ds(pl.multiple_of(half * width, width), width)]
+        copies.append(pltpu.make_async_copy(source, near.at[j], arrived.at[j]))
+    for copy in copies:
+        copy.start()
+    for j, out in enumerate((mine, theirs)):
+        copies[j].wait()
+        out[...] = fold(near[j].astype(F32)).astype(BF16)
+
+
+def pack(side, references):
+    _, rotations, full = references.shape
+    width = full // 2
+    vmem = pl.BlockSpec(memory_space=pltpu.VMEM)
+    out = pltpu.VMEM((TOP, folded_width(rotations, width)), BF16)
+    return pl.pallas_call(
+        pack_body,
+        out_shape=(out, out),
+        in_specs=[pl.BlockSpec(memory_space=pltpu.SMEM), pl.BlockSpec(memory_space=pltpu.HBM)],
+        out_specs=(vmem, vmem),
+        scratch_shapes=[pltpu.VMEM((2, rotations, width), BF16), pltpu.SemaphoreType.DMA((2,))],
+        compiler_params=pltpu.CompilerParams(vmem_limit_bytes=4 * 2**20),
+        name="pack",
+    )(side, pltpu.with_memory_space_constraint(references, pltpu.HBM))
+
+
+def half_scores(h, rotated, powers, packed, stack):
+    classes = len(packed)
+    rows, width = stack.shape
+    rest = rows // classes - TOP
+    pieces = TOP // rest
+    step = width // pieces
+    for d, ref in enumerate(packed):
+        value = ref[...].astype(F32)
+        stack[d * TOP:(d + 1) * TOP, :] = value[:, :width]
+        low = classes * TOP + d * rest
+        for j in range(pieces):
+            stack[low:low + rest, j * step:(j + 1) * step] = value[j * rest:(j + 1) * rest, width:]
+    planes = width // LANES
+    value = stack[...]
+    inter = dot_rows(value.astype(BF16), side_by_side(rotated, h * planes, planes))
+    high, low = split(value * value)
+    power = dot_rows(jnp.concatenate([high, low], axis=0), side_by_side(powers, 0, planes))
+    power = power[:rows] + power[rows:]
+    power = 0.5 * (power + pltpu.roll(power, power.shape[1] // 2, axis=1))
+    return [inter[:, j:j + LANES] - power for j in range(0, inter.shape[1], LANES)]
+
+
+def first_body(side, rotated, powers, *refs):
+    *packed, scores, stack = refs
+    parts = half_scores(side[0], rotated, powers, packed, stack)
+    for j, part in enumerate(parts):
+        scores[:, j * LANES:(j + 1) * LANES] = part
+
+
+def half_sums(half, soft, by_class, digits, rotated, squares, out):
+    classes = out.shape[0]
+    rows = soft.shape[0]
+    rest = rows // classes - TOP
+    planes = rotated.shape[0] // 2
+    width = planes * LANES
+    pieces = TOP // rest
+    step = width // pieces
+    sums = jnp.dot(soft, side_by_side(rotated, half * planes, planes), preferred_element_type=F32)
+    narrow = planes // 2
+    extra = jnp.dot(by_class, side_by_side(squares, half * narrow, narrow), preferred_element_type=F32)
+    extra = extra[:classes] + extra[extra.shape[0] // 2:extra.shape[0] // 2 + classes]
+    at = width + step
     for d in range(classes):
-        slot = lax.rem(g - d + classes, classes)
-        prior = jnp.where(lane // SLOT == d, priors[slots[slot]], prior)
-    prior = jnp.where(lane % SLOT < rotations, prior, -1e30)
-    inter = dot_rows(rotated[...], stack[...])
-    logits = []
-    top = None
-    for s in range(shifts):
-        l = inter[s * count:(s + 1) * count] - 0.5 * own_power
-        l = (l - 0.5 * data_power[:, 0:1]) + prior
-        logits.append(l)
-        top = l if top is None else jnp.maximum(top, l)
-    row_max = jnp.max(top, axis=1, keepdims=True)
-    raised = [jnp.exp(l - row_max) for l in logits]
-    norm = jnp.sum(functools.reduce(jnp.add, raised), axis=1, keepdims=True)
-    weight = jnp.zeros((count, lanes), F32)
-    for s in range(shifts):
-        w = raised[s] / norm
-        weight += w
-        soft[s * count:(s + 1) * count, :] = w.astype(BF16)
-    evidence = jnp.sum(row_max + jnp.log(norm), axis=0, keepdims=True)
-
-    sums[...] = dot_columns(soft[...], rotated[...])
-
-    wide = lax.broadcasted_iota(jnp.int32, (count, LANES), 1)
-    by_class = jnp.zeros((count, LANES), F32)
+        out[d, :, 0:width] = sums[d * TOP:(d + 1) * TOP, :].astype(out.dtype)
+        low = sums[classes * TOP + d * rest:classes * TOP + (d + 1) * rest, :]
+        tail = jnp.concatenate([low[:, j * step:(j + 1) * step] for j in range(pieces)], axis=0)
+        out[d, :, width:at] = tail.astype(out.dtype)
+        lines = extra[d:d + 1, :]
+        tall = jnp.concatenate([lines[:, j * LANES:(j + 1) * LANES] for j in range(narrow)], axis=0)
+        out[d, :, at:at + LANES] = tall.astype(out.dtype)
+        out[d, :, at + LANES:at + 2 * LANES] = digits.astype(out.dtype)
+
+
+def second_body(digit_bits, ring, side, slots, priors, *refs):
+    rotated, powers, squares, data_power, scores = refs[:5]
+    *packed, send, soft_out, class_out, digits_out, stack = refs[5:]
+    classes = len(packed)
+    rows = scores.shape[0]
+    rest = rows // classes - TOP
+    count = powers.shape[1] // 2
+    there = 1 - side[0]
+    parts = half_scores(there, rotated, powers, packed, stack)
+
+    line = lax.broadcasted_iota(jnp.int32, (rows, LANES), 0)
+    owner = jnp.where(line < classes * TOP, line // TOP, (line - classes * TOP) // rest)
+    prior = jnp.zeros((rows, LANES), F32)
     for d in range(classes):
-        part = jnp.sum(jnp.where(lane // SLOT == d, weight, 0.0), axis=1, keepdims=True)
-        by_class = jnp.where(wide == d, part, by_class)
-    class_high, class_low = split(by_class)
-    extra[...] = (
-        dot_columns(class_high, square_high[...])
-        + dot_columns(class_high, square_low[...])
-        + dot_columns(class_low, square_high[...])
-    )
-
-    column = lax.broadcasted_iota(jnp.int32, (1, width), 1)
-    number = jnp.round(jnp.broadcast_to(evidence, (1, width)) * float(2**FIXED)).astype(jnp.int32)
-    digit = lax.shift_right_logical(jnp.abs(number), jnp.minimum(column * digit_bits, 31))
-    digit = jnp.where(column * digit_bits < 31, digit & (2**digit_bits - 1), 0)
+        slot = lax.rem(ring[0] - d + classes, classes)
+        prior = jnp.where(owner == d, priors[slots[slot]], prior)
+    energy = 0.5 * data_power[...]
+    logits = [
+        ((scores[:, j * LANES:(j + 1) * LANES] + part) - energy) + prior for j, part in enumerate(parts)
+    ]
+    top = jnp.max(functools.reduce(jnp.maximum, logits), axis=0, keepdims=True)
+    top = jnp.maximum(top, pltpu.roll(top, count, axis=1))
+    raised = [jnp.exp(l - top) for l in logits]
+    norm = jnp.sum(functools.reduce(jnp.add, raised), axis=0, keepdims=True)
+    norm = norm + pltpu.roll(norm, count, axis=1)
+    scale = 1.0 / norm
+    weights = [r * scale for r in raised]
+    soft = jnp.concatenate([w.astype(BF16) for w in weights], axis=1)
+    soft_out[...] = soft
+
+    weight = functools.reduce(jnp.add, weights)
+    weight = weight + pltpu.roll(weight, count, axis=1)
+    base = classes * TOP
+    per_class = jnp.concatenate(
+        [
+            jnp.sum(weight[d * TOP:(d + 1) * TOP], axis=0, keepdims=True)
+            + jnp.sum(weight[base + d * rest:base + (d + 1) * rest], axis=0, keepdims=True)
+            for d in range(classes)
+        ]
+        + [jnp.zeros((-classes % 8, LANES), F32)] * (1 if classes % 8 else 0),
+        axis=0,
+    )
+    high = per_class.astype(BF16).astype(F32)
+    lane = lax.broadcasted_iota(jnp.int32, per_class.shape, 1)
+    by_class = jnp.concatenate([high, jnp.where(lane < count, per_class - high, 0.0)], axis=0).astype(BF16)
+    class_out[...] = by_class
+
+    lane = lax.broadcasted_iota(jnp.int32, (1, LANES), 1)
+    evidence = jnp.sum(jnp.where(lane < count, top + jnp.log(norm), 0.0), axis=1, keepdims=True)
+    number = jnp.round(jnp.broadcast_to(evidence, (1, LANES)) * float(2**FIXED)).astype(jnp.int32)
+    digit = lax.shift_right_logical(jnp.abs(number), jnp.minimum(lane * digit_bits, 31))
+    digit = jnp.where(lane * digit_bits < 31, digit & (2**digit_bits - 1), 0)
     digit = jnp.where(number < 0, -digit, digit).astype(F32)
-
-    empty = jnp.zeros((SLOT - rotations - 2, width), F32)
-    for d in range(classes):
-        rows = slice(d * SLOT, d * SLOT + rotations)
-        tail = jnp.concatenate([extra[d:d + 1, :], digit, empty], axis=0)
-        keep[d, 0:rotations, :] = sums[rows, here]
-        keep[d, rotations:SLOT, :] = tail
-        send[d, :, :] = jnp.concatenate([sums[rows, there], tail], axis=0).astype(BF16)
-
-
-def classes_call(ring, side, slot_class, log_prior, spectra_out, own, mine, theirs, digit_bits):
-    classes = len(mine) + 1
-    rotated, *_, data_power = spectra_out
-    rows, full = rotated.shape
-    width = full // 2
-    lanes = classes * SLOT
-    vmem = pl.BlockSpec(memory_space=pltpu.VMEM)
-    smem = pl.BlockSpec(memory_space=pltpu.SMEM)
-    shape = pltpu.VMEM
-    spectra_out = [pltpu.with_memory_space_constraint(x, pltpu.VMEM) for x in spectra_out]
+    digits = jnp.broadcast_to(digit, (TOP, LANES))
+    digits_out[...] = digits
+    half_sums(there, soft, by_class, digits, rotated, squares, send)
+
+
+def third_body(side, rotated, squares, soft, by_class, digits, keep):
+    half_sums(side[0], soft[...], by_class[...], digits[...], rotated, squares, keep)
+
+
+def local_call(body, out_shape, smem, vmem, scratch, name):
+    chip = pl.BlockSpec(memory_space=pltpu.VMEM)
     return pl.pallas_call(
-        functools.partial(classes_body, digit_bits, classes),
-        out_shape=(shape((classes, SLOT, width), F32), shape((classes, SLOT, width), BF16)),
-        in_specs=[smem] * 4 + [vmem] * (7 + 2 * len(mine)),
-        out_specs=(vmem, vmem),
-        scratch_shapes=[
-            pltpu.VMEM((lanes, full), BF16),
-            pltpu.VMEM((rows, lanes), BF16),
-            pltpu.VMEM((lanes, full), F32),
-            pltpu.VMEM((LANES, width), F32),
-        ],
-        compiler_params=pltpu.CompilerParams(vmem_limit_bytes=24 * 2**20),
-        name="classes",
-    )(ring, side, slot_class, log_prior, *spectra_out, own, *mine, *theirs)
+        body,
+        out_shape=out_shape,
+        in_specs=[pl.BlockSpec(memory_space=pltpu.SMEM)] * len(smem) + [chip] * len(vmem),
+        out_specs=jax.tree.map(lambda _: chip, out_shape, is_leaf=lambda x: not isinstance(x, tuple)),
+        scratch_shapes=scratch,
+        compiler_params=pltpu.CompilerParams(vmem_limit_bytes=16 * 2**20),
+        cost_estimate=pl.CostEstimate(flops=2**31, transcendentals=0, bytes_accessed=2**21),
+        name=name,
+    )(*smem, *(pltpu.with_memory_space_constraint(x, pltpu.VMEM) for x in vmem))
 
 
 def finish_body(side, owned, other, scale, sums, ctf_power, log_evidence):
     rotations, _, full = sums.shape
     width = full // 2
-    h = side[0]
-    here = pl.ds(pl.multiple_of(h * width, width), width)
-    there = pl.ds(pl.multiple_of((1 - h) * width, width), width)
-    sums[:, 0, here] = owned[:rotations, :]
-    sums[:, 0, there] = other[:rotations, :]
-    tail = jnp.where(h == 0, owned[rotations:, :], other[rotations:, :])
-    ctf_power[...] = tail[0:1, :]
-    log_evidence[...] = jnp.sum(tail[1:2, :LANES] * scale[...], axis=1, keepdims=True)
-
-
-def finish(side, owned, other, rotations, scale):
-    width = owned.shape[1]
+    rest = rotations - TOP
+    pieces = TOP // rest
+    step = width // pieces
+    at = width + step
+    narrow = width // 2
+    for half, source in ((side[0], owned), (1 - side[0], other)):
+        sums[0:TOP, 0, pl.ds(pl.multiple_of(half * width, width), width)] = source[:, :width]
+        for j in range(pieces):
+            here = pl.ds(pl.multiple_of(half * width + j * step, step), step)
+            sums[TOP:, 0, here] = source[j * rest:(j + 1) * rest, width:at]
+        for j in range(narrow // LANES):
+            here = pl.ds(pl.multiple_of(half * narrow + j * LANES, LANES), LANES)
+            ctf_power[:, here] = source[j:j + 1, at:at + LANES]
+    log_evidence[...] = jnp.sum(owned[0:1, at + LANES:at + 2 * LANES] * scale[...], axis=1, keepdims=True)
+
+
+def finish(side, owned, other, rotations, width, scale):
     vmem = pl.BlockSpec(memory_space=pltpu.VMEM)
     shape = jax.ShapeDtypeStruct
     return pl.pallas_call(
@@ -420,15 +493,41 @@
     def hop(bit):
         return lambda z, c, core: (z, c ^ (1 << bit), core ^ 1)
 
-    half_stack = lax.dynamic_slice_in_dim(references[0], h * width, width, 1)
-    mine = [move(half_stack, shift(d)) for d in range(1, rings)]
-    spectra_out = spectra(group_ids, particles, shift_offsets, ctf_table, noise_power)
-    mine, spectra_out = lax.optimization_barrier((mine, spectra_out))
+    ring, side = g.reshape(1), h.reshape(1)
+    near, far = pack(side, references)
+    mine = [move(near, shift(d)) for d in range(1, rings)]
+    rotated, squares, powers, data_power = spectra(group_ids, particles, shift_offsets, ctf_table, noise_power)
+    mine, near, far, rotated, squares, powers, data_power = lax.optimization_barrier(
+        (mine, near, far, rotated, squares, powers, data_power)
+    )
     theirs = [move(value, swap) for value in mine]
-    ring, side = g.reshape(1), h.reshape(1)
-    keep, send = classes_call(ring, side, slot_class, log_prior, spectra_out, references, mine, theirs, digit_bits)
-
-    pair = keep + move(send, swap).astype(F32)
+    rows = rings * rotations
+    planes = rotated.shape[1]
+    stack = pltpu.VMEM((rows, width), F32)
+    scores = local_call(
+        first_body, pltpu.VMEM((rows, planes), F32), (side,), (rotated, powers, near, *mine), [stack], "first"
+    )
+    theirs, scores = lax.optimization_barrier((theirs, scores))
+    block = (rings, TOP, folded_width(rotations, width) + 2 * LANES)
+    send, soft, by_class, digits = local_call(
+        functools.partial(second_body, digit_bits),
+        (
+            pltpu.VMEM(block, BF16),
+            pltpu.VMEM((rows, planes), BF16),
+            pltpu.VMEM((2 * (rings + -rings % 8), LANES), BF16),
+            pltpu.VMEM((TOP, LANES), F32),
+        ),
+        (ring, side, slot_class, log_prior),
+        (rotated, powers, squares, data_power, scores, far, *theirs),
+        [stack],
+        "second",
+    )
+    arrived = move(send, swap)
+    keep = local_call(
+        third_body, pltpu.VMEM(block, F32), (side,), (rotated, squares, soft, by_class, digits), [], "third"
+    )
+    arrived, keep = lax.optimization_barrier((arrived, keep))
+    pair = keep + arrived.astype(F32)
     gathered = [pair[0]]
     for d in range(1, rings):
         gathered.append(move(pair[d].astype(BF16), shift(rings - d)).astype(F32))
@@ -442,7 +541,7 @@
     for j in range(-(-31 // digit_bits)):
         scale[0, j] = 2.0 ** (j * digit_bits - FIXED)
     scale = scale / (count * rings * spread * width)
-    sums, ctf_power, log_evidence = finish(side, owned, other, rotations, jnp.asarray(scale, F32))
+    sums, ctf_power, log_evidence = finish(side, owned, other, rotations, width, jnp.asarray(scale, F32))
     return sums.reshape(1, rotations, 2 * width), ctf_power, log_evidence.reshape(())
 
 

time: 41.6 us -> 35.9 us (0.86)
  waiting for transfers between devices: 14.2 us -> 9.81 us
  Pallas kernels: 11.4 us -> 10.1 us
  local copies, waits for them, and re-layouts: 0.88 us -> 0.03 us
  starting transfers between devices: 14 us -> 14.8 us
    ppermute x13, waiting for transfers between devices: 14.2 us -> 9.81 us  [move(): return lax.ppermute(value, ('gx', 'gy'), pairs)]
    pallas_call x2 -> x5, Pallas kernels: 10.7 us -> 9.43 us  [the longest x1 4.64 us: spectra(): pl.pallas_call(spectra_body, out_shape=(shape((2 * columns, shifts * coun...]
    dynamic_slice x1 -> x0, local copies, waits for them, and re-layouts: 0.85 us -> none  [shards(): half_stack = lax.dynamic_slice_in_dim(references[0], h * width, width, 1)]
    ppermute x13, starting transfers between devices: 14 us -> 14.8 us  [move(): return lax.ppermute(value, ('gx', 'gy'), pairs)]
  transfers between devices with their start and end apart: 13 -> 13, of which waited for: 9 -> 7; matrix products, arithmetic and copies ran while one was open for 0% -> 0% of each run, Pallas kernels for 13% -> 17%
where the time goes in v3:
time: 35.9 us; the launch traced here: 35.7 us
  starting transfers between devices  14.8 us (41%)
  Pallas kernels  10.1 us (28%)
  waiting for transfers between devices  9.81 us (27%)
  between operations  0.75 us (2%)
    ppermute x13, starting transfers between devices, move(): return lax.ppermute(value, ('gx', 'gy'), pairs)  14.8 us
    ppermute x13, waiting for transfers between devices, move(): return lax.ppermute(value, ('gx', 'gy'), pairs)  9.81 us
    pallas_call x1, Pallas kernels, spectra(): pl.pallas_call(spectra_body, out_shape=(shape((2 * columns, shifts * coun...  4.64 us
    pallas_call x3, Pallas kernels, local_call(): pl.pallas_call(body, out_shape=out_shape, in_specs=[pl.BlockSpec(memory_s...  3.88 us
    pallas_call x1, Pallas kernels, pack(): pl.pallas_call(pack_body, out_shape=(out, out), in_specs=[pl.BlockSpec(me...  0.9 us
  transfers between devices with their start and end apart: 13, of which 7 were waited for; matrix products, arithmetic and copies ran while one was open for 0% of the time, Pallas kernels for 17%

profile of v3, /device:TPU:0, one launch (start us, length us, event | category | flops | bytes accessed | tf_op | source)
XLA Modules:
  0.0 35.7 jit_solution(15235073099327334849)
XLA Ops:
  0.6 0.9 %pack.1 = (bf16[8,3072]{1,0:T(8,128)(2,1)S(1)}, bf16[8,3072]{1,0:T(8,128)(2,1)S(1)}) custom-call(s32[1]{0:T(128)} %bitcast.side, bf16[1,12,4096]{2,1,0:T(8,128)(2,1)} %far.1), custom_call_target="tpu_custom_call" | custom-call | tf_op jit(solution)/shard_map/pack/pallas_call | solution.py:278
  1.6 4.6 %collective-permute-start.2 = (bf16[8,3072]{1,0:T(8,128)(2,1)S(1)}, bf16[8,3072]{1,0:T(8,128)(2,1)S(1)}, u32[]{:S(2)}, u32[]{:S(2)}) collective-permute-start(bf16[8,3072]{1,0:T(8,128)(2,1)S(1)} %get-tuple-element.44.refs_0_), channel_id=1, source_target_pairs={{0,25},{1,24},{2,27},{3,26},{4,29},{5,28},{6,31},{7,30},{8,1},{9,0... | collective-permute-start | bytes 147464 | tf_op jit(solution)/shard_map/ppermute | solution.py:485
  6.1 0.0 collective-permute-start.1
  6.1 1.0 %collective-permute-start = (bf16[8,3072]{1,0:T(8,128)(2,1)S(1)}, bf16[8,3072]{1,0:T(8,128)(2,1)S(1)}, u32[]{:S(2)}, u32[]{:S(2)}) collective-permute-start(bf16[8,3072]{1,0:T(8,128)(2,1)S(1)} %get-tuple-element.44.refs_0_), channel_id=1, source_target_pairs={{0,9},{1,8},{2,11},{3,10},{4,13},{5,12},{6,15},{7,14},{8,17},{9,16... | collective-permute-start | bytes 147464 | tf_op jit(solution)/shard_map/ppermute | solution.py:485
  7.1 4.6 %spectra.1 = (bf16[32,512,128]{2,1,0:T(8,128)(2,1)S(1)}, bf16[16,128,128]{2,1,0:T(8,128)(2,1)S(1)}, bf16[16,128,128]{2,1,0:T(8,128)(2,1)S(1)}, f32[1,128]{1,0:T(1,128)S(1)}) custom-call(s32[64]{0:T(128)} %ids_far.1, bf16[64,4096]{1,0:T(8,128)(2,1)} %images_far.1, bf16[512,512]{1,0:T(8,128)(2,1)} %constant.34.clone.high_far, ...), custom_call_target="tpu_custom_call" | custom-call | flops 4294967296 | bytes 8388608 | tf_op jit(solution)/shard_map/spectra/pallas_call | solution.py:201
  11.8 0.0 copy-start.1
  11.8 0.0 copy-start.2
  11.8 0.0 collective-permute-done.2.refs_3_
  11.8 0.6 %collective-permute-done.1.refs_2_ = bf16[8,3072]{1,0:T(8,128)(2,1)S(1)} collective-permute-done((bf16[8,3072]{1,0:T(8,128)(2,1)S(1)}, bf16[8,3072]{1,0:T(8,128)(2,1)S(1)}, u32[]{:S(2)}, u32[]{:S(2)}) %collective-permute-start.1) | collective-permute-done | bytes 49184 | tf_op jit(solution)/shard_map/ppermute | solution.py:485
  12.4 0.0 collective-permute-done.refs_1_
  12.4 0.0 collective-permute-start.3
  12.4 0.5 %collective-permute-start.4 = (bf16[8,3072]{1,0:T(8,128)(2,1)S(1)}, bf16[8,3072]{1,0:T(8,128)(2,1)S(1)}, u32[]{:S(2)}, u32[]{:S(2)}) collective-permute-start(bf16[8,3072]{1,0:T(8,128)(2,1)S(1)} %collective-permute-done.1.refs_2_), channel_id=1, source_target_pairs={{0,1},{1,0},{2,3},{3,2},{4,5},{5,4},{6,7},{7,6},{8,9},{9,8},{10,11... | collective-permute-start | bytes 147464 | tf_op jit(solution)/shard_map/ppermute | solution.py:485
  12.9 0.0 collective-permute-start.5
  12.9 1.0 %first.1.refs_4_ = f32[48,512]{1,0:T(8,128)S(1)} custom-call(s32[1]{0:T(128)} %bitcast.side, bf16[32,512,128]{2,1,0:T(8,128)(2,1)S(1)} %get-tuple-element.37.rotated.refs_0_, bf16[16,128,128]{2,1,0:T(8,128)(2,1)S(1)} %get-tuple-element.38.powers.refs_1_, bf16[8,3072]{1,0:T(8,128)(2,1)S(1)} %get-tuple-element.44.refs_0_, ...), custom_call_target="tpu_custom_call" | custom-call | flops 2147483648 | bytes 2097152 | tf_op jit(solution)/shard_map/first/pallas_call | solution.py:406
  13.9 0.0 collective-permute-done.3.refs_6_
  13.9 0.2 collective-permute-done.5.refs_8_
  14.2 2.4 %second.1 = (bf16[4,8,3328]{2,1,0:T(8,128)(2,1)S(1)}, bf16[48,512]{1,0:T(8,128)(2,1)S(1)}, bf16[16,128]{1,0:T(8,128)(2,1)S(1)}, f32[8,128]{1,0:T(8,128)S(1)}) custom-call(s32[1]{0:T(128)} %bitcast.1.ring, s32[1]{0:T(128)} %bitcast.side, s32[4]{0:T(128)S(1)} %copy-done.1, f32[4]{0:T(128)S(1)} %copy-done.2, ...), custom_call_target="tpu_custom_call" | custom-call | flops 2147483648 | bytes 2097152 | tf_op jit(solution)/shard_map/second/pallas_call | solution.py:406
  16.6 0.4 %collective-permute-start.6 = (bf16[4,8,3328]{2,1,0:T(8,128)(2,1)S(1)}, bf16[4,8,3328]{2,1,0:T(8,128)(2,1)S(1)}, u32[]{:S(2)}, u32[]{:S(2)}) collective-permute-start(bf16[4,8,3328]{2,1,0:T(8,128)(2,1)S(1)} %get-tuple-element.50), channel_id=1, source_target_pairs={{0,1},{1,0},{2,3},{3,2},{4,5},{5,4},{6,7},{7,6},{8,9},{9,8},{10,11... | collective-permute-start | bytes 638984 | tf_op jit(solution)/shard_map/ppermute | solution.py:485
  16.9 0.5 %third.1 = f32[4,8,3328]{2,1,0:T(8,128)S(1)} custom-call(s32[1]{0:T(128)} %bitcast.side, bf16[32,512,128]{2,1,0:T(8,128)(2,1)S(1)} %get-tuple-element.37.rotated.refs_0_, bf16[16,128,128]{2,1,0:T(8,128)(2,1)S(1)} %get-tuple-element.39.refs_2_.squares, bf16[48,512]{1,0:T(8,128)(2,1)S(1)} %get-tuple-element.51.soft, ...), custom_call_target="tpu_custom_call" | custom-call | flops 2147483648 | bytes 2097152 | tf_op jit(solution)/shard_map/third/pallas_call | solution.py:406
  17.5 0.6 %collective-permute-done.6 = bf16[4,8,3328]{2,1,0:T(8,128)(2,1)S(1)} collective-permute-done((bf16[4,8,3328]{2,1,0:T(8,128)(2,1)S(1)}, bf16[4,8,3328]{2,1,0:T(8,128)(2,1)S(1)}, u32[]{:S(2)}, u32[]{:S(2)}) %collective-permute-start.6) | collective-permute-done | bytes 213024 | tf_op jit(solution)/shard_map/ppermute | solution.py:485
  18.1 0.1 fusion.5
  18.2 1.7 %collective-permute-start.7 = (bf16[8,3328]{1,0:T(8,128)(2,1)S(1)}, bf16[8,3328]{1,0:T(8,128)(2,1)S(1)}, u32[]{:S(2)}, u32[]{:S(2)}) collective-permute-start(bf16[8,3328]{1,0:T(8,128)(2,1)S(1)} %get-tuple-element.63), channel_id=1, source_target_pairs={{0,16},{1,17},{2,18},{3,19},{4,20},{5,21},{6,22},{7,23},{8,24},{9,... | collective-permute-start | bytes 159752 | tf_op jit(solution)/shard_map/ppermute | solution.py:485
  19.8 1.2 %collective-permute-start.9 = (bf16[8,3328]{1,0:T(8,128)(2,1)S(1)}, bf16[8,3328]{1,0:T(8,128)(2,1)S(1)}, u32[]{:S(2)}, u32[]{:S(2)}) collective-permute-start(bf16[8,3328]{1,0:T(8,128)(2,1)S(1)} %get-tuple-element.64), channel_id=1, source_target_pairs={{0,9},{1,8},{2,11},{3,10},{4,13},{5,12},{6,15},{7,14},{8,17},{9,16... | collective-permute-start | bytes 159752 | tf_op jit(solution)/shard_map/ppermute | solution.py:485
  21.0 2.4 %collective-permute-start.8 = (bf16[8,3328]{1,0:T(8,128)(2,1)S(1)}, bf16[8,3328]{1,0:T(8,128)(2,1)S(1)}, u32[]{:S(2)}, u32[]{:S(2)}) collective-permute-start(bf16[8,3328]{1,0:T(8,128)(2,1)S(1)} %get-tuple-element.65), channel_id=1, source_target_pairs={{0,25},{1,24},{2,27},{3,26},{4,29},{5,28},{6,31},{7,30},{8,1},{9,0... | collective-permute-start | bytes 159752 | tf_op jit(solution)/shard_map/ppermute | solution.py:485
  23.4 2.6 %collective-permute-done.9 = bf16[8,3328]{1,0:T(8,128)(2,1)S(1)} collective-permute-done((bf16[8,3328]{1,0:T(8,128)(2,1)S(1)}, bf16[8,3328]{1,0:T(8,128)(2,1)S(1)}, u32[]{:S(2)}, u32[]{:S(2)}) %collective-permute-start.9) | collective-permute-done | bytes 53280 | tf_op jit(solution)/shard_map/ppermute | solution.py:485
  26.0 1.4 %collective-permute-start.10 = (bf16[8,3328]{1,0:T(8,128)(2,1)S(1)}, bf16[8,3328]{1,0:T(8,128)(2,1)S(1)}, u32[]{:S(2)}, u32[]{:S(2)}) collective-permute-start(bf16[8,3328]{1,0:T(8,128)(2,1)S(1)} %get-tuple-element.59), channel_id=1, source_target_pairs={{0,3},{1,2},{2,1},{3,0},{4,7},{5,6},{6,5},{7,4},{8,11},{9,10},{10,... | collective-permute-start | bytes 159752 | tf_op jit(solution)/shard_map/ppermute | solution.py:485
  27.4 2.4 %collective-permute-done.10 = bf16[8,3328]{1,0:T(8,128)(2,1)S(1)} collective-permute-done((bf16[8,3328]{1,0:T(8,128)(2,1)S(1)}, bf16[8,3328]{1,0:T(8,128)(2,1)S(1)}, u32[]{:S(2)}, u32[]{:S(2)}) %collective-permute-start.10) | collective-permute-done | bytes 53280 | tf_op jit(solution)/shard_map/ppermute | solution.py:485
  29.8 1.4 %collective-permute-start.11 = (bf16[8,3328]{1,0:T(8,128)(2,1)S(1)}, bf16[8,3328]{1,0:T(8,128)(2,1)S(1)}, u32[]{:S(2)}, u32[]{:S(2)}) collective-permute-start(bf16[8,3328]{1,0:T(8,128)(2,1)S(1)} %fusion.2), channel_id=1, source_target_pairs={{0,5},{1,4},{2,7},{3,6},{4,1},{5,0},{6,3},{7,2},{8,13},{9,12},{10,... | collective-permute-start | bytes 159752 | tf_op jit(solution)/shard_map/ppermute | solution.py:485
  31.2 2.3 %collective-permute-done.11 = bf16[8,3328]{1,0:T(8,128)(2,1)S(1)} collective-permute-done((bf16[8,3328]{1,0:T(8,128)(2,1)S(1)}, bf16[8,3328]{1,0:T(8,128)(2,1)S(1)}, u32[]{:S(2)}, u32[]{:S(2)}) %collective-permute-start.11) | collective-permute-done | bytes 53280 | tf_op jit(solution)/shard_map/ppermute | solution.py:485
  33.6 0.3 collective-permute-start.12
  33.9 1.1 %collective-permute-done.12.other = f32[8,3328]{1,0:T(8,128)S(1)} collective-permute-done((f32[8,3328]{1,0:T(8,128)S(1)}, f32[8,3328]{1,0:T(8,128)S(1)}, u32[]{:S(2)}, u32[]{:S(2)}) %collective-permute-start.12) | collective-permute-done | bytes 106528 | tf_op jit(solution)/shard_map/ppermute | solution.py:485
  35.0 0.7 %finish.1 = (f32[12,1,4096]{2,1,0:T(1,128)}, f32[1,2048]{1,0:T(1,128)}, f32[1,1]{1,0:T(1,128)}) custom-call(s32[1]{0:T(128)} %bitcast.side, f32[8,3328]{1,0:T(8,128)S(1)} %convert_add_fusion.1.owned, f32[8,3328]{1,0:T(8,128)S(1)} %collective-permute-done.12.other, f32[1,128]{1,0:T(1,128)S(1)} %copy-done), custom_call_target="tpu_custom_call" | custom-call | tf_op jit(solution)/shard_map/finish/pallas_call | solution.py:440
  (11 shorter events, 0.1 us)
Async XLA Ops:
  1.6 10.3 %collective-permute-start.2 = (bf16[8,3072]{1,0:T(8,128)(2,1)S(1)}, bf16[8,3072]{1,0:T(8,128)(2,1)S(1)}, u32[]{:S(2)}, u32[]{:S(2)}) collective-permute-start(bf16[8,3072]{1,0:T(8,128)(2,1)S(1)} %get-tuple-element.44.refs_0_), channel_id=1, source_target_pairs={{0,25},{1,24},{2,27},{3,26},{4,29},{5,28},{6,31},{7,30},{8,1},{9,0... | collective-permute-start | bytes 147464 | tf_op jit(solution)/shard_map/ppermute | solution.py:485
  6.1 6.3 %collective-permute-start.1 = (bf16[8,3072]{1,0:T(8,128)(2,1)S(1)}, bf16[8,3072]{1,0:T(8,128)(2,1)S(1)}, u32[]{:S(2)}, u32[]{:S(2)}) collective-permute-start(bf16[8,3072]{1,0:T(8,128)(2,1)S(1)} %get-tuple-element.44.refs_0_), channel_id=1, source_target_pairs={{0,16},{1,17},{2,18},{3,19},{4,20},{5,21},{6,22},{7,23},{8,24},{9,... | collective-permute-start | bytes 147464 | tf_op jit(solution)/shard_map/ppermute | solution.py:485
  6.1 6.3 %collective-permute-start = (bf16[8,3072]{1,0:T(8,128)(2,1)S(1)}, bf16[8,3072]{1,0:T(8,128)(2,1)S(1)}, u32[]{:S(2)}, u32[]{:S(2)}) collective-permute-start(bf16[8,3072]{1,0:T(8,128)(2,1)S(1)} %get-tuple-element.44.refs_0_), channel_id=1, source_target_pairs={{0,9},{1,8},{2,11},{3,10},{4,13},{5,12},{6,15},{7,14},{8,17},{9,16... | collective-permute-start | bytes 147464 | tf_op jit(solution)/shard_map/ppermute | solution.py:485
  11.8 2.4 %copy-start.1 = (s32[4]{0:T(128)S(1)}, s32[4]{0:T(128)}, u32[]{:S(2)}) copy-start(s32[4]{0:T(128)} %slots.1) | copy-start | bytes 52
  11.8 2.3 %copy-start.2 = (f32[4]{0:T(128)S(1)}, f32[4]{0:T(128)}, u32[]{:S(2)}) copy-start(f32[4]{0:T(128)} %priors.1) | copy-start | bytes 52
  12.4 1.5 %collective-permute-start.3 = (bf16[8,3072]{1,0:T(8,128)(2,1)S(1)}, bf16[8,3072]{1,0:T(8,128)(2,1)S(1)}, u32[]{:S(2)}, u32[]{:S(2)}) collective-permute-start(bf16[8,3072]{1,0:T(8,128)(2,1)S(1)} %collective-permute-done.refs_1_), channel_id=1, source_target_pairs={{0,1},{1,0},{2,3},{3,2},{4,5},{5,4},{6,7},{7,6},{8,9},{9,8},{10,11... | collective-permute-start | bytes 147464 | tf_op jit(solution)/shard_map/ppermute | solution.py:485
  12.4 1.5 %collective-permute-start.4 = (bf16[8,3072]{1,0:T(8,128)(2,1)S(1)}, bf16[8,3072]{1,0:T(8,128)(2,1)S(1)}, u32[]{:S(2)}, u32[]{:S(2)}) collective-permute-start(bf16[8,3072]{1,0:T(8,128)(2,1)S(1)} %collective-permute-done.1.refs_2_), channel_id=1, source_target_pairs={{0,1},{1,0},{2,3},{3,2},{4,5},{5,4},{6,7},{7,6},{8,9},{9,8},{10,11... | collective-permute-start | bytes 147464 | tf_op jit(solution)/shard_map/ppermute | solution.py:485
  12.9 1.2 %collective-permute-start.5 = (bf16[8,3072]{1,0:T(8,128)(2,1)S(1)}, bf16[8,3072]{1,0:T(8,128)(2,1)S(1)}, u32[]{:S(2)}, u32[]{:S(2)}) collective-permute-start(bf16[8,3072]{1,0:T(8,128)(2,1)S(1)} %collective-permute-done.2.refs_3_), channel_id=1, source_target_pairs={{0,1},{1,0},{2,3},{3,2},{4,5},{5,4},{6,7},{7,6},{8,9},{9,8},{10,11... | collective-permute-start | bytes 147464 | tf_op jit(solution)/shard_map/ppermute | solution.py:485
  16.6 1.5 %collective-permute-start.6 = (bf16[4,8,3328]{2,1,0:T(8,128)(2,1)S(1)}, bf16[4,8,3328]{2,1,0:T(8,128)(2,1)S(1)}, u32[]{:S(2)}, u32[]{:S(2)}) collective-permute-start(bf16[4,8,3328]{2,1,0:T(8,128)(2,1)S(1)} %get-tuple-element.50), channel_id=1, source_target_pairs={{0,1},{1,0},{2,3},{3,2},{4,5},{5,4},{6,7},{7,6},{8,9},{9,8},{10,11... | collective-permute-start | bytes 638984 | tf_op jit(solution)/shard_map/ppermute | solution.py:485
  16.9 18.1 %copy-start = (f32[1,128]{1,0:T(1,128)S(1)}, f32[1,128]{1,0:T(1,128)}, u32[]{:S(2)}) copy-start(f32[1,128]{1,0:T(1,128)} %constant.38.clone.scale) | copy-start | bytes 1540
  18.2 5.2 %collective-permute-start.7 = (bf16[8,3328]{1,0:T(8,128)(2,1)S(1)}, bf16[8,3328]{1,0:T(8,128)(2,1)S(1)}, u32[]{:S(2)}, u32[]{:S(2)}) collective-permute-start(bf16[8,3328]{1,0:T(8,128)(2,1)S(1)} %get-tuple-element.63), channel_id=1, source_target_pairs={{0,16},{1,17},{2,18},{3,19},{4,20},{5,21},{6,22},{7,23},{8,24},{9,... | collective-permute-start | bytes 159752 | tf_op jit(solution)/shard_map/ppermute | solution.py:485
  19.8 6.1 %collective-permute-start.9 = (bf16[8,3328]{1,0:T(8,128)(2,1)S(1)}, bf16[8,3328]{1,0:T(8,128)(2,1)S(1)}, u32[]{:S(2)}, u32[]{:S(2)}) collective-permute-start(bf16[8,3328]{1,0:T(8,128)(2,1)S(1)} %get-tuple-element.64), channel_id=1, source_target_pairs={{0,9},{1,8},{2,11},{3,10},{4,13},{5,12},{6,15},{7,14},{8,17},{9,16... | collective-permute-start | bytes 159752 | tf_op jit(solution)/shard_map/ppermute | solution.py:485
  21.0 5.0 %collective-permute-start.8 = (bf16[8,3328]{1,0:T(8,128)(2,1)S(1)}, bf16[8,3328]{1,0:T(8,128)(2,1)S(1)}, u32[]{:S(2)}, u32[]{:S(2)}) collective-permute-start(bf16[8,3328]{1,0:T(8,128)(2,1)S(1)} %get-tuple-element.65), channel_id=1, source_target_pairs={{0,25},{1,24},{2,27},{3,26},{4,29},{5,28},{6,31},{7,30},{8,1},{9,0... | collective-permute-start | bytes 159752 | tf_op jit(solution)/shard_map/ppermute | solution.py:485
  26.0 3.8 %collective-permute-start.10 = (bf16[8,3328]{1,0:T(8,128)(2,1)S(1)}, bf16[8,3328]{1,0:T(8,128)(2,1)S(1)}, u32[]{:S(2)}, u32[]{:S(2)}) collective-permute-start(bf16[8,3328]{1,0:T(8,128)(2,1)S(1)} %get-tuple-element.59), channel_id=1, source_target_pairs={{0,3},{1,2},{2,1},{3,0},{4,7},{5,6},{6,5},{7,4},{8,11},{9,10},{10,... | collective-permute-start | bytes 159752 | tf_op jit(solution)/shard_map/ppermute | solution.py:485
  29.8 3.8 %collective-permute-start.11 = (bf16[8,3328]{1,0:T(8,128)(2,1)S(1)}, bf16[8,3328]{1,0:T(8,128)(2,1)S(1)}, u32[]{:S(2)}, u32[]{:S(2)}) collective-permute-start(bf16[8,3328]{1,0:T(8,128)(2,1)S(1)} %fusion.2), channel_id=1, source_target_pairs={{0,5},{1,4},{2,7},{3,6},{4,1},{5,0},{6,3},{7,2},{8,13},{9,12},{10,... | collective-permute-start | bytes 159752 | tf_op jit(solution)/shard_map/ppermute | solution.py:485
  33.6 1.4 %collective-permute-start.12 = (f32[8,3328]{1,0:T(8,128)S(1)}, f32[8,3328]{1,0:T(8,128)S(1)}, u32[]{:S(2)}, u32[]{:S(2)}) collective-permute-start(f32[8,3328]{1,0:T(8,128)S(1)} %convert_add_fusion.1.owned), channel_id=1, source_target_pairs={{0,1},{1,0},{2,3},{3,2},{4,5},{5,4},{6,7},{7,6},{8,9},{9,8},{10,11... | collective-permute-start | bytes 319496 | tf_op jit(solution)/shard_map/ppermute | solution.py:485

commit v4 on v3

--- a/solution.py
+++ b/solution.py
@@ -14,6 +14,14 @@
 LANES = 128
 TOP = 8
 FIXED = 6
+
+
+def own_half():
+    place = lax.axis_index("gy")
+    half = place & 1
+    for bit in range(1, (lax.axis_size("gy") - 1).bit_length()):
+        half = half ^ ((place >> bit) & 1)
+    return half
 
 
 def dft_tables(side):
@@ -76,16 +84,16 @@
 
 
 def spectra_body(
-    ids_far, images_far, high_far, low_far, twiddle_far, wave_far, offsets_far, ctf_far, noise_far,
-    rotated, squares, powers, data_power,
-    ids, images, high, low, twiddle, wave, offsets, ctf, noise,
+    ids_far, images_far, high_far, low_far, twiddle_far, wave_far, offsets_far, ctf_far, noise_far, slots_far, priors_far,
+    rotated, squares, powers, data_power, prior,
+    ids, images, high, low, twiddle, wave, offsets, ctf, noise, slots, priors,
     stacked, partial, rows, w_real, w_imag, cosine, sine, inverse, total, arrived,
 ):
     copies = [
         pltpu.make_async_copy(far, near, arrived.at[j])
         for j, (far, near) in enumerate((
-            (images_far, images), (high_far, high), (low_far, low), (offsets_far, offsets), (wave_far, wave),
-            (noise_far, noise), (ids_far, ids), (ctf_far, ctf), (twiddle_far, twiddle),
+            (offsets_far, offsets), (wave_far, wave), (noise_far, noise), (slots_far, slots), (priors_far, priors),
+            (images_far, images), (high_far, high), (low_far, low), (ids_far, ids), (ctf_far, ctf), (twiddle_far, twiddle),
         ))
     ]
     for copy in copies:
@@ -101,25 +109,9 @@
     columns = noise.shape[1] // LANES
     width = noise.shape[1]
 
-    for copy in copies[:6]:
+    for copy in copies[:5]:
         copy.wait()
-    for m in range(groups):
-        for y in range(fold):
-            source = (m + groups * y) * LANES
-            stacked[m * count:(m + 1) * count, y * LANES:(y + 1) * LANES] = images[:, source:source + LANES]
-    partial[...] = jnp.dot(stacked[...], high[...], preferred_element_type=F32)
-    partial[...] += jnp.dot(stacked[...], low[...], preferred_element_type=F32)
-
     inverse[...] = 1.0 / noise[...]
-    for copy in copies[6:]:
-        copy.wait()
-
-    def fetch(p, carry):
-        rows[pl.ds(p, 1), :] = ctf[pl.ds(ids[p], 1), :]
-        return carry
-
-    lax.fori_loop(0, count, fetch, 0, unroll=8)
-
     lane = lax.broadcasted_iota(jnp.int32, (shifts, LANES), 1)
     shift = lax.broadcasted_iota(jnp.int32, (shifts, LANES), 0)
     step_u = jnp.zeros((shifts, LANES), jnp.int32)
@@ -133,6 +125,35 @@
         at = slice(column * LANES, (column + 1) * LANES)
         cosine[:, at] = jnp.take_along_axis(wave[...], turn, axis=1)
         sine[:, at] = jnp.take_along_axis(wave[...], turn + side, axis=1)
+
+    classes = slots.shape[0]
+    scored = prior.shape[0]
+    rest = scored // classes - TOP
+    line = lax.broadcasted_iota(jnp.int32, prior.shape, 0)
+    owner = jnp.where(line < classes * TOP, line // TOP, (line - classes * TOP) // rest)
+    ring = lax.axis_index("gx")
+    value = jnp.zeros(prior.shape, F32)
+    for d in range(classes):
+        value = jnp.where(owner == d, priors[slots[lax.rem(ring - d + classes, classes)]], value)
+    prior[...] = value
+
+    for copy in copies[5:8]:
+        copy.wait()
+    for m in range(groups):
+        for y in range(fold):
+            source = (m + groups * y) * LANES
+            stacked[m * count:(m + 1) * count, y * LANES:(y + 1) * LANES] = images[:, source:source + LANES]
+    partial[...] = jnp.dot(stacked[...], high[...], preferred_element_type=F32)
+    partial[...] += jnp.dot(stacked[...], low[...], preferred_element_type=F32)
+
+    for copy in copies[8:]:
+        copy.wait()
+
+    def fetch(p, carry):
+        rows[pl.ds(p, 1), :] = ctf[pl.ds(ids[p], 1), :]
+        return carry
+
+    lax.fori_loop(0, count, fetch, 0, unroll=16)
 
     def transform(block, carry):
         base = block * 8
@@ -185,7 +206,7 @@
     lax.fori_loop(0, columns, rotate, 0)
 
 
-def spectra(group_ids, particles, shift_offsets, ctf_table, noise_power):
+def spectra(group_ids, particles, shift_offsets, ctf_table, noise_power, slot_class, log_prior, rotations):
     count, pixels = particles.shape
     side = math.isqrt(pixels)
     width = noise_power.shape[0]
@@ -196,14 +217,15 @@
     shape = pltpu.VMEM
     columns = width // LANES
     plane = shape((columns, 2 * count, LANES), BF16)
+    scored = shape((slot_class.shape[0] * rotations, LANES), F32)
     k = high.shape[0]
     groups = pixels // k
     return pl.pallas_call(
         spectra_body,
-        out_shape=(shape((2 * columns, shifts * count, LANES), BF16), plane, plane, shape((1, 2 * count), F32)),
+        out_shape=(shape((2 * columns, shifts * count, LANES), BF16), plane, plane, shape((1, 2 * count), F32), scored),
         cost_estimate=pl.CostEstimate(flops=2**32, transcendentals=0, bytes_accessed=2**23),
-        in_specs=[far] * 9,
-        out_specs=(vmem,) * 4,
+        in_specs=[far] * 11,
+        out_specs=(vmem,) * 5,
         scratch_shapes=[
             pltpu.SMEM(group_ids.shape, jnp.int32),
             pltpu.VMEM(particles.shape, particles.dtype),
@@ -214,6 +236,8 @@
             pltpu.SMEM(shift_offsets.shape[::-1], jnp.int32),
             pltpu.VMEM(ctf_table.shape, F32),
             pltpu.VMEM((1, width), F32),
+            pltpu.SMEM(slot_class.shape, jnp.int32),
+            pltpu.SMEM(log_prior.shape, F32),
             pltpu.VMEM((groups * count, k), BF16),
             pltpu.VMEM((groups * count, high.shape[1]), F32),
             pltpu.VMEM((count, width), F32),
@@ -223,7 +247,7 @@
             pltpu.VMEM((shifts, width), F32),
             pltpu.VMEM((1, width), F32),
             pltpu.VMEM((count, LANES), F32),
-            pltpu.SemaphoreType.DMA((9,)),
+            pltpu.SemaphoreType.DMA((11,)),
         ],
         compiler_params=pltpu.CompilerParams(vmem_limit_bytes=24 * 2**20),
         name="spectra",
@@ -231,7 +255,7 @@
         pltpu.with_memory_space_constraint(x, pltpu.HBM)
         for x in (
             group_ids, particles, jnp.asarray(high), jnp.asarray(low), jnp.asarray(twiddle), jnp.asarray(wave),
-            shift_offsets.T, ctf_table, noise_power.reshape(1, width),
+            shift_offsets.T, ctf_table, noise_power.reshape(1, width), slot_class, log_prior,
         )
     ))
 
@@ -256,9 +280,9 @@
     return width + (rotations - TOP) * width // TOP
 
 
-def pack_body(side, far, mine, theirs, near, arrived):
+def pack_body(far, mine, theirs, near, arrived):
     width = near.shape[2]
-    h = side[0]
+    h = own_half()
     copies = []
     for j, half in enumerate((h, 1 - h)):
         source = far.at[0, :, pl.ds(pl.multiple_of(half * width, width), width)]
@@ -270,7 +294,7 @@
         out[...] = fold(near[j].astype(F32)).astype(BF16)
 
 
-def pack(side, references):
+def pack(references):
     _, rotations, full = references.shape
     width = full // 2
     vmem = pl.BlockSpec(memory_space=pltpu.VMEM)
@@ -278,12 +302,12 @@
     return pl.pallas_call(
         pack_body,
         out_shape=(out, out),
-        in_specs=[pl.BlockSpec(memory_space=pltpu.SMEM), pl.BlockSpec(memory_space=pltpu.HBM)],
+        in_specs=[pl.BlockSpec(memory_space=pltpu.HBM)],
         out_specs=(vmem, vmem),
         scratch_shapes=[pltpu.VMEM((2, rotations, width), BF16), pltpu.SemaphoreType.DMA((2,))],
         compiler_params=pltpu.CompilerParams(vmem_limit_bytes=4 * 2**20),
         name="pack",
-    )(side, pltpu.with_memory_space_constraint(references, pltpu.HBM))
+    )(pltpu.with_memory_space_constraint(references, pltpu.HBM))
 
 
 def half_scores(h, rotated, powers, packed, stack):
@@ -308,9 +332,9 @@
     return [inter[:, j:j + LANES] - power for j in range(0, inter.shape[1], LANES)]
 
 
-def first_body(side, rotated, powers, *refs):
+def first_body(rotated, powers, *refs):
     *packed, scores, stack = refs
-    parts = half_scores(side[0], rotated, powers, packed, stack)
+    parts = half_scores(own_half(), rotated, powers, packed, stack)
     for j, part in enumerate(parts):
         scores[:, j * LANES:(j + 1) * LANES] = part
 
@@ -339,25 +363,17 @@
         out[d, :, at + LANES:at + 2 * LANES] = digits.astype(out.dtype)
 
 
-def second_body(digit_bits, ring, side, slots, priors, *refs):
-    rotated, powers, squares, data_power, scores = refs[:5]
-    *packed, send, soft_out, class_out, digits_out, stack = refs[5:]
+def second_body(digit_bits, rotated, powers, squares, data_power, prior, scores, *refs):
+    *packed, send, soft_out, class_out, digits_out, stack = refs
     classes = len(packed)
     rows = scores.shape[0]
     rest = rows // classes - TOP
     count = powers.shape[1] // 2
-    there = 1 - side[0]
+    there = 1 - own_half()
     parts = half_scores(there, rotated, powers, packed, stack)
-
-    line = lax.broadcasted_iota(jnp.int32, (rows, LANES), 0)
-    owner = jnp.where(line < classes * TOP, line // TOP, (line - classes * TOP) // rest)
-    prior = jnp.zeros((rows, LANES), F32)
-    for d in range(classes):
-        slot = lax.rem(ring[0] - d + classes, classes)
-        prior = jnp.where(owner == d, priors[slots[slot]], prior)
     energy = 0.5 * data_power[...]
     logits = [
-        ((scores[:, j * LANES:(j + 1) * LANES] + part) - energy) + prior for j, part in enumerate(parts)
+        ((scores[:, j * LANES:(j + 1) * LANES] + part) - energy) + prior[...] for j, part in enumerate(parts)
     ]
     top = jnp.max(functools.reduce(jnp.maximum, logits), axis=0, keepdims=True)
     top = jnp.maximum(top, pltpu.roll(top, count, axis=1))
@@ -397,25 +413,25 @@
     half_sums(there, soft, by_class, digits, rotated, squares, send)
 
 
-def third_body(side, rotated, squares, soft, by_class, digits, keep):
-    half_sums(side[0], soft[...], by_class[...], digits[...], rotated, squares, keep)
-
-
-def local_call(body, out_shape, smem, vmem, scratch, name):
+def third_body(rotated, squares, soft, by_class, digits, keep):
+    half_sums(own_half(), soft[...], by_class[...], digits[...], rotated, squares, keep)
+
+
+def local_call(body, out_shape, operands, scratch, name):
     chip = pl.BlockSpec(memory_space=pltpu.VMEM)
     return pl.pallas_call(
         body,
         out_shape=out_shape,
-        in_specs=[pl.BlockSpec(memory_space=pltpu.SMEM)] * len(smem) + [chip] * len(vmem),
+        in_specs=[chip] * len(operands),
         out_specs=jax.tree.map(lambda _: chip, out_shape, is_leaf=lambda x: not isinstance(x, tuple)),
         scratch_shapes=scratch,
         compiler_params=pltpu.CompilerParams(vmem_limit_bytes=16 * 2**20),
         cost_estimate=pl.CostEstimate(flops=2**31, transcendentals=0, bytes_accessed=2**21),
         name=name,
-    )(*smem, *(pltpu.with_memory_space_constraint(x, pltpu.VMEM) for x in vmem))
-
-
-def finish_body(side, owned, other, scale, sums, ctf_power, log_evidence):
+    )(*(pltpu.with_memory_space_constraint(x, pltpu.VMEM) for x in operands))
+
+
+def finish_body(owned, other, scale, sums, ctf_power, log_evidence):
     rotations, _, full = sums.shape
     width = full // 2
     rest = rotations - TOP
@@ -423,7 +439,8 @@
     step = width // pieces
     at = width + step
     narrow = width // 2
-    for half, source in ((side[0], owned), (1 - side[0], other)):
+    h = own_half()
+    for half, source in ((h, owned), (1 - h, other)):
         sums[0:TOP, 0, pl.ds(pl.multiple_of(half * width, width), width)] = source[:, :width]
         for j in range(pieces):
             here = pl.ds(pl.multiple_of(half * width + j * step, step), step)
@@ -434,23 +451,29 @@
     log_evidence[...] = jnp.sum(owned[0:1, at + LANES:at + 2 * LANES] * scale[...], axis=1, keepdims=True)
 
 
-def finish(side, owned, other, rotations, width, scale):
+def finish(owned, other, rotations, width, scale):
     vmem = pl.BlockSpec(memory_space=pltpu.VMEM)
     shape = jax.ShapeDtypeStruct
     return pl.pallas_call(
         finish_body,
         out_shape=(shape((rotations, 1, 2 * width), F32), shape((1, width), F32), shape((1, 1), F32)),
-        in_specs=[pl.BlockSpec(memory_space=pltpu.SMEM)] + [vmem] * 3,
+        in_specs=[vmem] * 3,
         out_specs=(vmem,) * 3,
         compiler_params=pltpu.CompilerParams(vmem_limit_bytes=8 * 2**20),
         name="finish",
-    )(side, owned, other, scale)
+    )(owned, other, scale)
 
 
 def tree(parts):
     while len(parts) > 1:
         middle = len(parts) // 2
         parts = [parts[j] + parts[j + middle] for j in range(middle)]
+    return parts[0]
+
+
+def pairwise(parts):
+    while len(parts) > 1:
+        parts = [a + b for a, b in zip(parts[0::2], parts[1::2], strict=True)]
     return parts[0]
 
 
@@ -463,17 +486,7 @@
     count = particles.shape[0]
     width = noise_power.shape[0]
     rotations = references.shape[1]
-    g = lax.axis_index("gx")
-    q = lax.axis_index("gy")
     digit_bits = max(1, 8 - (rings * spread - 1).bit_length())
-
-    def parity(number):
-        return bin(number).count("1") & 1
-
-    chip = q // 2
-    h = (q & 1) ^ (g & 1)
-    for bit in range((chips - 1).bit_length()):
-        h = h ^ ((chip >> bit) & 1)
 
     def move(value, rule):
         pairs = []
@@ -485,28 +498,26 @@
         return lax.ppermute(value, ("gx", "gy"), pairs)
 
     def shift(d):
-        return lambda z, c, core: ((z + d) % rings, c, core ^ (d & 1))
+        return lambda z, c, core: ((z + d) % rings, c, core)
 
     def swap(z, c, core):
         return z, c, core ^ 1
 
-    def hop(bit):
-        return lambda z, c, core: (z, c ^ (1 << bit), core ^ 1)
-
-    ring, side = g.reshape(1), h.reshape(1)
-    near, far = pack(side, references)
+    def hop(mask):
+        return lambda z, c, core: (z, c ^ mask, core ^ (bin(mask).count("1") & 1))
+
+    near, far = pack(references)
     mine = [move(near, shift(d)) for d in range(1, rings)]
-    rotated, squares, powers, data_power = spectra(group_ids, particles, shift_offsets, ctf_table, noise_power)
-    mine, near, far, rotated, squares, powers, data_power = lax.optimization_barrier(
-        (mine, near, far, rotated, squares, powers, data_power)
+    spectra_out = spectra(
+        group_ids, particles, shift_offsets, ctf_table, noise_power, slot_class, log_prior, rotations
     )
+    mine, near, far, spectra_out = lax.optimization_barrier((mine, near, far, spectra_out))
+    rotated, squares, powers, data_power, prior = spectra_out
     theirs = [move(value, swap) for value in mine]
     rows = rings * rotations
     planes = rotated.shape[1]
     stack = pltpu.VMEM((rows, width), F32)
-    scores = local_call(
-        first_body, pltpu.VMEM((rows, planes), F32), (side,), (rotated, powers, near, *mine), [stack], "first"
-    )
+    scores = local_call(first_body, pltpu.VMEM((rows, planes), F32), (rotated, powers, near, *mine), [stack], "first")
     theirs, scores = lax.optimization_barrier((theirs, scores))
     block = (rings, TOP, folded_width(rotations, width) + 2 * LANES)
     send, soft, by_class, digits = local_call(
@@ -517,14 +528,13 @@
             pltpu.VMEM((2 * (rings + -rings % 8), LANES), BF16),
             pltpu.VMEM((TOP, LANES), F32),
         ),
-        (ring, side, slot_class, log_prior),
-        (rotated, powers, squares, data_power, scores, far, *theirs),
+        (rotated, powers, squares, data_power, prior, scores, far, *theirs),
         [stack],
         "second",
     )
     arrived = move(send, swap)
     keep = local_call(
-        third_body, pltpu.VMEM(block, F32), (side,), (rotated, squares, soft, by_class, digits), [], "third"
+        third_body, pltpu.VMEM(block, F32), (rotated, squares, soft, by_class, digits), [], "third"
     )
     arrived, keep = lax.optimization_barrier((arrived, keep))
     pair = keep + arrived.astype(F32)
@@ -532,16 +542,15 @@
     for d in range(1, rings):
         gathered.append(move(pair[d].astype(BF16), shift(rings - d)).astype(F32))
     owned = tree(gathered)
-    for bit in range((chips - 1).bit_length()):
-        low = owned.astype(BF16)
-        owned = lax.reduce_precision(owned, 8, 7) + move(low, hop(bit)).astype(F32)
-
+    low = owned.astype(BF16)
+    parts = [low] + [move(low, hop(mask)) for mask in range(1, chips)]
+    owned = pairwise([part.astype(F32) for part in parts])
     other = move(owned, swap)
     scale = np.zeros((1, LANES), np.float64)
     for j in range(-(-31 // digit_bits)):
         scale[0, j] = 2.0 ** (j * digit_bits - FIXED)
     scale = scale / (count * rings * spread * width)
-    sums, ctf_power, log_evidence = finish(side, owned, other, rotations, width, jnp.asarray(scale, F32))
+    sums, ctf_power, log_evidence = finish(owned, other, rotations, width, jnp.asarray(scale, F32))
     return sums.reshape(1, rotations, 2 * width), ctf_power, log_evidence.reshape(())
 
 

time: 35.9 us -> 34.9 us (0.972)
  waiting for transfers between devices: 9.81 us -> 8.02 us
  starting transfers between devices: 14.8 us -> 16.3 us
  Pallas kernels: 10.1 us -> 9.49 us
    ppermute x13 -> x14, waiting for transfers between devices: 9.81 us -> 8.02 us  [move(): return lax.ppermute(value, ('gx', 'gy'), pairs)]
    ppermute x13 -> x14, starting transfers between devices: 14.8 us -> 16.3 us  [move(): return lax.ppermute(value, ('gx', 'gy'), pairs)]
    pallas_call x3, Pallas kernels: 3.88 us -> 3.35 us  [local_call(): pl.pallas_call(body, out_shape=out_shape, in_specs=[chip] * len(operands)...]
  transfers between devices with their start and end apart: 13 -> 14, of which waited for: 7 -> 7; matrix products, arithmetic and copies ran while one was open for 0% -> 0% of each run, Pallas kernels for 17% -> 17%
where the time goes in v4:
time: 34.9 us; the launch traced here: 34.7 us
  starting transfers between devices  16.3 us (47%)
  Pallas kernels  9.49 us (27%)
  waiting for transfers between devices  8.02 us (23%)
  between operations  0.72 us (2%)
    ppermute x14, starting transfers between devices, move(): return lax.ppermute(value, ('gx', 'gy'), pairs)  16.3 us
    ppermute x14, waiting for transfers between devices, move(): return lax.ppermute(value, ('gx', 'gy'), pairs)  8.02 us
    pallas_call x1, Pallas kernels, spectra(): pl.pallas_call(spectra_body, out_shape=(shape((2 * columns, shifts * coun...  4.51 us
    pallas_call x3, Pallas kernels, local_call(): pl.pallas_call(body, out_shape=out_shape, in_specs=[chip] * len(operands)...  3.35 us
    pallas_call x1, Pallas kernels, pack(): pl.pallas_call(pack_body, out_shape=(out, out), in_specs=[pl.BlockSpec(me...  0.91 us
    pallas_call x1, Pallas kernels, finish(): pl.pallas_call(finish_body, out_shape=(shape((rotations, 1, 2 * width), F...  0.72 us
  transfers between devices with their start and end apart: 14, of which 7 were waited for; matrix products, arithmetic and copies ran while one was open for 0% of the time, Pallas kernels for 17%

profile of v4, /device:TPU:0, one launch (start us, length us, event | category | flops | bytes accessed | tf_op | source)
XLA Modules:
  0.0 34.7 jit_solution(158805722565909833)
XLA Ops:
  0.6 0.9 %pack.1 = (bf16[8,3072]{1,0:T(8,128)(2,1)S(1)}, bf16[8,3072]{1,0:T(8,128)(2,1)S(1)}) custom-call(bf16[1,12,4096]{2,1,0:T(8,128)(2,1)} %far.1), custom_call_target="tpu_custom_call" | custom-call | tf_op jit(solution)/shard_map/pack/pallas_call | solution.py:302
  1.5 5.1 %collective-permute-start.2 = (bf16[8,3072]{1,0:T(8,128)(2,1)S(1)}, bf16[8,3072]{1,0:T(8,128)(2,1)S(1)}, u32[]{:S(2)}, u32[]{:S(2)}) collective-permute-start(bf16[8,3072]{1,0:T(8,128)(2,1)S(1)} %get-tuple-element.48.refs_0_), channel_id=1, source_target_pairs={{0,24},{1,25},{2,26},{3,27},{4,28},{5,29},{6,30},{7,31},{8,0},{9,1... | collective-permute-start | bytes 147464 | tf_op jit(solution)/shard_map/ppermute | solution.py:498
  6.7 0.0 collective-permute-start.1
  6.7 1.0 %collective-permute-start = (bf16[8,3072]{1,0:T(8,128)(2,1)S(1)}, bf16[8,3072]{1,0:T(8,128)(2,1)S(1)}, u32[]{:S(2)}, u32[]{:S(2)}) collective-permute-start(bf16[8,3072]{1,0:T(8,128)(2,1)S(1)} %get-tuple-element.48.refs_0_), channel_id=1, source_target_pairs={{0,8},{1,9},{2,10},{3,11},{4,12},{5,13},{6,14},{7,15},{8,16},{9,17... | collective-permute-start | bytes 147464 | tf_op jit(solution)/shard_map/ppermute | solution.py:498
  7.7 4.5 %spectra.1 = (bf16[32,512,128]{2,1,0:T(8,128)(2,1)S(1)}, bf16[16,128,128]{2,1,0:T(8,128)(2,1)S(1)}, bf16[16,128,128]{2,1,0:T(8,128)(2,1)S(1)}, f32[1,128]{1,0:T(1,128)S(1)}, f32[48,128]{1,0:T(8,128)S(1)}) custom-call(s32[64]{0:T(128)} %ids_far.1, bf16[64,4096]{1,0:T(8,128)(2,1)} %images_far.1, bf16[512,512]{1,0:T(8,128)(2,1)} %constant.10.clone.high_far, ...), custom_call_target="tpu_custom_call" | custom-call | flops 4294967296 | bytes 8388608 | tf_op jit(solution)/shard_map/spectra/pallas_call | solution.py:223
  12.2 0.0 collective-permute-done.2.refs_3_
  12.2 0.0 collective-permute-done.1.refs_2_
  12.2 0.3 collective-permute-done.refs_1_
  12.6 0.0 collective-permute-start.3
  12.6 0.5 %collective-permute-start.4 = (bf16[8,3072]{1,0:T(8,128)(2,1)S(1)}, bf16[8,3072]{1,0:T(8,128)(2,1)S(1)}, u32[]{:S(2)}, u32[]{:S(2)}) collective-permute-start(bf16[8,3072]{1,0:T(8,128)(2,1)S(1)} %collective-permute-done.1.refs_2_), channel_id=1, source_target_pairs={{0,1},{1,0},{2,3},{3,2},{4,5},{5,4},{6,7},{7,6},{8,9},{9,8},{10,11... | collective-permute-start | bytes 147464 | tf_op jit(solution)/shard_map/ppermute | solution.py:498
  13.1 0.0 collective-permute-start.5
  13.1 1.0 %first.1.scores = f32[48,512]{1,0:T(8,128)S(1)} custom-call(bf16[32,512,128]{2,1,0:T(8,128)(2,1)S(1)} %get-tuple-element.40.rotated, bf16[16,128,128]{2,1,0:T(8,128)(2,1)S(1)} %get-tuple-element.41.powers, bf16[8,3072]{1,0:T(8,128)(2,1)S(1)} %get-tuple-element.48.refs_0_, bf16[8,3072]{1,0:T(8,128)(2,1)S(1)} %collective-permute-done.refs_1_, ...), custom_call_target="tpu_custom_call" | custom-call | flops 2147483648 | bytes 2097152 | tf_op jit(solution)/shard_map/first/pallas_call | solution.py:422
  14.1 0.0 collective-permute-done.3.refs_1_
  14.1 0.0 collective-permute-done.4.refs_2_
  14.1 0.2 collective-permute-done.5.refs_3_
  14.3 1.9 %second.1 = (bf16[4,8,3328]{2,1,0:T(8,128)(2,1)S(1)}, bf16[48,512]{1,0:T(8,128)(2,1)S(1)}, bf16[16,128]{1,0:T(8,128)(2,1)S(1)}, f32[8,128]{1,0:T(8,128)S(1)}) custom-call(bf16[32,512,128]{2,1,0:T(8,128)(2,1)S(1)} %get-tuple-element.40.rotated, bf16[16,128,128]{2,1,0:T(8,128)(2,1)S(1)} %get-tuple-element.41.powers, ...), custom_call_target="tpu_custom_call" | custom-call | flops 2147483648 | bytes 2097152 | tf_op jit(solution)/shard_map/second/pallas_call | solution.py:422
  16.2 0.4 %collective-permute-start.6 = (bf16[4,8,3328]{2,1,0:T(8,128)(2,1)S(1)}, bf16[4,8,3328]{2,1,0:T(8,128)(2,1)S(1)}, u32[]{:S(2)}, u32[]{:S(2)}) collective-permute-start(bf16[4,8,3328]{2,1,0:T(8,128)(2,1)S(1)} %get-tuple-element.54), channel_id=1, source_target_pairs={{0,1},{1,0},{2,3},{3,2},{4,5},{5,4},{6,7},{7,6},{8,9},{9,8},{10,11... | collective-permute-start | bytes 638984 | tf_op jit(solution)/shard_map/ppermute | solution.py:498
  16.5 0.5 %third.1 = f32[4,8,3328]{2,1,0:T(8,128)S(1)} custom-call(bf16[32,512,128]{2,1,0:T(8,128)(2,1)S(1)} %get-tuple-element.40.rotated, bf16[16,128,128]{2,1,0:T(8,128)(2,1)S(1)} %get-tuple-element.42.squares, bf16[48,512]{1,0:T(8,128)(2,1)S(1)} %get-tuple-element.55.soft, bf16[16,128]{1,0:T(8,128)(2,1)S(1)} %get-tuple-element.56.by_class, ...), custom_call_target="tpu_custom_call" | custom-call | flops 2147483648 | bytes 2097152 | tf_op jit(solution)/shard_map/third/pallas_call | solution.py:422
  17.1 0.6 %collective-permute-done.6 = bf16[4,8,3328]{2,1,0:T(8,128)(2,1)S(1)} collective-permute-done((bf16[4,8,3328]{2,1,0:T(8,128)(2,1)S(1)}, bf16[4,8,3328]{2,1,0:T(8,128)(2,1)S(1)}, u32[]{:S(2)}, u32[]{:S(2)}) %collective-permute-start.6) | collective-permute-done | bytes 213024 | tf_op jit(solution)/shard_map/ppermute | solution.py:498
  17.8 1.7 %collective-permute-start.7 = (bf16[8,3328]{1,0:T(8,128)(2,1)S(1)}, bf16[8,3328]{1,0:T(8,128)(2,1)S(1)}, u32[]{:S(2)}, u32[]{:S(2)}) collective-permute-start(bf16[8,3328]{1,0:T(8,128)(2,1)S(1)} %get-tuple-element.65), channel_id=1, source_target_pairs={{0,16},{1,17},{2,18},{3,19},{4,20},{5,21},{6,22},{7,23},{8,24},{9,... | collective-permute-start | bytes 159752 | tf_op jit(solution)/shard_map/ppermute | solution.py:498
  19.5 1.5 %collective-permute-start.9 = (bf16[8,3328]{1,0:T(8,128)(2,1)S(1)}, bf16[8,3328]{1,0:T(8,128)(2,1)S(1)}, u32[]{:S(2)}, u32[]{:S(2)}) collective-permute-start(bf16[8,3328]{1,0:T(8,128)(2,1)S(1)} %get-tuple-element.66), channel_id=1, source_target_pairs={{0,8},{1,9},{2,10},{3,11},{4,12},{5,13},{6,14},{7,15},{8,16},{9,17... | collective-permute-start | bytes 159752 | tf_op jit(solution)/shard_map/ppermute | solution.py:498
  21.0 2.4 %collective-permute-start.8 = (bf16[8,3328]{1,0:T(8,128)(2,1)S(1)}, bf16[8,3328]{1,0:T(8,128)(2,1)S(1)}, u32[]{:S(2)}, u32[]{:S(2)}) collective-permute-start(bf16[8,3328]{1,0:T(8,128)(2,1)S(1)} %get-tuple-element.67), channel_id=1, source_target_pairs={{0,24},{1,25},{2,26},{3,27},{4,28},{5,29},{6,30},{7,31},{8,0},{9,1... | collective-permute-start | bytes 159752 | tf_op jit(solution)/shard_map/ppermute | solution.py:498
  23.3 0.0 collective-permute-done.7
  23.3 2.9 %collective-permute-done.9 = bf16[8,3328]{1,0:T(8,128)(2,1)S(1)} collective-permute-done((bf16[8,3328]{1,0:T(8,128)(2,1)S(1)}, bf16[8,3328]{1,0:T(8,128)(2,1)S(1)}, u32[]{:S(2)}, u32[]{:S(2)}) %collective-permute-start.9) | collective-permute-done | bytes 53280 | tf_op jit(solution)/shard_map/ppermute | solution.py:498
  26.2 2.5 %collective-permute-start.12 = (bf16[8,3328]{1,0:T(8,128)(2,1)S(1)}, bf16[8,3328]{1,0:T(8,128)(2,1)S(1)}, u32[]{:S(2)}, u32[]{:S(2)}) collective-permute-start(bf16[8,3328]{1,0:T(8,128)(2,1)S(1)} %fusion.2), channel_id=1, source_target_pairs={{0,6},{1,7},{2,4},{3,5},{4,2},{5,3},{6,0},{7,1},{8,14},{9,15},{10,... | collective-permute-start | bytes 159752 | tf_op jit(solution)/shard_map/ppermute | solution.py:498
  28.7 0.0 collective-permute-start.11
  28.7 0.8 %collective-permute-start.10 = (bf16[8,3328]{1,0:T(8,128)(2,1)S(1)}, bf16[8,3328]{1,0:T(8,128)(2,1)S(1)}, u32[]{:S(2)}, u32[]{:S(2)}) collective-permute-start(bf16[8,3328]{1,0:T(8,128)(2,1)S(1)} %fusion.2), channel_id=1, source_target_pairs={{0,3},{1,2},{2,1},{3,0},{4,7},{5,6},{6,5},{7,4},{8,11},{9,10},{10,... | collective-permute-start | bytes 159752 | tf_op jit(solution)/shard_map/ppermute | solution.py:498
  29.5 1.9 %collective-permute-done.12 = bf16[8,3328]{1,0:T(8,128)(2,1)S(1)} collective-permute-done((bf16[8,3328]{1,0:T(8,128)(2,1)S(1)}, bf16[8,3328]{1,0:T(8,128)(2,1)S(1)}, u32[]{:S(2)}, u32[]{:S(2)}) %collective-permute-start.12) | collective-permute-done | bytes 53280 | tf_op jit(solution)/shard_map/ppermute | solution.py:498
  31.4 1.1 %collective-permute-done.11 = bf16[8,3328]{1,0:T(8,128)(2,1)S(1)} collective-permute-done((bf16[8,3328]{1,0:T(8,128)(2,1)S(1)}, bf16[8,3328]{1,0:T(8,128)(2,1)S(1)}, u32[]{:S(2)}, u32[]{:S(2)}) %collective-permute-start.11) | collective-permute-done | bytes 53280 | tf_op jit(solution)/shard_map/ppermute | solution.py:498
  32.5 0.5 %collective-permute-start.13 = (f32[8,3328]{1,0:T(8,128)S(1)}, f32[8,3328]{1,0:T(8,128)S(1)}, u32[]{:S(2)}, u32[]{:S(2)}) collective-permute-start(f32[8,3328]{1,0:T(8,128)S(1)} %add_add_fusion.owned), channel_id=1, source_target_pairs={{0,1},{1,0},{2,3},{3,2},{4,5},{5,4},{6,7},{7,6},{8,9},{9,8},{10,11... | collective-permute-start | bytes 319496 | tf_op jit(solution)/shard_map/ppermute | solution.py:498
  33.0 1.0 %collective-permute-done.13.other = f32[8,3328]{1,0:T(8,128)S(1)} collective-permute-done((f32[8,3328]{1,0:T(8,128)S(1)}, f32[8,3328]{1,0:T(8,128)S(1)}, u32[]{:S(2)}, u32[]{:S(2)}) %collective-permute-start.13) | collective-permute-done | bytes 106528 | tf_op jit(solution)/shard_map/ppermute | solution.py:498
  34.0 0.7 %finish.1 = (f32[12,1,4096]{2,1,0:T(1,128)}, f32[1,2048]{1,0:T(1,128)}, f32[1,1]{1,0:T(1,128)}) custom-call(f32[8,3328]{1,0:T(8,128)S(1)} %add_add_fusion.owned, f32[8,3328]{1,0:T(8,128)S(1)} %collective-permute-done.13.other, f32[1,128]{1,0:T(1,128)S(1)} %copy-done), custom_call_target="tpu_custom_call" | custom-call | tf_op jit(solution)/shard_map/finish/pallas_call | solution.py:457
  (8 shorter events, 0.1 us)
Async XLA Ops:
  1.5 10.7 %collective-permute-start.2 = (bf16[8,3072]{1,0:T(8,128)(2,1)S(1)}, bf16[8,3072]{1,0:T(8,128)(2,1)S(1)}, u32[]{:S(2)}, u32[]{:S(2)}) collective-permute-start(bf16[8,3072]{1,0:T(8,128)(2,1)S(1)} %get-tuple-element.48.refs_0_), channel_id=1, source_target_pairs={{0,24},{1,25},{2,26},{3,27},{4,28},{5,29},{6,30},{7,31},{8,0},{9,1... | collective-permute-start | bytes 147464 | tf_op jit(solution)/shard_map/ppermute | solution.py:498
  6.7 5.5 %collective-permute-start.1 = (bf16[8,3072]{1,0:T(8,128)(2,1)S(1)}, bf16[8,3072]{1,0:T(8,128)(2,1)S(1)}, u32[]{:S(2)}, u32[]{:S(2)}) collective-permute-start(bf16[8,3072]{1,0:T(8,128)(2,1)S(1)} %get-tuple-element.48.refs_0_), channel_id=1, source_target_pairs={{0,16},{1,17},{2,18},{3,19},{4,20},{5,21},{6,22},{7,23},{8,24},{9,... | collective-permute-start | bytes 147464 | tf_op jit(solution)/shard_map/ppermute | solution.py:498
  6.7 5.9 %collective-permute-start = (bf16[8,3072]{1,0:T(8,128)(2,1)S(1)}, bf16[8,3072]{1,0:T(8,128)(2,1)S(1)}, u32[]{:S(2)}, u32[]{:S(2)}) collective-permute-start(bf16[8,3072]{1,0:T(8,128)(2,1)S(1)} %get-tuple-element.48.refs_0_), channel_id=1, source_target_pairs={{0,8},{1,9},{2,10},{3,11},{4,12},{5,13},{6,14},{7,15},{8,16},{9,17... | collective-permute-start | bytes 147464 | tf_op jit(solution)/shard_map/ppermute | solution.py:498
  12.6 1.5 %collective-permute-start.3 = (bf16[8,3072]{1,0:T(8,128)(2,1)S(1)}, bf16[8,3072]{1,0:T(8,128)(2,1)S(1)}, u32[]{:S(2)}, u32[]{:S(2)}) collective-permute-start(bf16[8,3072]{1,0:T(8,128)(2,1)S(1)} %collective-permute-done.refs_1_), channel_id=1, source_target_pairs={{0,1},{1,0},{2,3},{3,2},{4,5},{5,4},{6,7},{7,6},{8,9},{9,8},{10,11... | collective-permute-start | bytes 147464 | tf_op jit(solution)/shard_map/ppermute | solution.py:498
  12.6 1.5 %collective-permute-start.4 = (bf16[8,3072]{1,0:T(8,128)(2,1)S(1)}, bf16[8,3072]{1,0:T(8,128)(2,1)S(1)}, u32[]{:S(2)}, u32[]{:S(2)}) collective-permute-start(bf16[8,3072]{1,0:T(8,128)(2,1)S(1)} %collective-permute-done.1.refs_2_), channel_id=1, source_target_pairs={{0,1},{1,0},{2,3},{3,2},{4,5},{5,4},{6,7},{7,6},{8,9},{9,8},{10,11... | collective-permute-start | bytes 147464 | tf_op jit(solution)/shard_map/ppermute | solution.py:498
  13.1 1.2 %collective-permute-start.5 = (bf16[8,3072]{1,0:T(8,128)(2,1)S(1)}, bf16[8,3072]{1,0:T(8,128)(2,1)S(1)}, u32[]{:S(2)}, u32[]{:S(2)}) collective-permute-start(bf16[8,3072]{1,0:T(8,128)(2,1)S(1)} %collective-permute-done.2.refs_3_), channel_id=1, source_target_pairs={{0,1},{1,0},{2,3},{3,2},{4,5},{5,4},{6,7},{7,6},{8,9},{9,8},{10,11... | collective-permute-start | bytes 147464 | tf_op jit(solution)/shard_map/ppermute | solution.py:498
  16.2 1.5 %collective-permute-start.6 = (bf16[4,8,3328]{2,1,0:T(8,128)(2,1)S(1)}, bf16[4,8,3328]{2,1,0:T(8,128)(2,1)S(1)}, u32[]{:S(2)}, u32[]{:S(2)}) collective-permute-start(bf16[4,8,3328]{2,1,0:T(8,128)(2,1)S(1)} %get-tuple-element.54), channel_id=1, source_target_pairs={{0,1},{1,0},{2,3},{3,2},{4,5},{5,4},{6,7},{7,6},{8,9},{9,8},{10,11... | collective-permute-start | bytes 638984 | tf_op jit(solution)/shard_map/ppermute | solution.py:498
  16.5 17.4 %copy-start = (f32[1,128]{1,0:T(1,128)S(1)}, f32[1,128]{1,0:T(1,128)}, u32[]{:S(2)}) copy-start(f32[1,128]{1,0:T(1,128)} %constant.14.clone.scale) | copy-start | bytes 1540
  17.8 5.5 %collective-permute-start.7 = (bf16[8,3328]{1,0:T(8,128)(2,1)S(1)}, bf16[8,3328]{1,0:T(8,128)(2,1)S(1)}, u32[]{:S(2)}, u32[]{:S(2)}) collective-permute-start(bf16[8,3328]{1,0:T(8,128)(2,1)S(1)} %get-tuple-element.65), channel_id=1, source_target_pairs={{0,16},{1,17},{2,18},{3,19},{4,20},{5,21},{6,22},{7,23},{8,24},{9,... | collective-permute-start | bytes 159752 | tf_op jit(solution)/shard_map/ppermute | solution.py:498
  19.5 6.7 %collective-permute-start.9 = (bf16[8,3328]{1,0:T(8,128)(2,1)S(1)}, bf16[8,3328]{1,0:T(8,128)(2,1)S(1)}, u32[]{:S(2)}, u32[]{:S(2)}) collective-permute-start(bf16[8,3328]{1,0:T(8,128)(2,1)S(1)} %get-tuple-element.66), channel_id=1, source_target_pairs={{0,8},{1,9},{2,10},{3,11},{4,12},{5,13},{6,14},{7,15},{8,16},{9,17... | collective-permute-start | bytes 159752 | tf_op jit(solution)/shard_map/ppermute | solution.py:498
  21.0 5.2 %collective-permute-start.8 = (bf16[8,3328]{1,0:T(8,128)(2,1)S(1)}, bf16[8,3328]{1,0:T(8,128)(2,1)S(1)}, u32[]{:S(2)}, u32[]{:S(2)}) collective-permute-start(bf16[8,3328]{1,0:T(8,128)(2,1)S(1)} %get-tuple-element.67), channel_id=1, source_target_pairs={{0,24},{1,25},{2,26},{3,27},{4,28},{5,29},{6,30},{7,31},{8,0},{9,1... | collective-permute-start | bytes 159752 | tf_op jit(solution)/shard_map/ppermute | solution.py:498
  26.2 5.2 %collective-permute-start.12 = (bf16[8,3328]{1,0:T(8,128)(2,1)S(1)}, bf16[8,3328]{1,0:T(8,128)(2,1)S(1)}, u32[]{:S(2)}, u32[]{:S(2)}) collective-permute-start(bf16[8,3328]{1,0:T(8,128)(2,1)S(1)} %fusion.2), channel_id=1, source_target_pairs={{0,6},{1,7},{2,4},{3,5},{4,2},{5,3},{6,0},{7,1},{8,14},{9,15},{10,... | collective-permute-start | bytes 159752 | tf_op jit(solution)/shard_map/ppermute | solution.py:498
  28.7 3.7 %collective-permute-start.11 = (bf16[8,3328]{1,0:T(8,128)(2,1)S(1)}, bf16[8,3328]{1,0:T(8,128)(2,1)S(1)}, u32[]{:S(2)}, u32[]{:S(2)}) collective-permute-start(bf16[8,3328]{1,0:T(8,128)(2,1)S(1)} %fusion.2), channel_id=1, source_target_pairs={{0,5},{1,4},{2,7},{3,6},{4,1},{5,0},{6,3},{7,2},{8,13},{9,12},{10,... | collective-permute-start | bytes 159752 | tf_op jit(solution)/shard_map/ppermute | solution.py:498
  28.7 3.7 %collective-permute-start.10 = (bf16[8,3328]{1,0:T(8,128)(2,1)S(1)}, bf16[8,3328]{1,0:T(8,128)(2,1)S(1)}, u32[]{:S(2)}, u32[]{:S(2)}) collective-permute-start(bf16[8,3328]{1,0:T(8,128)(2,1)S(1)} %fusion.2), channel_id=1, source_target_pairs={{0,3},{1,2},{2,1},{3,0},{4,7},{5,6},{6,5},{7,4},{8,11},{9,10},{10,... | collective-permute-start | bytes 159752 | tf_op jit(solution)/shard_map/ppermute | solution.py:498
  32.5 1.5 %collective-permute-start.13 = (f32[8,3328]{1,0:T(8,128)S(1)}, f32[8,3328]{1,0:T(8,128)S(1)}, u32[]{:S(2)}, u32[]{:S(2)}) collective-permute-start(f32[8,3328]{1,0:T(8,128)S(1)} %add_add_fusion.owned), channel_id=1, source_target_pairs={{0,1},{1,0},{2,3},{3,2},{4,5},{5,4},{6,7},{7,6},{8,9},{9,8},{10,11... | collective-permute-start | bytes 319496 | tf_op jit(solution)/shard_map/ppermute | solution.py:498

commit v5 on v4

--- a/solution.py
+++ b/solution.py
@@ -18,7 +18,7 @@
 
 def own_half():
     place = lax.axis_index("gy")
-    half = place & 1
+    half = (place & 1) ^ (lax.axis_index("gx") & 1)
     for bit in range(1, (lax.axis_size("gy") - 1).bit_length()):
         half = half ^ ((place >> bit) & 1)
     return half
@@ -498,7 +498,7 @@
         return lax.ppermute(value, ("gx", "gy"), pairs)
 
     def shift(d):
-        return lambda z, c, core: ((z + d) % rings, c, core)
+        return lambda z, c, core: ((z + d) % rings, c, core ^ (d & 1))
 
     def swap(z, c, core):
         return z, c, core ^ 1

time: 34.9 us -> 34 us (0.974)
  starting transfers between devices: 16.3 us -> 15.1 us
  waiting for transfers between devices: 8.02 us -> 8.38 us
    ppermute x14, starting transfers between devices: 16.3 us -> 15.1 us  [move(): return lax.ppermute(value, ('gx', 'gy'), pairs)]
    ppermute x14, waiting for transfers between devices: 8.02 us -> 8.38 us  [move(): return lax.ppermute(value, ('gx', 'gy'), pairs)]
  transfers between devices with their start and end apart: 14 -> 14, of which waited for: 7 -> 7; matrix products, arithmetic and copies ran while one was open for 0% -> 0% of each run, Pallas kernels for 17% -> 18%
where the time goes in v5:
time: 34 us; the launch traced here: 33.8 us
  starting transfers between devices  15.1 us (44%)
  Pallas kernels  9.49 us (28%)
  waiting for transfers between devices  8.38 us (25%)
  between operations  0.72 us (2%)
    ppermute x14, starting transfers between devices, move(): return lax.ppermute(value, ('gx', 'gy'), pairs)  15.1 us
    ppermute x14, waiting for transfers between devices, move(): return lax.ppermute(value, ('gx', 'gy'), pairs)  8.38 us
    pallas_call x1, Pallas kernels, spectra(): pl.pallas_call(spectra_body, out_shape=(shape((2 * columns, shifts * coun...  4.51 us
    pallas_call x3, Pallas kernels, local_call(): pl.pallas_call(body, out_shape=out_shape, in_specs=[chip] * len(operands)...  3.35 us
    pallas_call x1, Pallas kernels, pack(): pl.pallas_call(pack_body, out_shape=(out, out), in_specs=[pl.BlockSpec(me...  0.91 us
    pallas_call x1, Pallas kernels, finish(): pl.pallas_call(finish_body, out_shape=(shape((rotations, 1, 2 * width), F...  0.72 us
  transfers between devices with their start and end apart: 14, of which 7 were waited for; matrix products, arithmetic and copies ran while one was open for 0% of the time, Pallas kernels for 18%

profile of v5, /device:TPU:0, one launch (start us, length us, event | category | flops | bytes accessed | tf_op | source)
XLA Modules:
  0.0 33.8 jit_solution(8959930718560793419)
XLA Ops:
  0.6 0.9 %pack.1 = (bf16[8,3072]{1,0:T(8,128)(2,1)S(1)}, bf16[8,3072]{1,0:T(8,128)(2,1)S(1)}) custom-call(bf16[1,12,4096]{2,1,0:T(8,128)(2,1)} %far.1), custom_call_target="tpu_custom_call" | custom-call | tf_op jit(solution)/shard_map/pack/pallas_call | solution.py:302
  1.5 4.6 %collective-permute-start.2 = (bf16[8,3072]{1,0:T(8,128)(2,1)S(1)}, bf16[8,3072]{1,0:T(8,128)(2,1)S(1)}, u32[]{:S(2)}, u32[]{:S(2)}) collective-permute-start(bf16[8,3072]{1,0:T(8,128)(2,1)S(1)} %get-tuple-element.48.refs_0_), channel_id=1, source_target_pairs={{0,25},{1,24},{2,27},{3,26},{4,29},{5,28},{6,31},{7,30},{8,1},{9,0... | collective-permute-start | bytes 147464 | tf_op jit(solution)/shard_map/ppermute | solution.py:498
  6.1 0.0 collective-permute-start.1
  6.1 1.0 %collective-permute-start = (bf16[8,3072]{1,0:T(8,128)(2,1)S(1)}, bf16[8,3072]{1,0:T(8,128)(2,1)S(1)}, u32[]{:S(2)}, u32[]{:S(2)}) collective-permute-start(bf16[8,3072]{1,0:T(8,128)(2,1)S(1)} %get-tuple-element.48.refs_0_), channel_id=1, source_target_pairs={{0,9},{1,8},{2,11},{3,10},{4,13},{5,12},{6,15},{7,14},{8,17},{9,16... | collective-permute-start | bytes 147464 | tf_op jit(solution)/shard_map/ppermute | solution.py:498
  7.1 4.5 %spectra.1 = (bf16[32,512,128]{2,1,0:T(8,128)(2,1)S(1)}, bf16[16,128,128]{2,1,0:T(8,128)(2,1)S(1)}, bf16[16,128,128]{2,1,0:T(8,128)(2,1)S(1)}, f32[1,128]{1,0:T(1,128)S(1)}, f32[48,128]{1,0:T(8,128)S(1)}) custom-call(s32[64]{0:T(128)} %ids_far.1, bf16[64,4096]{1,0:T(8,128)(2,1)} %images_far.1, bf16[512,512]{1,0:T(8,128)(2,1)} %constant.10.clone.high_far, ...), custom_call_target="tpu_custom_call" | custom-call | flops 4294967296 | bytes 8388608 | tf_op jit(solution)/shard_map/spectra/pallas_call | solution.py:223
  11.7 0.0 collective-permute-done.2.refs_3_
  11.7 0.7 %collective-permute-done.1.refs_2_ = bf16[8,3072]{1,0:T(8,128)(2,1)S(1)} collective-permute-done((bf16[8,3072]{1,0:T(8,128)(2,1)S(1)}, bf16[8,3072]{1,0:T(8,128)(2,1)S(1)}, u32[]{:S(2)}, u32[]{:S(2)}) %collective-permute-start.1) | collective-permute-done | bytes 49184 | tf_op jit(solution)/shard_map/ppermute | solution.py:498
  12.4 0.0 collective-permute-done.refs_1_
  12.4 0.0 collective-permute-start.3
  12.4 0.5 %collective-permute-start.4 = (bf16[8,3072]{1,0:T(8,128)(2,1)S(1)}, bf16[8,3072]{1,0:T(8,128)(2,1)S(1)}, u32[]{:S(2)}, u32[]{:S(2)}) collective-permute-start(bf16[8,3072]{1,0:T(8,128)(2,1)S(1)} %collective-permute-done.1.refs_2_), channel_id=1, source_target_pairs={{0,1},{1,0},{2,3},{3,2},{4,5},{5,4},{6,7},{7,6},{8,9},{9,8},{10,11... | collective-permute-start | bytes 147464 | tf_op jit(solution)/shard_map/ppermute | solution.py:498
  12.9 0.0 collective-permute-start.5
  12.9 1.0 %first.1.scores = f32[48,512]{1,0:T(8,128)S(1)} custom-call(bf16[32,512,128]{2,1,0:T(8,128)(2,1)S(1)} %get-tuple-element.40.rotated, bf16[16,128,128]{2,1,0:T(8,128)(2,1)S(1)} %get-tuple-element.41.powers, bf16[8,3072]{1,0:T(8,128)(2,1)S(1)} %get-tuple-element.48.refs_0_, bf16[8,3072]{1,0:T(8,128)(2,1)S(1)} %collective-permute-done.refs_1_, ...), custom_call_target="tpu_custom_call" | custom-call | flops 2147483648 | bytes 2097152 | tf_op jit(solution)/shard_map/first/pallas_call | solution.py:422
  13.9 0.0 collective-permute-done.3.refs_1_
  13.9 0.0 collective-permute-done.4.refs_2_
  13.9 0.2 collective-permute-done.5.refs_3_
  14.1 1.9 %second.1 = (bf16[4,8,3328]{2,1,0:T(8,128)(2,1)S(1)}, bf16[48,512]{1,0:T(8,128)(2,1)S(1)}, bf16[16,128]{1,0:T(8,128)(2,1)S(1)}, f32[8,128]{1,0:T(8,128)S(1)}) custom-call(bf16[32,512,128]{2,1,0:T(8,128)(2,1)S(1)} %get-tuple-element.40.rotated, bf16[16,128,128]{2,1,0:T(8,128)(2,1)S(1)} %get-tuple-element.41.powers, ...), custom_call_target="tpu_custom_call" | custom-call | flops 2147483648 | bytes 2097152 | tf_op jit(solution)/shard_map/second/pallas_call | solution.py:422
  16.0 0.4 %collective-permute-start.6 = (bf16[4,8,3328]{2,1,0:T(8,128)(2,1)S(1)}, bf16[4,8,3328]{2,1,0:T(8,128)(2,1)S(1)}, u32[]{:S(2)}, u32[]{:S(2)}) collective-permute-start(bf16[4,8,3328]{2,1,0:T(8,128)(2,1)S(1)} %get-tuple-element.54), channel_id=1, source_target_pairs={{0,1},{1,0},{2,3},{3,2},{4,5},{5,4},{6,7},{7,6},{8,9},{9,8},{10,11... | collective-permute-start | bytes 638984 | tf_op jit(solution)/shard_map/ppermute | solution.py:498
  16.4 0.5 %third.1 = f32[4,8,3328]{2,1,0:T(8,128)S(1)} custom-call(bf16[32,512,128]{2,1,0:T(8,128)(2,1)S(1)} %get-tuple-element.40.rotated, bf16[16,128,128]{2,1,0:T(8,128)(2,1)S(1)} %get-tuple-element.42.squares, bf16[48,512]{1,0:T(8,128)(2,1)S(1)} %get-tuple-element.55.soft, bf16[16,128]{1,0:T(8,128)(2,1)S(1)} %get-tuple-element.56.by_class, ...), custom_call_target="tpu_custom_call" | custom-call | flops 2147483648 | bytes 2097152 | tf_op jit(solution)/shard_map/third/pallas_call | solution.py:422
  16.9 0.6 %collective-permute-done.6 = bf16[4,8,3328]{2,1,0:T(8,128)(2,1)S(1)} collective-permute-done((bf16[4,8,3328]{2,1,0:T(8,128)(2,1)S(1)}, bf16[4,8,3328]{2,1,0:T(8,128)(2,1)S(1)}, u32[]{:S(2)}, u32[]{:S(2)}) %collective-permute-start.6) | collective-permute-done | bytes 213024 | tf_op jit(solution)/shard_map/ppermute | solution.py:498
  17.6 1.5 %collective-permute-start.7 = (bf16[8,3328]{1,0:T(8,128)(2,1)S(1)}, bf16[8,3328]{1,0:T(8,128)(2,1)S(1)}, u32[]{:S(2)}, u32[]{:S(2)}) collective-permute-start(bf16[8,3328]{1,0:T(8,128)(2,1)S(1)} %get-tuple-element.65), channel_id=1, source_target_pairs={{0,16},{1,17},{2,18},{3,19},{4,20},{5,21},{6,22},{7,23},{8,24},{9,... | collective-permute-start | bytes 159752 | tf_op jit(solution)/shard_map/ppermute | solution.py:498
  19.1 1.2 %collective-permute-start.9 = (bf16[8,3328]{1,0:T(8,128)(2,1)S(1)}, bf16[8,3328]{1,0:T(8,128)(2,1)S(1)}, u32[]{:S(2)}, u32[]{:S(2)}) collective-permute-start(bf16[8,3328]{1,0:T(8,128)(2,1)S(1)} %get-tuple-element.66), channel_id=1, source_target_pairs={{0,9},{1,8},{2,11},{3,10},{4,13},{5,12},{6,15},{7,14},{8,17},{9,16... | collective-permute-start | bytes 159752 | tf_op jit(solution)/shard_map/ppermute | solution.py:498
  20.3 2.4 %collective-permute-start.8 = (bf16[8,3328]{1,0:T(8,128)(2,1)S(1)}, bf16[8,3328]{1,0:T(8,128)(2,1)S(1)}, u32[]{:S(2)}, u32[]{:S(2)}) collective-permute-start(bf16[8,3328]{1,0:T(8,128)(2,1)S(1)} %get-tuple-element.67), channel_id=1, source_target_pairs={{0,25},{1,24},{2,27},{3,26},{4,29},{5,28},{6,31},{7,30},{8,1},{9,0... | collective-permute-start | bytes 159752 | tf_op jit(solution)/shard_map/ppermute | solution.py:498
  22.7 0.0 collective-permute-done.7
  22.7 2.5 %collective-permute-done.9 = bf16[8,3328]{1,0:T(8,128)(2,1)S(1)} collective-permute-done((bf16[8,3328]{1,0:T(8,128)(2,1)S(1)}, bf16[8,3328]{1,0:T(8,128)(2,1)S(1)}, u32[]{:S(2)}, u32[]{:S(2)}) %collective-permute-start.9) | collective-permute-done | bytes 53280 | tf_op jit(solution)/shard_map/ppermute | solution.py:498
  25.2 2.5 %collective-permute-start.12 = (bf16[8,3328]{1,0:T(8,128)(2,1)S(1)}, bf16[8,3328]{1,0:T(8,128)(2,1)S(1)}, u32[]{:S(2)}, u32[]{:S(2)}) collective-permute-start(bf16[8,3328]{1,0:T(8,128)(2,1)S(1)} %fusion.2), channel_id=1, source_target_pairs={{0,6},{1,7},{2,4},{3,5},{4,2},{5,3},{6,0},{7,1},{8,14},{9,15},{10,... | collective-permute-start | bytes 159752 | tf_op jit(solution)/shard_map/ppermute | solution.py:498
  27.7 0.1 collective-permute-start.11
  27.9 0.6 %collective-permute-start.10 = (bf16[8,3328]{1,0:T(8,128)(2,1)S(1)}, bf16[8,3328]{1,0:T(8,128)(2,1)S(1)}, u32[]{:S(2)}, u32[]{:S(2)}) collective-permute-start(bf16[8,3328]{1,0:T(8,128)(2,1)S(1)} %fusion.2), channel_id=1, source_target_pairs={{0,3},{1,2},{2,1},{3,0},{4,7},{5,6},{6,5},{7,4},{8,11},{9,10},{10,... | collective-permute-start | bytes 159752 | tf_op jit(solution)/shard_map/ppermute | solution.py:498
  28.5 1.8 %collective-permute-done.12 = bf16[8,3328]{1,0:T(8,128)(2,1)S(1)} collective-permute-done((bf16[8,3328]{1,0:T(8,128)(2,1)S(1)}, bf16[8,3328]{1,0:T(8,128)(2,1)S(1)}, u32[]{:S(2)}, u32[]{:S(2)}) %collective-permute-start.12) | collective-permute-done | bytes 53280 | tf_op jit(solution)/shard_map/ppermute | solution.py:498
  30.3 1.3 %collective-permute-done.11 = bf16[8,3328]{1,0:T(8,128)(2,1)S(1)} collective-permute-done((bf16[8,3328]{1,0:T(8,128)(2,1)S(1)}, bf16[8,3328]{1,0:T(8,128)(2,1)S(1)}, u32[]{:S(2)}, u32[]{:S(2)}) %collective-permute-start.11) | collective-permute-done | bytes 53280 | tf_op jit(solution)/shard_map/ppermute | solution.py:498
  31.7 0.3 collective-permute-start.13
  32.0 1.1 %collective-permute-done.13.other = f32[8,3328]{1,0:T(8,128)S(1)} collective-permute-done((f32[8,3328]{1,0:T(8,128)S(1)}, f32[8,3328]{1,0:T(8,128)S(1)}, u32[]{:S(2)}, u32[]{:S(2)}) %collective-permute-start.13) | collective-permute-done | bytes 106528 | tf_op jit(solution)/shard_map/ppermute | solution.py:498
  33.1 0.7 %finish.1 = (f32[12,1,4096]{2,1,0:T(1,128)}, f32[1,2048]{1,0:T(1,128)}, f32[1,1]{1,0:T(1,128)}) custom-call(f32[8,3328]{1,0:T(8,128)S(1)} %add_add_fusion.owned, f32[8,3328]{1,0:T(8,128)S(1)} %collective-permute-done.13.other, f32[1,128]{1,0:T(1,128)S(1)} %copy-done), custom_call_target="tpu_custom_call" | custom-call | tf_op jit(solution)/shard_map/finish/pallas_call | solution.py:457
  (8 shorter events, 0.1 us)
Async XLA Ops:
  1.5 10.1 %collective-permute-start.2 = (bf16[8,3072]{1,0:T(8,128)(2,1)S(1)}, bf16[8,3072]{1,0:T(8,128)(2,1)S(1)}, u32[]{:S(2)}, u32[]{:S(2)}) collective-permute-start(bf16[8,3072]{1,0:T(8,128)(2,1)S(1)} %get-tuple-element.48.refs_0_), channel_id=1, source_target_pairs={{0,25},{1,24},{2,27},{3,26},{4,29},{5,28},{6,31},{7,30},{8,1},{9,0... | collective-permute-start | bytes 147464 | tf_op jit(solution)/shard_map/ppermute | solution.py:498
  6.1 6.3 %collective-permute-start.1 = (bf16[8,3072]{1,0:T(8,128)(2,1)S(1)}, bf16[8,3072]{1,0:T(8,128)(2,1)S(1)}, u32[]{:S(2)}, u32[]{:S(2)}) collective-permute-start(bf16[8,3072]{1,0:T(8,128)(2,1)S(1)} %get-tuple-element.48.refs_0_), channel_id=1, source_target_pairs={{0,16},{1,17},{2,18},{3,19},{4,20},{5,21},{6,22},{7,23},{8,24},{9,... | collective-permute-start | bytes 147464 | tf_op jit(solution)/shard_map/ppermute | solution.py:498
  6.1 6.3 %collective-permute-start = (bf16[8,3072]{1,0:T(8,128)(2,1)S(1)}, bf16[8,3072]{1,0:T(8,128)(2,1)S(1)}, u32[]{:S(2)}, u32[]{:S(2)}) collective-permute-start(bf16[8,3072]{1,0:T(8,128)(2,1)S(1)} %get-tuple-element.48.refs_0_), channel_id=1, source_target_pairs={{0,9},{1,8},{2,11},{3,10},{4,13},{5,12},{6,15},{7,14},{8,17},{9,16... | collective-permute-start | bytes 147464 | tf_op jit(solution)/shard_map/ppermute | solution.py:498
  12.4 1.5 %collective-permute-start.3 = (bf16[8,3072]{1,0:T(8,128)(2,1)S(1)}, bf16[8,3072]{1,0:T(8,128)(2,1)S(1)}, u32[]{:S(2)}, u32[]{:S(2)}) collective-permute-start(bf16[8,3072]{1,0:T(8,128)(2,1)S(1)} %collective-permute-done.refs_1_), channel_id=1, source_target_pairs={{0,1},{1,0},{2,3},{3,2},{4,5},{5,4},{6,7},{7,6},{8,9},{9,8},{10,11... | collective-permute-start | bytes 147464 | tf_op jit(solution)/shard_map/ppermute | solution.py:498
  12.4 1.5 %collective-permute-start.4 = (bf16[8,3072]{1,0:T(8,128)(2,1)S(1)}, bf16[8,3072]{1,0:T(8,128)(2,1)S(1)}, u32[]{:S(2)}, u32[]{:S(2)}) collective-permute-start(bf16[8,3072]{1,0:T(8,128)(2,1)S(1)} %collective-permute-done.1.refs_2_), channel_id=1, source_target_pairs={{0,1},{1,0},{2,3},{3,2},{4,5},{5,4},{6,7},{7,6},{8,9},{9,8},{10,11... | collective-permute-start | bytes 147464 | tf_op jit(solution)/shard_map/ppermute | solution.py:498
  12.9 1.2 %collective-permute-start.5 = (bf16[8,3072]{1,0:T(8,128)(2,1)S(1)}, bf16[8,3072]{1,0:T(8,128)(2,1)S(1)}, u32[]{:S(2)}, u32[]{:S(2)}) collective-permute-start(bf16[8,3072]{1,0:T(8,128)(2,1)S(1)} %collective-permute-done.2.refs_3_), channel_id=1, source_target_pairs={{0,1},{1,0},{2,3},{3,2},{4,5},{5,4},{6,7},{7,6},{8,9},{9,8},{10,11... | collective-permute-start | bytes 147464 | tf_op jit(solution)/shard_map/ppermute | solution.py:498
  16.0 1.5 %collective-permute-start.6 = (bf16[4,8,3328]{2,1,0:T(8,128)(2,1)S(1)}, bf16[4,8,3328]{2,1,0:T(8,128)(2,1)S(1)}, u32[]{:S(2)}, u32[]{:S(2)}) collective-permute-start(bf16[4,8,3328]{2,1,0:T(8,128)(2,1)S(1)} %get-tuple-element.54), channel_id=1, source_target_pairs={{0,1},{1,0},{2,3},{3,2},{4,5},{5,4},{6,7},{7,6},{8,9},{9,8},{10,11... | collective-permute-start | bytes 638984 | tf_op jit(solution)/shard_map/ppermute | solution.py:498
  16.4 16.7 %copy-start = (f32[1,128]{1,0:T(1,128)S(1)}, f32[1,128]{1,0:T(1,128)}, u32[]{:S(2)}) copy-start(f32[1,128]{1,0:T(1,128)} %constant.14.clone.scale) | copy-start | bytes 1540
  17.6 5.1 %collective-permute-start.7 = (bf16[8,3328]{1,0:T(8,128)(2,1)S(1)}, bf16[8,3328]{1,0:T(8,128)(2,1)S(1)}, u32[]{:S(2)}, u32[]{:S(2)}) collective-permute-start(bf16[8,3328]{1,0:T(8,128)(2,1)S(1)} %get-tuple-element.65), channel_id=1, source_target_pairs={{0,16},{1,17},{2,18},{3,19},{4,20},{5,21},{6,22},{7,23},{8,24},{9,... | collective-permute-start | bytes 159752 | tf_op jit(solution)/shard_map/ppermute | solution.py:498
  19.1 6.1 %collective-permute-start.9 = (bf16[8,3328]{1,0:T(8,128)(2,1)S(1)}, bf16[8,3328]{1,0:T(8,128)(2,1)S(1)}, u32[]{:S(2)}, u32[]{:S(2)}) collective-permute-start(bf16[8,3328]{1,0:T(8,128)(2,1)S(1)} %get-tuple-element.66), channel_id=1, source_target_pairs={{0,9},{1,8},{2,11},{3,10},{4,13},{5,12},{6,15},{7,14},{8,17},{9,16... | collective-permute-start | bytes 159752 | tf_op jit(solution)/shard_map/ppermute | solution.py:498
  20.3 4.9 %collective-permute-start.8 = (bf16[8,3328]{1,0:T(8,128)(2,1)S(1)}, bf16[8,3328]{1,0:T(8,128)(2,1)S(1)}, u32[]{:S(2)}, u32[]{:S(2)}) collective-permute-start(bf16[8,3328]{1,0:T(8,128)(2,1)S(1)} %get-tuple-element.67), channel_id=1, source_target_pairs={{0,25},{1,24},{2,27},{3,26},{4,29},{5,28},{6,31},{7,30},{8,1},{9,0... | collective-permute-start | bytes 159752 | tf_op jit(solution)/shard_map/ppermute | solution.py:498
  25.2 5.1 %collective-permute-start.12 = (bf16[8,3328]{1,0:T(8,128)(2,1)S(1)}, bf16[8,3328]{1,0:T(8,128)(2,1)S(1)}, u32[]{:S(2)}, u32[]{:S(2)}) collective-permute-start(bf16[8,3328]{1,0:T(8,128)(2,1)S(1)} %fusion.2), channel_id=1, source_target_pairs={{0,6},{1,7},{2,4},{3,5},{4,2},{5,3},{6,0},{7,1},{8,14},{9,15},{10,... | collective-permute-start | bytes 159752 | tf_op jit(solution)/shard_map/ppermute | solution.py:498
  27.7 3.9 %collective-permute-start.11 = (bf16[8,3328]{1,0:T(8,128)(2,1)S(1)}, bf16[8,3328]{1,0:T(8,128)(2,1)S(1)}, u32[]{:S(2)}, u32[]{:S(2)}) collective-permute-start(bf16[8,3328]{1,0:T(8,128)(2,1)S(1)} %fusion.2), channel_id=1, source_target_pairs={{0,5},{1,4},{2,7},{3,6},{4,1},{5,0},{6,3},{7,2},{8,13},{9,12},{10,... | collective-permute-start | bytes 159752 | tf_op jit(solution)/shard_map/ppermute | solution.py:498
  27.9 3.8 %collective-permute-start.10 = (bf16[8,3328]{1,0:T(8,128)(2,1)S(1)}, bf16[8,3328]{1,0:T(8,128)(2,1)S(1)}, u32[]{:S(2)}, u32[]{:S(2)}) collective-permute-start(bf16[8,3328]{1,0:T(8,128)(2,1)S(1)} %fusion.2), channel_id=1, source_target_pairs={{0,3},{1,2},{2,1},{3,0},{4,7},{5,6},{6,5},{7,4},{8,11},{9,10},{10,... | collective-permute-start | bytes 159752 | tf_op jit(solution)/shard_map/ppermute | solution.py:498
  31.7 1.4 %collective-permute-start.13 = (f32[8,3328]{1,0:T(8,128)S(1)}, f32[8,3328]{1,0:T(8,128)S(1)}, u32[]{:S(2)}, u32[]{:S(2)}) collective-permute-start(f32[8,3328]{1,0:T(8,128)S(1)} %add_add_fusion.owned), channel_id=1, source_target_pairs={{0,1},{1,0},{2,3},{3,2},{4,5},{5,4},{6,7},{7,6},{8,9},{9,8},{10,11... | collective-permute-start | bytes 319496 | tf_op jit(solution)/shard_map/ppermute | solution.py:498

commit v6 on v5

--- a/solution.py
+++ b/solution.py
@@ -41,13 +41,14 @@
     table = np.where(parity == out_par, table, 0.0).astype(np.float32)
     high = table.astype(BF16)
     low = (table - high.astype(np.float32)).astype(BF16)
+    pair = np.concatenate([high, low], axis=0)
     lane_u = np.arange(LANES) // half
     turn = (np.arange(outer)[:, None] * lane_u[None, :]) % side
     angle = 2.0 * np.pi * turn / side
     twiddle = np.stack([np.cos(angle), np.sin(angle)], 1).astype(np.float32)
     turn = 2.0 * np.pi * np.arange(side) / side
     wave = np.concatenate([np.cos(turn), np.sin(turn)]).astype(np.float32)
-    return high, low, twiddle.reshape(2 * outer, LANES), np.tile(wave[None], (8, 1))
+    return pair, twiddle.reshape(2 * outer, LANES), np.tile(wave[None], (8, 1))
 
 
 def butterflies(real, imag):
@@ -84,20 +85,12 @@
 
 
 def spectra_body(
-    ids_far, images_far, high_far, low_far, twiddle_far, wave_far, offsets_far, ctf_far, noise_far, slots_far, priors_far,
+    ids_near, offsets_near, slots_near, priors_near, images, pair, twiddle, wave, ctf, noise,
     rotated, squares, powers, data_power, prior,
-    ids, images, high, low, twiddle, wave, offsets, ctf, noise, slots, priors,
-    stacked, partial, rows, w_real, w_imag, cosine, sine, inverse, total, arrived,
+    ids, partial, rows, w_real, w_imag, cosine, sine, inverse, total, arrived,
 ):
-    copies = [
-        pltpu.make_async_copy(far, near, arrived.at[j])
-        for j, (far, near) in enumerate((
-            (offsets_far, offsets), (wave_far, wave), (noise_far, noise), (slots_far, slots), (priors_far, priors),
-            (images_far, images), (high_far, high), (low_far, low), (ids_far, ids), (ctf_far, ctf), (twiddle_far, twiddle),
-        ))
-    ]
-    for copy in copies:
-        copy.start()
+    copy = pltpu.make_async_copy(ids_near, ids, arrived.at[0])
+    copy.start()
     count, pixels = images.shape
     side = math.isqrt(pixels)
     half = side // 2
@@ -105,20 +98,24 @@
     outer = side // fold
     per_row = LANES // side
     groups = outer // per_row
-    shifts = offsets.shape[1]
+    shifts = cosine.shape[0]
     columns = noise.shape[1] // LANES
-    width = noise.shape[1]
-
-    for copy in copies[:5]:
-        copy.wait()
+
+    tall = []
+    for m in range(groups):
+        tall.append(jnp.concatenate(
+            [images[:, (m + groups * y) * LANES:(m + groups * y + 1) * LANES] for y in range(fold)], axis=1
+        ))
+    tall = jnp.concatenate(tall, axis=0)
+    partial[...] = jnp.dot(jnp.concatenate([tall, tall], axis=1), pair[...], preferred_element_type=F32)
     inverse[...] = 1.0 / noise[...]
     lane = lax.broadcasted_iota(jnp.int32, (shifts, LANES), 1)
     shift = lax.broadcasted_iota(jnp.int32, (shifts, LANES), 0)
     step_u = jnp.zeros((shifts, LANES), jnp.int32)
     step_v = jnp.zeros((shifts, LANES), jnp.int32)
     for s in range(shifts):
-        step_u = jnp.where(shift == s, offsets[0, s], step_u)
-        step_v = jnp.where(shift == s, offsets[1, s], step_v)
+        step_u = jnp.where(shift == s, offsets_near[0:1, s:s + 1], step_u)
+        step_v = jnp.where(shift == s, offsets_near[1:2, s:s + 1], step_v)
     for column in range(columns):
         u = lane // half + fold * column
         turn = (u * step_u + (lane % half) * step_v) & (side - 1)
@@ -126,37 +123,25 @@
         cosine[:, at] = jnp.take_along_axis(wave[...], turn, axis=1)
         sine[:, at] = jnp.take_along_axis(wave[...], turn + side, axis=1)
 
-    classes = slots.shape[0]
+    classes = slots_near.shape[1]
     scored = prior.shape[0]
     rest = scored // classes - TOP
     line = lax.broadcasted_iota(jnp.int32, prior.shape, 0)
     owner = jnp.where(line < classes * TOP, line // TOP, (line - classes * TOP) // rest)
-    ring = lax.axis_index("gx")
+    slot = lax.rem(lax.axis_index("gx") - owner + classes, classes)
     value = jnp.zeros(prior.shape, F32)
+    by_slot = jnp.zeros((1, classes), F32)
     for d in range(classes):
-        value = jnp.where(owner == d, priors[slots[lax.rem(ring - d + classes, classes)]], value)
+        by_slot = jnp.where(slots_near[...] == d, priors_near[:, d:d + 1], by_slot)
+    for d in range(classes):
+        value = jnp.where(slot == d, by_slot[:, d:d + 1], value)
     prior[...] = value
-
-    for copy in copies[5:8]:
-        copy.wait()
-    for m in range(groups):
-        for y in range(fold):
-            source = (m + groups * y) * LANES
-            stacked[m * count:(m + 1) * count, y * LANES:(y + 1) * LANES] = images[:, source:source + LANES]
-    partial[...] = jnp.dot(stacked[...], high[...], preferred_element_type=F32)
-    partial[...] += jnp.dot(stacked[...], low[...], preferred_element_type=F32)
-
-    for copy in copies[8:]:
-        copy.wait()
-
-    def fetch(p, carry):
-        rows[pl.ds(p, 1), :] = ctf[pl.ds(ids[p], 1), :]
-        return carry
-
-    lax.fori_loop(0, count, fetch, 0, unroll=16)
+    copy.wait()
 
     def transform(block, carry):
         base = block * 8
+        for p in range(8):
+            rows[pl.ds(base + p, 1), :] = ctf[pl.ds(ids[base + p], 1), :]
         real, imag = [], []
         for y in range(outer):
             m, parity = y // per_row, y % per_row
@@ -211,35 +196,23 @@
     side = math.isqrt(pixels)
     width = noise_power.shape[0]
     shifts = shift_offsets.shape[0]
-    high, low, twiddle, wave = dft_tables(side)
+    pair, twiddle, wave = dft_tables(side)
     vmem = pl.BlockSpec(memory_space=pltpu.VMEM)
-    far = pl.BlockSpec(memory_space=pltpu.HBM)
     shape = pltpu.VMEM
     columns = width // LANES
     plane = shape((columns, 2 * count, LANES), BF16)
     scored = shape((slot_class.shape[0] * rotations, LANES), F32)
-    k = high.shape[0]
+    k = pair.shape[0] // 2
     groups = pixels // k
     return pl.pallas_call(
         spectra_body,
         out_shape=(shape((2 * columns, shifts * count, LANES), BF16), plane, plane, shape((1, 2 * count), F32), scored),
         cost_estimate=pl.CostEstimate(flops=2**32, transcendentals=0, bytes_accessed=2**23),
-        in_specs=[far] * 11,
+        in_specs=[vmem] * 10,
         out_specs=(vmem,) * 5,
         scratch_shapes=[
             pltpu.SMEM(group_ids.shape, jnp.int32),
-            pltpu.VMEM(particles.shape, particles.dtype),
-            pltpu.VMEM(high.shape, BF16),
-            pltpu.VMEM(low.shape, BF16),
-            pltpu.VMEM(twiddle.shape, F32),
-            pltpu.VMEM(wave.shape, F32),
-            pltpu.SMEM(shift_offsets.shape[::-1], jnp.int32),
-            pltpu.VMEM(ctf_table.shape, F32),
-            pltpu.VMEM((1, width), F32),
-            pltpu.SMEM(slot_class.shape, jnp.int32),
-            pltpu.SMEM(log_prior.shape, F32),
-            pltpu.VMEM((groups * count, k), BF16),
-            pltpu.VMEM((groups * count, high.shape[1]), F32),
+            pltpu.VMEM((groups * count, pair.shape[1]), F32),
             pltpu.VMEM((count, width), F32),
             pltpu.VMEM((count, width), F32),
             pltpu.VMEM((count, width), F32),
@@ -247,15 +220,15 @@
             pltpu.VMEM((shifts, width), F32),
             pltpu.VMEM((1, width), F32),
             pltpu.VMEM((count, LANES), F32),
-            pltpu.SemaphoreType.DMA((11,)),
+            pltpu.SemaphoreType.DMA((1,)),
         ],
         compiler_params=pltpu.CompilerParams(vmem_limit_bytes=24 * 2**20),
         name="spectra",
     )(*(
-        pltpu.with_memory_space_constraint(x, pltpu.HBM)
+        pltpu.with_memory_space_constraint(x, pltpu.VMEM)
         for x in (
-            group_ids, particles, jnp.asarray(high), jnp.asarray(low), jnp.asarray(twiddle), jnp.asarray(wave),
-            shift_offsets.T, ctf_table, noise_power.reshape(1, width), slot_class, log_prior,
+            group_ids, shift_offsets.T, slot_class.reshape(1, -1), log_prior.reshape(1, -1), particles, jnp.asarray(pair), jnp.asarray(twiddle),
+            jnp.asarray(wave), ctf_table, noise_power.reshape(1, width),
         )
     ))
 
@@ -305,6 +278,7 @@
         in_specs=[pl.BlockSpec(memory_space=pltpu.HBM)],
         out_specs=(vmem, vmem),
         scratch_shapes=[pltpu.VMEM((2, rotations, width), BF16), pltpu.SemaphoreType.DMA((2,))],
+        cost_estimate=pl.CostEstimate(flops=2**33, transcendentals=0, bytes_accessed=2**20),
         compiler_params=pltpu.CompilerParams(vmem_limit_bytes=4 * 2**20),
         name="pack",
     )(pltpu.with_memory_space_constraint(references, pltpu.HBM))
@@ -417,7 +391,7 @@
     half_sums(own_half(), soft[...], by_class[...], digits[...], rotated, squares, keep)
 
 
-def local_call(body, out_shape, operands, scratch, name):
+def local_call(body, out_shape, operands, scratch):
     chip = pl.BlockSpec(memory_space=pltpu.VMEM)
     return pl.pallas_call(
         body,
@@ -427,7 +401,6 @@
         scratch_shapes=scratch,
         compiler_params=pltpu.CompilerParams(vmem_limit_bytes=16 * 2**20),
         cost_estimate=pl.CostEstimate(flops=2**31, transcendentals=0, bytes_accessed=2**21),
-        name=name,
     )(*(pltpu.with_memory_space_constraint(x, pltpu.VMEM) for x in operands))
 
 
@@ -507,7 +480,9 @@
         return lambda z, c, core: (z, c ^ mask, core ^ (bin(mask).count("1") & 1))
 
     near, far = pack(references)
-    mine = [move(near, shift(d)) for d in range(1, rings)]
+    mine = []
+    for d in range(1, rings):
+        mine.append(move(near, shift(d)))
     spectra_out = spectra(
         group_ids, particles, shift_offsets, ctf_table, noise_power, slot_class, log_prior, rotations
     )
@@ -517,7 +492,7 @@
     rows = rings * rotations
     planes = rotated.shape[1]
     stack = pltpu.VMEM((rows, width), F32)
-    scores = local_call(first_body, pltpu.VMEM((rows, planes), F32), (rotated, powers, near, *mine), [stack], "first")
+    scores = local_call(first_body, pltpu.VMEM((rows, planes), F32), (rotated, powers, near, *mine), [stack])
     theirs, scores = lax.optimization_barrier((theirs, scores))
     block = (rings, TOP, folded_width(rotations, width) + 2 * LANES)
     send, soft, by_class, digits = local_call(
@@ -530,20 +505,21 @@
         ),
         (rotated, powers, squares, data_power, prior, scores, far, *theirs),
         [stack],
-        "second",
     )
     arrived = move(send, swap)
-    keep = local_call(
-        third_body, pltpu.VMEM(block, F32), (rotated, squares, soft, by_class, digits), [], "third"
-    )
+    keep = local_call(third_body, pltpu.VMEM(block, F32), (rotated, squares, soft, by_class, digits), [])
     arrived, keep = lax.optimization_barrier((arrived, keep))
     pair = keep + arrived.astype(F32)
     gathered = [pair[0]]
     for d in range(1, rings):
-        gathered.append(move(pair[d].astype(BF16), shift(rings - d)).astype(F32))
+        value = pair[d].astype(BF16)
+        value = move(value, shift(rings - d))
+        gathered.append(value.astype(F32))
     owned = tree(gathered)
     low = owned.astype(BF16)
-    parts = [low] + [move(low, hop(mask)) for mask in range(1, chips)]
+    parts = [low]
+    for mask in range(1, chips):
+        parts.append(move(low, hop(mask)))
     owned = pairwise([part.astype(F32) for part in parts])
     other = move(owned, swap)
     scale = np.zeros((1, LANES), np.float64)

time: 34 us -> 34.9 us (1.026)
  waiting for transfers between devices: 8.38 us -> 10.5 us
  Pallas kernels: 9.49 us -> 8.28 us
    ppermute x14, waiting for transfers between devices: 8.38 us -> 10.5 us  [move(): return lax.ppermute(value, ('gx', 'gy'), pairs)]
    pallas_call x1, Pallas kernels: 4.51 us -> 3.15 us  [spectra(): pl.pallas_call(spectra_body, out_shape=(shape((2 * columns, shifts * coun...]
  transfers between devices with their start and end apart: 14 -> 14, of which waited for: 7 -> 9; matrix products, arithmetic and copies ran while one was open for 0% -> 0% of each run, Pallas kernels for 18% -> 13%
where the time goes in v6:
time: 34.9 us; the launch traced here: 34.7 us
  starting transfers between devices  14.9 us (43%)
  waiting for transfers between devices  10.5 us (30%)
  Pallas kernels  8.28 us (24%)
  between operations  0.85 us (2%)
    ppermute x14, starting transfers between devices, move(): return lax.ppermute(value, ('gx', 'gy'), pairs)  14.9 us
    ppermute x14, waiting for transfers between devices, move(): return lax.ppermute(value, ('gx', 'gy'), pairs)  10.5 us
    pallas_call x3, Pallas kernels, local_call(): pl.pallas_call(body, out_shape=out_shape, in_specs=[chip] * len(operands)...  3.34 us
    pallas_call x1, Pallas kernels, spectra(): pl.pallas_call(spectra_body, out_shape=(shape((2 * columns, shifts * coun...  3.15 us
    pallas_call x1, Pallas kernels, pack(): pl.pallas_call(pack_body, out_shape=(out, out), in_specs=[pl.BlockSpec(me...  1.06 us
    pallas_call x1, Pallas kernels, finish(): pl.pallas_call(finish_body, out_shape=(shape((rotations, 1, 2 * width), F...  0.72 us
  transfers between devices with their start and end apart: 14, of which 9 were waited for; matrix products, arithmetic and copies ran while one was open for 0% of the time, Pallas kernels for 13%

profile of v6, /device:TPU:0, one launch (start us, length us, event | category | flops | bytes accessed | tf_op | source)
XLA Modules:
  0.0 34.7 jit_solution(16431558965580263295)
XLA Ops:
  0.6 0.0 copy-start.8
  0.6 0.0 copy-start.9
  0.7 0.0 copy-start.10
  0.7 1.1 %pack.1 = (bf16[8,3072]{1,0:T(8,128)(2,1)S(1)}, bf16[8,3072]{1,0:T(8,128)(2,1)S(1)}) custom-call(bf16[1,12,4096]{2,1,0:T(8,128)(2,1)} %far.1), custom_call_target="tpu_custom_call" | custom-call | flops 8589934592 | bytes 1048576 | tf_op jit(solution)/shard_map/pack/pallas_call | solution.py:275
  1.8 4.6 %collective-permute-start.2 = (bf16[8,3072]{1,0:T(8,128)(2,1)S(1)}, bf16[8,3072]{1,0:T(8,128)(2,1)S(1)}, u32[]{:S(2)}, u32[]{:S(2)}) collective-permute-start(bf16[8,3072]{1,0:T(8,128)(2,1)S(1)} %get-tuple-element.48.refs_0_), channel_id=1, source_target_pairs={{0,25},{1,24},{2,27},{3,26},{4,29},{5,28},{6,31},{7,30},{8,1},{9,0... | collective-permute-start | bytes 147464 | tf_op jit(solution)/shard_map/ppermute | solution.py:471
  6.4 0.0 collective-permute-start.1
  6.4 1.0 %collective-permute-start = (bf16[8,3072]{1,0:T(8,128)(2,1)S(1)}, bf16[8,3072]{1,0:T(8,128)(2,1)S(1)}, u32[]{:S(2)}, u32[]{:S(2)}) collective-permute-start(bf16[8,3072]{1,0:T(8,128)(2,1)S(1)} %get-tuple-element.48.refs_0_), channel_id=1, source_target_pairs={{0,9},{1,8},{2,11},{3,10},{4,13},{5,12},{6,15},{7,14},{8,17},{9,16... | collective-permute-start | bytes 147464 | tf_op jit(solution)/shard_map/ppermute | solution.py:471
  7.5 3.2 %spectra.1 = (bf16[32,512,128]{2,1,0:T(8,128)(2,1)S(1)}, bf16[16,128,128]{2,1,0:T(8,128)(2,1)S(1)}, bf16[16,128,128]{2,1,0:T(8,128)(2,1)S(1)}, f32[1,128]{1,0:T(1,128)S(1)}, f32[48,128]{1,0:T(8,128)S(1)}) custom-call(s32[64]{0:T(128)S(1)} %copy-done.5, s32[2,8]{1,0:T(2,128)S(1)} %bitcast.21, s32[1,4]{1,0:T(1,128)S(1)} %bitcast.22, f32[1,4]{1,0:T(1,128)S(1)} %bitcast.23, ...), custom_call_target="tpu_custom_call" | custom-call | flops 4294967296 | bytes 8388608 | tf_op jit(solution)/shard_map/spectra/pallas_call | solution.py:207
  10.6 0.0 collective-permute-done.2.refs_3_
  10.6 2.0 %collective-permute-done.1.refs_2_ = bf16[8,3072]{1,0:T(8,128)(2,1)S(1)} collective-permute-done((bf16[8,3072]{1,0:T(8,128)(2,1)S(1)}, bf16[8,3072]{1,0:T(8,128)(2,1)S(1)}, u32[]{:S(2)}, u32[]{:S(2)}) %collective-permute-start.1) | collective-permute-done | bytes 49184 | tf_op jit(solution)/shard_map/ppermute | solution.py:471
  12.7 0.5 %collective-permute-start.4 = (bf16[8,3072]{1,0:T(8,128)(2,1)S(1)}, bf16[8,3072]{1,0:T(8,128)(2,1)S(1)}, u32[]{:S(2)}, u32[]{:S(2)}) collective-permute-start(bf16[8,3072]{1,0:T(8,128)(2,1)S(1)} %collective-permute-done.1.refs_2_), channel_id=1, source_target_pairs={{0,1},{1,0},{2,3},{3,2},{4,5},{5,4},{6,7},{7,6},{8,9},{9,8},{10,11... | collective-permute-start | bytes 147464 | tf_op jit(solution)/shard_map/ppermute | solution.py:471
  13.2 0.0 collective-permute-start.5
  13.2 1.0 %shard_map.139.scores = f32[48,512]{1,0:T(8,128)S(1)} custom-call(bf16[32,512,128]{2,1,0:T(8,128)(2,1)S(1)} %get-tuple-element.40.rotated, bf16[16,128,128]{2,1,0:T(8,128)(2,1)S(1)} %get-tuple-element.41.powers, bf16[8,3072]{1,0:T(8,128)(2,1)S(1)} %get-tuple-element.48.refs_0_, bf16[8,3072]{1,0:T(8,128)(2,1)S(1)} %collective-permute-done.refs_1_, ...), custom_call_target="tpu_custom_call" | custom-call | flops 2147483648 | bytes 2097152 | tf_op jit(solution)/shard_map/pallas_call | solution.py:396
  14.2 0.2 collective-permute-done.5.refs_3_
  14.4 1.9 %shard_map.140 = (bf16[4,8,3328]{2,1,0:T(8,128)(2,1)S(1)}, bf16[48,512]{1,0:T(8,128)(2,1)S(1)}, bf16[16,128]{1,0:T(8,128)(2,1)S(1)}, f32[8,128]{1,0:T(8,128)S(1)}) custom-call(bf16[32,512,128]{2,1,0:T(8,128)(2,1)S(1)} %get-tuple-element.40.rotated, bf16[16,128,128]{2,1,0:T(8,128)(2,1)S(1)} %get-tuple-element.41.powers, ...), custom_call_target="tpu_custom_call" | custom-call | flops 2147483648 | bytes 2097152 | tf_op jit(solution)/shard_map/pallas_call | solution.py:396
  16.3 0.4 %collective-permute-start.6 = (bf16[4,8,3328]{2,1,0:T(8,128)(2,1)S(1)}, bf16[4,8,3328]{2,1,0:T(8,128)(2,1)S(1)}, u32[]{:S(2)}, u32[]{:S(2)}) collective-permute-start(bf16[4,8,3328]{2,1,0:T(8,128)(2,1)S(1)} %get-tuple-element.54), channel_id=1, source_target_pairs={{0,1},{1,0},{2,3},{3,2},{4,5},{5,4},{6,7},{7,6},{8,9},{9,8},{10,11... | collective-permute-start | bytes 638984 | tf_op jit(solution)/shard_map/ppermute | solution.py:471
  16.6 0.5 %shard_map.141 = f32[4,8,3328]{2,1,0:T(8,128)S(1)} custom-call(bf16[32,512,128]{2,1,0:T(8,128)(2,1)S(1)} %get-tuple-element.40.rotated, bf16[16,128,128]{2,1,0:T(8,128)(2,1)S(1)} %get-tuple-element.42.squares, bf16[48,512]{1,0:T(8,128)(2,1)S(1)} %get-tuple-element.55.soft, bf16[16,128]{1,0:T(8,128)(2,1)S(1)} %get-tuple-element.56.by_class, ...), custom_call_target="tpu_custom_call" | custom-call | flops 2147483648 | bytes 2097152 | tf_op jit(solution)/shard_map/pallas_call | solution.py:396
  17.1 0.7 %collective-permute-done.6 = bf16[4,8,3328]{2,1,0:T(8,128)(2,1)S(1)} collective-permute-done((bf16[4,8,3328]{2,1,0:T(8,128)(2,1)S(1)}, bf16[4,8,3328]{2,1,0:T(8,128)(2,1)S(1)}, u32[]{:S(2)}, u32[]{:S(2)}) %collective-permute-start.6) | collective-permute-done | bytes 213024 | tf_op jit(solution)/shard_map/ppermute | solution.py:471
  17.8 0.1 fusion.3
  17.9 1.5 %collective-permute-start.7 = (bf16[8,3328]{1,0:T(8,128)(2,1)S(1)}, bf16[8,3328]{1,0:T(8,128)(2,1)S(1)}, u32[]{:S(2)}, u32[]{:S(2)}) collective-permute-start(bf16[8,3328]{1,0:T(8,128)(2,1)S(1)} %get-tuple-element.65), channel_id=1, source_target_pairs={{0,16},{1,17},{2,18},{3,19},{4,20},{5,21},{6,22},{7,23},{8,24},{9,... | collective-permute-start | bytes 159752 | tf_op jit(solution)/shard_map/ppermute | solution.py:471
  19.4 0.5 %collective-permute-start.9 = (bf16[8,3328]{1,0:T(8,128)(2,1)S(1)}, bf16[8,3328]{1,0:T(8,128)(2,1)S(1)}, u32[]{:S(2)}, u32[]{:S(2)}) collective-permute-start(bf16[8,3328]{1,0:T(8,128)(2,1)S(1)} %get-tuple-element.66), channel_id=1, source_target_pairs={{0,9},{1,8},{2,11},{3,10},{4,13},{5,12},{6,15},{7,14},{8,17},{9,16... | collective-permute-start | bytes 159752 | tf_op jit(solution)/shard_map/ppermute | solution.py:471
  19.9 3.0 %collective-permute-start.8 = (bf16[8,3328]{1,0:T(8,128)(2,1)S(1)}, bf16[8,3328]{1,0:T(8,128)(2,1)S(1)}, u32[]{:S(2)}, u32[]{:S(2)}) collective-permute-start(bf16[8,3328]{1,0:T(8,128)(2,1)S(1)} %get-tuple-element.67), channel_id=1, source_target_pairs={{0,25},{1,24},{2,27},{3,26},{4,29},{5,28},{6,31},{7,30},{8,1},{9,0... | collective-permute-start | bytes 159752 | tf_op jit(solution)/shard_map/ppermute | solution.py:471
  22.9 1.2 %collective-permute-done.7 = bf16[8,3328]{1,0:T(8,128)(2,1)S(1)} collective-permute-done((bf16[8,3328]{1,0:T(8,128)(2,1)S(1)}, bf16[8,3328]{1,0:T(8,128)(2,1)S(1)}, u32[]{:S(2)}, u32[]{:S(2)}) %collective-permute-start.7) | collective-permute-done | bytes 53280 | tf_op jit(solution)/shard_map/ppermute | solution.py:471
  24.1 1.1 %collective-permute-done.9 = bf16[8,3328]{1,0:T(8,128)(2,1)S(1)} collective-permute-done((bf16[8,3328]{1,0:T(8,128)(2,1)S(1)}, bf16[8,3328]{1,0:T(8,128)(2,1)S(1)}, u32[]{:S(2)}, u32[]{:S(2)}) %collective-permute-start.9) | collective-permute-done | bytes 53280 | tf_op jit(solution)/shard_map/ppermute | solution.py:471
  25.2 0.8 %collective-permute-done.8 = bf16[8,3328]{1,0:T(8,128)(2,1)S(1)} collective-permute-done((bf16[8,3328]{1,0:T(8,128)(2,1)S(1)}, bf16[8,3328]{1,0:T(8,128)(2,1)S(1)}, u32[]{:S(2)}, u32[]{:S(2)}) %collective-permute-start.8) | collective-permute-done | bytes 53280 | tf_op jit(solution)/shard_map/ppermute | solution.py:471
  26.0 2.5 %collective-permute-start.12 = (bf16[8,3328]{1,0:T(8,128)(2,1)S(1)}, bf16[8,3328]{1,0:T(8,128)(2,1)S(1)}, u32[]{:S(2)}, u32[]{:S(2)}) collective-permute-start(bf16[8,3328]{1,0:T(8,128)(2,1)S(1)} %fusion.2), channel_id=1, source_target_pairs={{0,6},{1,7},{2,4},{3,5},{4,2},{5,3},{6,0},{7,1},{8,14},{9,15},{10,... | collective-permute-start | bytes 159752 | tf_op jit(solution)/shard_map/ppermute | solution.py:471
  28.5 0.8 %collective-permute-start.10 = (bf16[8,3328]{1,0:T(8,128)(2,1)S(1)}, bf16[8,3328]{1,0:T(8,128)(2,1)S(1)}, u32[]{:S(2)}, u32[]{:S(2)}) collective-permute-start(bf16[8,3328]{1,0:T(8,128)(2,1)S(1)} %fusion.2), channel_id=1, source_target_pairs={{0,3},{1,2},{2,1},{3,0},{4,7},{5,6},{6,5},{7,4},{8,11},{9,10},{10,... | collective-permute-start | bytes 159752 | tf_op jit(solution)/shard_map/ppermute | solution.py:471
  29.3 1.8 %collective-permute-done.12 = bf16[8,3328]{1,0:T(8,128)(2,1)S(1)} collective-permute-done((bf16[8,3328]{1,0:T(8,128)(2,1)S(1)}, bf16[8,3328]{1,0:T(8,128)(2,1)S(1)}, u32[]{:S(2)}, u32[]{:S(2)}) %collective-permute-start.12) | collective-permute-done | bytes 53280 | tf_op jit(solution)/shard_map/ppermute | solution.py:471
  31.1 1.5 %collective-permute-done.11 = bf16[8,3328]{1,0:T(8,128)(2,1)S(1)} collective-permute-done((bf16[8,3328]{1,0:T(8,128)(2,1)S(1)}, bf16[8,3328]{1,0:T(8,128)(2,1)S(1)}, u32[]{:S(2)}, u32[]{:S(2)}) %collective-permute-start.11) | collective-permute-done | bytes 53280 | tf_op jit(solution)/shard_map/ppermute | solution.py:471
  32.6 0.2 collective-permute-start.13
  32.8 1.2 %collective-permute-done.13.other = f32[8,3328]{1,0:T(8,128)S(1)} collective-permute-done((f32[8,3328]{1,0:T(8,128)S(1)}, f32[8,3328]{1,0:T(8,128)S(1)}, u32[]{:S(2)}, u32[]{:S(2)}) %collective-permute-start.13) | collective-permute-done | bytes 106528 | tf_op jit(solution)/shard_map/ppermute | solution.py:471
  34.0 0.7 %finish.1 = (f32[12,1,4096]{2,1,0:T(1,128)}, f32[1,2048]{1,0:T(1,128)}, f32[1,1]{1,0:T(1,128)}) custom-call(f32[8,3328]{1,0:T(8,128)S(1)} %add_add_fusion.owned, f32[8,3328]{1,0:T(8,128)S(1)} %collective-permute-done.13.other, f32[1,128]{1,0:T(1,128)S(1)} %copy-done), custom_call_target="tpu_custom_call" | custom-call | tf_op jit(solution)/shard_map/finish/pallas_call | solution.py:430
  (28 shorter events, 0.1 us)
Async XLA Ops:
  0.6 6.8 %copy-start.8 = (bf16[1024,512]{1,0:T(8,128)(2,1)S(1)}, bf16[1024,512]{1,0:T(8,128)(2,1)}, u32[]{:S(2)}) copy-start(bf16[1024,512]{1,0:T(8,128)(2,1)} %constant.8.clone.pair) | copy-start | bytes 3145732
  0.6 6.8 %copy-start.9 = (f32[32,128]{1,0:T(8,128)S(1)}, f32[32,128]{1,0:T(8,128)}, u32[]{:S(2)}) copy-start(f32[32,128]{1,0:T(8,128)} %constant.9.clone.twiddle) | copy-start | bytes 49156
  0.7 6.7 %copy-start.10 = (f32[8,128]{1,0:T(8,128)S(1)}, f32[8,128]{1,0:T(8,128)}, u32[]{:S(2)}) copy-start(f32[8,128]{1,0:T(8,128)} %constant.10.clone.wave) | copy-start | bytes 12292
  0.7 6.7 %copy-start.3 = (f32[2048]{0:T(1024)S(1)}, f32[2048]{0:T(1024)}, u32[]{:S(2)}) copy-start(f32[2048]{0:T(1024)} %param.19) | copy-start | bytes 24580
  0.7 6.7 %copy-start.1 = (f32[128,2048]{1,0:T(8,128)S(1)}, f32[128,2048]{1,0:T(8,128)}, u32[]{:S(2)}) copy-start(f32[128,2048]{1,0:T(8,128)} %ctf.1) | copy-start | bytes 3145732
  0.7 6.7 %copy-start.5 = (s32[64]{0:T(128)S(1)}, s32[64]{0:T(128)}, u32[]{:S(2)}) copy-start(s32[64]{0:T(128)} %ids_near.1) | copy-start | bytes 772
  0.7 6.7 %copy-start.4 = (s32[8,2]{0,1:T(2,128)S(1)}, s32[8,2]{0,1:T(2,128)}, u32[]{:S(2)}) copy-start(s32[8,2]{0,1:T(2,128)} %param.16) | copy-start | bytes 196
  0.7 6.7 %copy-start.7 = (f32[4]{0:T(128)S(1)}, f32[4]{0:T(128)}, u32[]{:S(2)}) copy-start(f32[4]{0:T(128)} %param.15) | copy-start | bytes 52
  0.7 6.7 %copy-start.6 = (s32[4]{0:T(128)S(1)}, s32[4]{0:T(128)}, u32[]{:S(2)}) copy-start(s32[4]{0:T(128)} %param.14) | copy-start | bytes 52
  0.7 6.7 %copy-start.2 = (bf16[64,4096]{1,0:T(8,128)(2,1)S(1)}, bf16[64,4096]{1,0:T(8,128)(2,1)}, u32[]{:S(2)}) copy-start(bf16[64,4096]{1,0:T(8,128)(2,1)} %images.1) | copy-start | bytes 1572868
  1.8 8.8 %collective-permute-start.2 = (bf16[8,3072]{1,0:T(8,128)(2,1)S(1)}, bf16[8,3072]{1,0:T(8,128)(2,1)S(1)}, u32[]{:S(2)}, u32[]{:S(2)}) collective-permute-start(bf16[8,3072]{1,0:T(8,128)(2,1)S(1)} %get-tuple-element.48.refs_0_), channel_id=1, source_target_pairs={{0,25},{1,24},{2,27},{3,26},{4,29},{5,28},{6,31},{7,30},{8,1},{9,0... | collective-permute-start | bytes 147464 | tf_op jit(solution)/shard_map/ppermute | solution.py:471
  6.4 6.3 %collective-permute-start.1 = (bf16[8,3072]{1,0:T(8,128)(2,1)S(1)}, bf16[8,3072]{1,0:T(8,128)(2,1)S(1)}, u32[]{:S(2)}, u32[]{:S(2)}) collective-permute-start(bf16[8,3072]{1,0:T(8,128)(2,1)S(1)} %get-tuple-element.48.refs_0_), channel_id=1, source_target_pairs={{0,16},{1,17},{2,18},{3,19},{4,20},{5,21},{6,22},{7,23},{8,24},{9,... | collective-permute-start | bytes 147464 | tf_op jit(solution)/shard_map/ppermute | solution.py:471
  6.4 6.3 %collective-permute-start = (bf16[8,3072]{1,0:T(8,128)(2,1)S(1)}, bf16[8,3072]{1,0:T(8,128)(2,1)S(1)}, u32[]{:S(2)}, u32[]{:S(2)}) collective-permute-start(bf16[8,3072]{1,0:T(8,128)(2,1)S(1)} %get-tuple-element.48.refs_0_), channel_id=1, source_target_pairs={{0,9},{1,8},{2,11},{3,10},{4,13},{5,12},{6,15},{7,14},{8,17},{9,16... | collective-permute-start | bytes 147464 | tf_op jit(solution)/shard_map/ppermute | solution.py:471
  12.7 1.5 %collective-permute-start.3 = (bf16[8,3072]{1,0:T(8,128)(2,1)S(1)}, bf16[8,3072]{1,0:T(8,128)(2,1)S(1)}, u32[]{:S(2)}, u32[]{:S(2)}) collective-permute-start(bf16[8,3072]{1,0:T(8,128)(2,1)S(1)} %collective-permute-done.refs_1_), channel_id=1, source_target_pairs={{0,1},{1,0},{2,3},{3,2},{4,5},{5,4},{6,7},{7,6},{8,9},{9,8},{10,11... | collective-permute-start | bytes 147464 | tf_op jit(solution)/shard_map/ppermute | solution.py:471
  12.7 1.5 %collective-permute-start.4 = (bf16[8,3072]{1,0:T(8,128)(2,1)S(1)}, bf16[8,3072]{1,0:T(8,128)(2,1)S(1)}, u32[]{:S(2)}, u32[]{:S(2)}) collective-permute-start(bf16[8,3072]{1,0:T(8,128)(2,1)S(1)} %collective-permute-done.1.refs_2_), channel_id=1, source_target_pairs={{0,1},{1,0},{2,3},{3,2},{4,5},{5,4},{6,7},{7,6},{8,9},{9,8},{10,11... | collective-permute-start | bytes 147464 | tf_op jit(solution)/shard_map/ppermute | solution.py:471
  13.2 1.2 %collective-permute-start.5 = (bf16[8,3072]{1,0:T(8,128)(2,1)S(1)}, bf16[8,3072]{1,0:T(8,128)(2,1)S(1)}, u32[]{:S(2)}, u32[]{:S(2)}) collective-permute-start(bf16[8,3072]{1,0:T(8,128)(2,1)S(1)} %collective-permute-done.2.refs_3_), channel_id=1, source_target_pairs={{0,1},{1,0},{2,3},{3,2},{4,5},{5,4},{6,7},{7,6},{8,9},{9,8},{10,11... | collective-permute-start | bytes 147464 | tf_op jit(solution)/shard_map/ppermute | solution.py:471
  16.3 1.5 %collective-permute-start.6 = (bf16[4,8,3328]{2,1,0:T(8,128)(2,1)S(1)}, bf16[4,8,3328]{2,1,0:T(8,128)(2,1)S(1)}, u32[]{:S(2)}, u32[]{:S(2)}) collective-permute-start(bf16[4,8,3328]{2,1,0:T(8,128)(2,1)S(1)} %get-tuple-element.54), channel_id=1, source_target_pairs={{0,1},{1,0},{2,3},{3,2},{4,5},{5,4},{6,7},{7,6},{8,9},{9,8},{10,11... | collective-permute-start | bytes 638984 | tf_op jit(solution)/shard_map/ppermute | solution.py:471
  16.6 17.4 %copy-start = (f32[1,128]{1,0:T(1,128)S(1)}, f32[1,128]{1,0:T(1,128)}, u32[]{:S(2)}) copy-start(f32[1,128]{1,0:T(1,128)} %constant.11.clone.scale) | copy-start | bytes 1540
  17.9 6.2 %collective-permute-start.7 = (bf16[8,3328]{1,0:T(8,128)(2,1)S(1)}, bf16[8,3328]{1,0:T(8,128)(2,1)S(1)}, u32[]{:S(2)}, u32[]{:S(2)}) collective-permute-start(bf16[8,3328]{1,0:T(8,128)(2,1)S(1)} %get-tuple-element.65), channel_id=1, source_target_pairs={{0,16},{1,17},{2,18},{3,19},{4,20},{5,21},{6,22},{7,23},{8,24},{9,... | collective-permute-start | bytes 159752 | tf_op jit(solution)/shard_map/ppermute | solution.py:471
  19.4 5.8 %collective-permute-start.9 = (bf16[8,3328]{1,0:T(8,128)(2,1)S(1)}, bf16[8,3328]{1,0:T(8,128)(2,1)S(1)}, u32[]{:S(2)}, u32[]{:S(2)}) collective-permute-start(bf16[8,3328]{1,0:T(8,128)(2,1)S(1)} %get-tuple-element.66), channel_id=1, source_target_pairs={{0,9},{1,8},{2,11},{3,10},{4,13},{5,12},{6,15},{7,14},{8,17},{9,16... | collective-permute-start | bytes 159752 | tf_op jit(solution)/shard_map/ppermute | solution.py:471
  19.9 6.1 %collective-permute-start.8 = (bf16[8,3328]{1,0:T(8,128)(2,1)S(1)}, bf16[8,3328]{1,0:T(8,128)(2,1)S(1)}, u32[]{:S(2)}, u32[]{:S(2)}) collective-permute-start(bf16[8,3328]{1,0:T(8,128)(2,1)S(1)} %get-tuple-element.67), channel_id=1, source_target_pairs={{0,25},{1,24},{2,27},{3,26},{4,29},{5,28},{6,31},{7,30},{8,1},{9,0... | collective-permute-start | bytes 159752 | tf_op jit(solution)/shard_map/ppermute | solution.py:471
  26.0 5.1 %collective-permute-start.12 = (bf16[8,3328]{1,0:T(8,128)(2,1)S(1)}, bf16[8,3328]{1,0:T(8,128)(2,1)S(1)}, u32[]{:S(2)}, u32[]{:S(2)}) collective-permute-start(bf16[8,3328]{1,0:T(8,128)(2,1)S(1)} %fusion.2), channel_id=1, source_target_pairs={{0,6},{1,7},{2,4},{3,5},{4,2},{5,3},{6,0},{7,1},{8,14},{9,15},{10,... | collective-permute-start | bytes 159752 | tf_op jit(solution)/shard_map/ppermute | solution.py:471
  28.5 4.1 %collective-permute-start.11 = (bf16[8,3328]{1,0:T(8,128)(2,1)S(1)}, bf16[8,3328]{1,0:T(8,128)(2,1)S(1)}, u32[]{:S(2)}, u32[]{:S(2)}) collective-permute-start(bf16[8,3328]{1,0:T(8,128)(2,1)S(1)} %fusion.2), channel_id=1, source_target_pairs={{0,5},{1,4},{2,7},{3,6},{4,1},{5,0},{6,3},{7,2},{8,13},{9,12},{10,... | collective-permute-start | bytes 159752 | tf_op jit(solution)/shard_map/ppermute | solution.py:471
  28.5 4.1 %collective-permute-start.10 = (bf16[8,3328]{1,0:T(8,128)(2,1)S(1)}, bf16[8,3328]{1,0:T(8,128)(2,1)S(1)}, u32[]{:S(2)}, u32[]{:S(2)}) collective-permute-start(bf16[8,3328]{1,0:T(8,128)(2,1)S(1)} %fusion.2), channel_id=1, source_target_pairs={{0,3},{1,2},{2,1},{3,0},{4,7},{5,6},{6,5},{7,4},{8,11},{9,10},{10,... | collective-permute-start | bytes 159752 | tf_op jit(solution)/shard_map/ppermute | solution.py:471
  32.6 1.4 %collective-permute-start.13 = (f32[8,3328]{1,0:T(8,128)S(1)}, f32[8,3328]{1,0:T(8,128)S(1)}, u32[]{:S(2)}, u32[]{:S(2)}) collective-permute-start(f32[8,3328]{1,0:T(8,128)S(1)} %add_add_fusion.owned), channel_id=1, source_target_pairs={{0,1},{1,0},{2,3},{3,2},{4,5},{5,4},{6,7},{7,6},{8,9},{9,8},{10,11... | collective-permute-start | bytes 319496 | tf_op jit(solution)/shard_map/ppermute | solution.py:471

commit v7 on v6

--- a/solution.py
+++ b/solution.py
@@ -168,7 +168,7 @@
         total[here, :] = energy
         return carry
 
-    lax.fori_loop(0, count // 8, transform, 0)
+    lax.fori_loop(0, count // 8, transform, 0, unroll=4)
     energy = jnp.sum(jnp.transpose(total[...]), axis=0, keepdims=True)
     data_power[...] = jnp.concatenate([energy] * (data_power.shape[1] // count), axis=1)
 
@@ -188,7 +188,7 @@
             rotated[columns + column, s * count:(s + 1) * count, :] = (wi * c + wr * n).astype(BF16)
         return carry
 
-    lax.fori_loop(0, columns, rotate, 0)
+    lax.fori_loop(0, columns, rotate, 0, unroll=8)
 
 
 def spectra(group_ids, particles, shift_offsets, ctf_table, noise_power, slot_class, log_prior, rotations):
@@ -253,7 +253,7 @@
     return width + (rotations - TOP) * width // TOP
 
 
-def pack_body(far, mine, theirs, near, arrived):
+def fetch_body(far, near, arrived):
     width = near.shape[2]
     h = own_half()
     copies = []
@@ -262,8 +262,12 @@
         copies.append(pltpu.make_async_copy(source, near.at[j], arrived.at[j]))
     for copy in copies:
         copy.start()
+    for copy in copies:
+        copy.wait()
+
+
+def pack_body(near, mine, theirs):
     for j, out in enumerate((mine, theirs)):
-        copies[j].wait()
         out[...] = fold(near[j].astype(F32)).astype(BF16)
 
 
@@ -271,17 +275,25 @@
     _, rotations, full = references.shape
     width = full // 2
     vmem = pl.BlockSpec(memory_space=pltpu.VMEM)
+    near = pl.pallas_call(
+        fetch_body,
+        out_shape=pltpu.VMEM((2, rotations, width), BF16),
+        in_specs=[pl.BlockSpec(memory_space=pltpu.HBM)],
+        out_specs=vmem,
+        scratch_shapes=[pltpu.SemaphoreType.DMA((2,))],
+        compiler_params=pltpu.CompilerParams(vmem_limit_bytes=4 * 2**20),
+        name="fetch",
+    )(pltpu.with_memory_space_constraint(references, pltpu.HBM))
     out = pltpu.VMEM((TOP, folded_width(rotations, width)), BF16)
     return pl.pallas_call(
         pack_body,
         out_shape=(out, out),
-        in_specs=[pl.BlockSpec(memory_space=pltpu.HBM)],
+        in_specs=[vmem],
         out_specs=(vmem, vmem),
-        scratch_shapes=[pltpu.VMEM((2, rotations, width), BF16), pltpu.SemaphoreType.DMA((2,))],
         cost_estimate=pl.CostEstimate(flops=2**33, transcendentals=0, bytes_accessed=2**20),
         compiler_params=pltpu.CompilerParams(vmem_limit_bytes=4 * 2**20),
         name="pack",
-    )(pltpu.with_memory_space_constraint(references, pltpu.HBM))
+    )(pltpu.with_memory_space_constraint(near, pltpu.VMEM))
 
 
 def half_scores(h, rotated, powers, packed, stack):

time: 34.9 us -> 34.9 us (level)
  Pallas kernels: 8.28 us -> 7.87 us
  waiting for transfers between devices: 10.5 us -> 10.9 us
    ppermute x14, waiting for transfers between devices: 10.5 us -> 10.9 us  [move(): return lax.ppermute(value, ('gx', 'gy'), pairs)]
    pallas_call x1 -> x2, Pallas kernels: 1.06 us -> 0.92 us  [the longest x1 0.9 us: pack(): pl.pallas_call(fetch_body, out_shape=pltpu.VMEM((2, rotations, width), BF...]
where the time goes in v7:
time: 34.9 us; the launch traced here: 34.7 us
  starting transfers between devices  14.9 us (43%)
  waiting for transfers between devices  10.9 us (31%)
  Pallas kernels  7.87 us (23%)
  between operations  0.85 us (2%)
    ppermute x14, starting transfers between devices, move(): return lax.ppermute(value, ('gx', 'gy'), pairs)  14.9 us
    ppermute x14, waiting for transfers between devices, move(): return lax.ppermute(value, ('gx', 'gy'), pairs)  10.9 us
    pallas_call x3, Pallas kernels, local_call(): pl.pallas_call(body, out_shape=out_shape, in_specs=[chip] * len(operands)...  3.35 us
    pallas_call x1, Pallas kernels, spectra(): pl.pallas_call(spectra_body, out_shape=(shape((2 * columns, shifts * coun...  2.89 us
    pallas_call x1, Pallas kernels, pack(): pl.pallas_call(fetch_body, out_shape=pltpu.VMEM((2, rotations, width), BF...  0.9 us
    pallas_call x1, Pallas kernels, finish(): pl.pallas_call(finish_body, out_shape=(shape((rotations, 1, 2 * width), F...  0.72 us
  transfers between devices with their start and end apart: 14, of which 9 were waited for; matrix products, arithmetic and copies ran while one was open for 0% of the time, Pallas kernels for 13%

profile of v7, /device:TPU:0, one launch (start us, length us, event | category | flops | bytes accessed | tf_op | source)
XLA Modules:
  0.0 34.7 jit_solution(14073311672538603873)
XLA Ops:
  0.6 0.9 %fetch.1.near = bf16[2,12,2048]{2,1,0:T(8,128)(2,1)S(1)} custom-call(bf16[1,12,4096]{2,1,0:T(8,128)(2,1)} %far.1), custom_call_target="tpu_custom_call" | custom-call | tf_op jit(solution)/shard_map/fetch/pallas_call | solution.py:278
  1.6 0.0 copy-start.3
  1.6 0.0 copy-start.4
  1.6 0.0 copy-start.7
  1.6 0.0 copy-start.8
  1.6 0.0 copy-start.9
  1.6 0.0 copy-start.10
  1.7 4.6 %collective-permute-start.2 = (bf16[8,3072]{1,0:T(8,128)(2,1)S(1)}, bf16[8,3072]{1,0:T(8,128)(2,1)S(1)}, u32[]{:S(2)}, u32[]{:S(2)}) collective-permute-start(bf16[8,3072]{1,0:T(8,128)(2,1)S(1)} %get-tuple-element.48.refs_0_), channel_id=1, source_target_pairs={{0,25},{1,24},{2,27},{3,26},{4,29},{5,28},{6,31},{7,30},{8,1},{9,0... | collective-permute-start | bytes 147464 | tf_op jit(solution)/shard_map/ppermute | solution.py:483
  6.3 1.0 %collective-permute-start = (bf16[8,3072]{1,0:T(8,128)(2,1)S(1)}, bf16[8,3072]{1,0:T(8,128)(2,1)S(1)}, u32[]{:S(2)}, u32[]{:S(2)}) collective-permute-start(bf16[8,3072]{1,0:T(8,128)(2,1)S(1)} %get-tuple-element.48.refs_0_), channel_id=1, source_target_pairs={{0,9},{1,8},{2,11},{3,10},{4,13},{5,12},{6,15},{7,14},{8,17},{9,16... | collective-permute-start | bytes 147464 | tf_op jit(solution)/shard_map/ppermute | solution.py:483
  7.3 2.9 %spectra.1 = (bf16[32,512,128]{2,1,0:T(8,128)(2,1)S(1)}, bf16[16,128,128]{2,1,0:T(8,128)(2,1)S(1)}, bf16[16,128,128]{2,1,0:T(8,128)(2,1)S(1)}, f32[1,128]{1,0:T(1,128)S(1)}, f32[48,128]{1,0:T(8,128)S(1)}) custom-call(s32[64]{0:T(128)S(1)} %copy-done.5, s32[2,8]{1,0:T(2,128)S(1)} %bitcast.21, s32[1,4]{1,0:T(1,128)S(1)} %bitcast.22, f32[1,4]{1,0:T(1,128)S(1)} %bitcast.23, ...), custom_call_target="tpu_custom_call" | custom-call | flops 4294967296 | bytes 8388608 | tf_op jit(solution)/shard_map/spectra/pallas_call | solution.py:207
  10.2 2.3 %collective-permute-done.1.refs_2_ = bf16[8,3072]{1,0:T(8,128)(2,1)S(1)} collective-permute-done((bf16[8,3072]{1,0:T(8,128)(2,1)S(1)}, bf16[8,3072]{1,0:T(8,128)(2,1)S(1)}, u32[]{:S(2)}, u32[]{:S(2)}) %collective-permute-start.1) | collective-permute-done | bytes 49184 | tf_op jit(solution)/shard_map/ppermute | solution.py:483
  12.5 0.5 %collective-permute-start.4 = (bf16[8,3072]{1,0:T(8,128)(2,1)S(1)}, bf16[8,3072]{1,0:T(8,128)(2,1)S(1)}, u32[]{:S(2)}, u32[]{:S(2)}) collective-permute-start(bf16[8,3072]{1,0:T(8,128)(2,1)S(1)} %collective-permute-done.1.refs_2_), channel_id=1, source_target_pairs={{0,1},{1,0},{2,3},{3,2},{4,5},{5,4},{6,7},{7,6},{8,9},{9,8},{10,11... | collective-permute-start | bytes 147464 | tf_op jit(solution)/shard_map/ppermute | solution.py:483
  13.0 1.0 %shard_map.139.scores = f32[48,512]{1,0:T(8,128)S(1)} custom-call(bf16[32,512,128]{2,1,0:T(8,128)(2,1)S(1)} %get-tuple-element.40.rotated, bf16[16,128,128]{2,1,0:T(8,128)(2,1)S(1)} %get-tuple-element.41.powers, bf16[8,3072]{1,0:T(8,128)(2,1)S(1)} %get-tuple-element.48.refs_0_, bf16[8,3072]{1,0:T(8,128)(2,1)S(1)} %collective-permute-done.refs_1_, ...), custom_call_target="tpu_custom_call" | custom-call | flops 2147483648 | bytes 2097152 | tf_op jit(solution)/shard_map/pallas_call | solution.py:408
  14.1 0.2 collective-permute-done.5.refs_3_
  14.3 1.9 %shard_map.140 = (bf16[4,8,3328]{2,1,0:T(8,128)(2,1)S(1)}, bf16[48,512]{1,0:T(8,128)(2,1)S(1)}, bf16[16,128]{1,0:T(8,128)(2,1)S(1)}, f32[8,128]{1,0:T(8,128)S(1)}) custom-call(bf16[32,512,128]{2,1,0:T(8,128)(2,1)S(1)} %get-tuple-element.40.rotated, bf16[16,128,128]{2,1,0:T(8,128)(2,1)S(1)} %get-tuple-element.41.powers, ...), custom_call_target="tpu_custom_call" | custom-call | flops 2147483648 | bytes 2097152 | tf_op jit(solution)/shard_map/pallas_call | solution.py:408
  16.1 0.4 %collective-permute-start.6 = (bf16[4,8,3328]{2,1,0:T(8,128)(2,1)S(1)}, bf16[4,8,3328]{2,1,0:T(8,128)(2,1)S(1)}, u32[]{:S(2)}, u32[]{:S(2)}) collective-permute-start(bf16[4,8,3328]{2,1,0:T(8,128)(2,1)S(1)} %get-tuple-element.54), channel_id=1, source_target_pairs={{0,1},{1,0},{2,3},{3,2},{4,5},{5,4},{6,7},{7,6},{8,9},{9,8},{10,11... | collective-permute-start | bytes 638984 | tf_op jit(solution)/shard_map/ppermute | solution.py:483
  16.5 0.5 %shard_map.141 = f32[4,8,3328]{2,1,0:T(8,128)S(1)} custom-call(bf16[32,512,128]{2,1,0:T(8,128)(2,1)S(1)} %get-tuple-element.40.rotated, bf16[16,128,128]{2,1,0:T(8,128)(2,1)S(1)} %get-tuple-element.42.squares, bf16[48,512]{1,0:T(8,128)(2,1)S(1)} %get-tuple-element.55.soft, bf16[16,128]{1,0:T(8,128)(2,1)S(1)} %get-tuple-element.56.by_class, ...), custom_call_target="tpu_custom_call" | custom-call | flops 2147483648 | bytes 2097152 | tf_op jit(solution)/shard_map/pallas_call | solution.py:408
  17.0 0.7 %collective-permute-done.6 = bf16[4,8,3328]{2,1,0:T(8,128)(2,1)S(1)} collective-permute-done((bf16[4,8,3328]{2,1,0:T(8,128)(2,1)S(1)}, bf16[4,8,3328]{2,1,0:T(8,128)(2,1)S(1)}, u32[]{:S(2)}, u32[]{:S(2)}) %collective-permute-start.6) | collective-permute-done | bytes 213024 | tf_op jit(solution)/shard_map/ppermute | solution.py:483
  17.7 0.1 fusion.3
  17.8 1.5 %collective-permute-start.7 = (bf16[8,3328]{1,0:T(8,128)(2,1)S(1)}, bf16[8,3328]{1,0:T(8,128)(2,1)S(1)}, u32[]{:S(2)}, u32[]{:S(2)}) collective-permute-start(bf16[8,3328]{1,0:T(8,128)(2,1)S(1)} %get-tuple-element.65), channel_id=1, source_target_pairs={{0,16},{1,17},{2,18},{3,19},{4,20},{5,21},{6,22},{7,23},{8,24},{9,... | collective-permute-start | bytes 159752 | tf_op jit(solution)/shard_map/ppermute | solution.py:483
  19.2 0.5 %collective-permute-start.9 = (bf16[8,3328]{1,0:T(8,128)(2,1)S(1)}, bf16[8,3328]{1,0:T(8,128)(2,1)S(1)}, u32[]{:S(2)}, u32[]{:S(2)}) collective-permute-start(bf16[8,3328]{1,0:T(8,128)(2,1)S(1)} %get-tuple-element.66), channel_id=1, source_target_pairs={{0,9},{1,8},{2,11},{3,10},{4,13},{5,12},{6,15},{7,14},{8,17},{9,16... | collective-permute-start | bytes 159752 | tf_op jit(solution)/shard_map/ppermute | solution.py:483
  19.7 3.1 %collective-permute-start.8 = (bf16[8,3328]{1,0:T(8,128)(2,1)S(1)}, bf16[8,3328]{1,0:T(8,128)(2,1)S(1)}, u32[]{:S(2)}, u32[]{:S(2)}) collective-permute-start(bf16[8,3328]{1,0:T(8,128)(2,1)S(1)} %get-tuple-element.67), channel_id=1, source_target_pairs={{0,25},{1,24},{2,27},{3,26},{4,29},{5,28},{6,31},{7,30},{8,1},{9,0... | collective-permute-start | bytes 159752 | tf_op jit(solution)/shard_map/ppermute | solution.py:483
  22.8 1.1 %collective-permute-done.7 = bf16[8,3328]{1,0:T(8,128)(2,1)S(1)} collective-permute-done((bf16[8,3328]{1,0:T(8,128)(2,1)S(1)}, bf16[8,3328]{1,0:T(8,128)(2,1)S(1)}, u32[]{:S(2)}, u32[]{:S(2)}) %collective-permute-start.7) | collective-permute-done | bytes 53280 | tf_op jit(solution)/shard_map/ppermute | solution.py:483
  23.9 1.2 %collective-permute-done.9 = bf16[8,3328]{1,0:T(8,128)(2,1)S(1)} collective-permute-done((bf16[8,3328]{1,0:T(8,128)(2,1)S(1)}, bf16[8,3328]{1,0:T(8,128)(2,1)S(1)}, u32[]{:S(2)}, u32[]{:S(2)}) %collective-permute-start.9) | collective-permute-done | bytes 53280 | tf_op jit(solution)/shard_map/ppermute | solution.py:483
  25.1 0.8 %collective-permute-done.8 = bf16[8,3328]{1,0:T(8,128)(2,1)S(1)} collective-permute-done((bf16[8,3328]{1,0:T(8,128)(2,1)S(1)}, bf16[8,3328]{1,0:T(8,128)(2,1)S(1)}, u32[]{:S(2)}, u32[]{:S(2)}) %collective-permute-start.8) | collective-permute-done | bytes 53280 | tf_op jit(solution)/shard_map/ppermute | solution.py:483
  25.9 2.5 %collective-permute-start.12 = (bf16[8,3328]{1,0:T(8,128)(2,1)S(1)}, bf16[8,3328]{1,0:T(8,128)(2,1)S(1)}, u32[]{:S(2)}, u32[]{:S(2)}) collective-permute-start(bf16[8,3328]{1,0:T(8,128)(2,1)S(1)} %fusion.2), channel_id=1, source_target_pairs={{0,6},{1,7},{2,4},{3,5},{4,2},{5,3},{6,0},{7,1},{8,14},{9,15},{10,... | collective-permute-start | bytes 159752 | tf_op jit(solution)/shard_map/ppermute | solution.py:483
  28.5 0.7 %collective-permute-start.10 = (bf16[8,3328]{1,0:T(8,128)(2,1)S(1)}, bf16[8,3328]{1,0:T(8,128)(2,1)S(1)}, u32[]{:S(2)}, u32[]{:S(2)}) collective-permute-start(bf16[8,3328]{1,0:T(8,128)(2,1)S(1)} %fusion.2), channel_id=1, source_target_pairs={{0,3},{1,2},{2,1},{3,0},{4,7},{5,6},{6,5},{7,4},{8,11},{9,10},{10,... | collective-permute-start | bytes 159752 | tf_op jit(solution)/shard_map/ppermute | solution.py:483
  29.2 1.8 %collective-permute-done.12 = bf16[8,3328]{1,0:T(8,128)(2,1)S(1)} collective-permute-done((bf16[8,3328]{1,0:T(8,128)(2,1)S(1)}, bf16[8,3328]{1,0:T(8,128)(2,1)S(1)}, u32[]{:S(2)}, u32[]{:S(2)}) %collective-permute-start.12) | collective-permute-done | bytes 53280 | tf_op jit(solution)/shard_map/ppermute | solution.py:483
  31.0 1.5 %collective-permute-done.11 = bf16[8,3328]{1,0:T(8,128)(2,1)S(1)} collective-permute-done((bf16[8,3328]{1,0:T(8,128)(2,1)S(1)}, bf16[8,3328]{1,0:T(8,128)(2,1)S(1)}, u32[]{:S(2)}, u32[]{:S(2)}) %collective-permute-start.11) | collective-permute-done | bytes 53280 | tf_op jit(solution)/shard_map/ppermute | solution.py:483
  32.6 0.2 collective-permute-start.13
  32.8 1.2 %collective-permute-done.13.other = f32[8,3328]{1,0:T(8,128)S(1)} collective-permute-done((f32[8,3328]{1,0:T(8,128)S(1)}, f32[8,3328]{1,0:T(8,128)S(1)}, u32[]{:S(2)}, u32[]{:S(2)}) %collective-permute-start.13) | collective-permute-done | bytes 106528 | tf_op jit(solution)/shard_map/ppermute | solution.py:483
  34.0 0.7 %finish.1 = (f32[12,1,4096]{2,1,0:T(1,128)}, f32[1,2048]{1,0:T(1,128)}, f32[1,1]{1,0:T(1,128)}) custom-call(f32[8,3328]{1,0:T(8,128)S(1)} %add_add_fusion.owned, f32[8,3328]{1,0:T(8,128)S(1)} %collective-permute-done.13.other, f32[1,128]{1,0:T(1,128)S(1)} %copy-done), custom_call_target="tpu_custom_call" | custom-call | tf_op jit(solution)/shard_map/finish/pallas_call | solution.py:442
  (29 shorter events, 0.2 us)
Async XLA Ops:
  1.5 5.7 %copy-start.1 = (f32[128,2048]{1,0:T(8,128)S(1)}, f32[128,2048]{1,0:T(8,128)}, u32[]{:S(2)}) copy-start(f32[128,2048]{1,0:T(8,128)} %ctf.1) | copy-start | bytes 3145732
  1.6 5.7 %copy-start.2 = (bf16[64,4096]{1,0:T(8,128)(2,1)S(1)}, bf16[64,4096]{1,0:T(8,128)(2,1)}, u32[]{:S(2)}) copy-start(bf16[64,4096]{1,0:T(8,128)(2,1)} %images.1) | copy-start | bytes 1572868
  1.6 5.7 %copy-start.3 = (f32[2048]{0:T(1024)S(1)}, f32[2048]{0:T(1024)}, u32[]{:S(2)}) copy-start(f32[2048]{0:T(1024)} %param.19) | copy-start | bytes 24580
  1.6 5.7 %copy-start.4 = (s32[8,2]{0,1:T(2,128)S(1)}, s32[8,2]{0,1:T(2,128)}, u32[]{:S(2)}) copy-start(s32[8,2]{0,1:T(2,128)} %param.16) | copy-start | bytes 196
  1.6 5.7 %copy-start.5 = (s32[64]{0:T(128)S(1)}, s32[64]{0:T(128)}, u32[]{:S(2)}) copy-start(s32[64]{0:T(128)} %ids_near.1) | copy-start | bytes 772
  1.6 5.7 %copy-start.6 = (s32[4]{0:T(128)S(1)}, s32[4]{0:T(128)}, u32[]{:S(2)}) copy-start(s32[4]{0:T(128)} %param.14) | copy-start | bytes 52
  1.6 5.7 %copy-start.7 = (f32[4]{0:T(128)S(1)}, f32[4]{0:T(128)}, u32[]{:S(2)}) copy-start(f32[4]{0:T(128)} %param.15) | copy-start | bytes 52
  1.6 5.7 %copy-start.8 = (bf16[1024,512]{1,0:T(8,128)(2,1)S(1)}, bf16[1024,512]{1,0:T(8,128)(2,1)}, u32[]{:S(2)}) copy-start(bf16[1024,512]{1,0:T(8,128)(2,1)} %constant.8.clone.pair) | copy-start | bytes 3145732
  1.6 5.7 %copy-start.9 = (f32[32,128]{1,0:T(8,128)S(1)}, f32[32,128]{1,0:T(8,128)}, u32[]{:S(2)}) copy-start(f32[32,128]{1,0:T(8,128)} %constant.9.clone.twiddle) | copy-start | bytes 49156
  1.6 5.7 %copy-start.10 = (f32[8,128]{1,0:T(8,128)S(1)}, f32[8,128]{1,0:T(8,128)}, u32[]{:S(2)}) copy-start(f32[8,128]{1,0:T(8,128)} %constant.10.clone.wave) | copy-start | bytes 12292
  1.7 8.6 %collective-permute-start.2 = (bf16[8,3072]{1,0:T(8,128)(2,1)S(1)}, bf16[8,3072]{1,0:T(8,128)(2,1)S(1)}, u32[]{:S(2)}, u32[]{:S(2)}) collective-permute-start(bf16[8,3072]{1,0:T(8,128)(2,1)S(1)} %get-tuple-element.48.refs_0_), channel_id=1, source_target_pairs={{0,25},{1,24},{2,27},{3,26},{4,29},{5,28},{6,31},{7,30},{8,1},{9,0... | collective-permute-start | bytes 147464 | tf_op jit(solution)/shard_map/ppermute | solution.py:483
  6.3 6.3 %collective-permute-start.1 = (bf16[8,3072]{1,0:T(8,128)(2,1)S(1)}, bf16[8,3072]{1,0:T(8,128)(2,1)S(1)}, u32[]{:S(2)}, u32[]{:S(2)}) collective-permute-start(bf16[8,3072]{1,0:T(8,128)(2,1)S(1)} %get-tuple-element.48.refs_0_), channel_id=1, source_target_pairs={{0,16},{1,17},{2,18},{3,19},{4,20},{5,21},{6,22},{7,23},{8,24},{9,... | collective-permute-start | bytes 147464 | tf_op jit(solution)/shard_map/ppermute | solution.py:483
  6.3 6.3 %collective-permute-start = (bf16[8,3072]{1,0:T(8,128)(2,1)S(1)}, bf16[8,3072]{1,0:T(8,128)(2,1)S(1)}, u32[]{:S(2)}, u32[]{:S(2)}) collective-permute-start(bf16[8,3072]{1,0:T(8,128)(2,1)S(1)} %get-tuple-element.48.refs_0_), channel_id=1, source_target_pairs={{0,9},{1,8},{2,11},{3,10},{4,13},{5,12},{6,15},{7,14},{8,17},{9,16... | collective-permute-start | bytes 147464 | tf_op jit(solution)/shard_map/ppermute | solution.py:483
  12.5 1.5 %collective-permute-start.3 = (bf16[8,3072]{1,0:T(8,128)(2,1)S(1)}, bf16[8,3072]{1,0:T(8,128)(2,1)S(1)}, u32[]{:S(2)}, u32[]{:S(2)}) collective-permute-start(bf16[8,3072]{1,0:T(8,128)(2,1)S(1)} %collective-permute-done.refs_1_), channel_id=1, source_target_pairs={{0,1},{1,0},{2,3},{3,2},{4,5},{5,4},{6,7},{7,6},{8,9},{9,8},{10,11... | collective-permute-start | bytes 147464 | tf_op jit(solution)/shard_map/ppermute | solution.py:483
  12.5 1.5 %collective-permute-start.4 = (bf16[8,3072]{1,0:T(8,128)(2,1)S(1)}, bf16[8,3072]{1,0:T(8,128)(2,1)S(1)}, u32[]{:S(2)}, u32[]{:S(2)}) collective-permute-start(bf16[8,3072]{1,0:T(8,128)(2,1)S(1)} %collective-permute-done.1.refs_2_), channel_id=1, source_target_pairs={{0,1},{1,0},{2,3},{3,2},{4,5},{5,4},{6,7},{7,6},{8,9},{9,8},{10,11... | collective-permute-start | bytes 147464 | tf_op jit(solution)/shard_map/ppermute | solution.py:483
  13.0 1.2 %collective-permute-start.5 = (bf16[8,3072]{1,0:T(8,128)(2,1)S(1)}, bf16[8,3072]{1,0:T(8,128)(2,1)S(1)}, u32[]{:S(2)}, u32[]{:S(2)}) collective-permute-start(bf16[8,3072]{1,0:T(8,128)(2,1)S(1)} %collective-permute-done.2.refs_3_), channel_id=1, source_target_pairs={{0,1},{1,0},{2,3},{3,2},{4,5},{5,4},{6,7},{7,6},{8,9},{9,8},{10,11... | collective-permute-start | bytes 147464 | tf_op jit(solution)/shard_map/ppermute | solution.py:483
  16.1 1.5 %collective-permute-start.6 = (bf16[4,8,3328]{2,1,0:T(8,128)(2,1)S(1)}, bf16[4,8,3328]{2,1,0:T(8,128)(2,1)S(1)}, u32[]{:S(2)}, u32[]{:S(2)}) collective-permute-start(bf16[4,8,3328]{2,1,0:T(8,128)(2,1)S(1)} %get-tuple-element.54), channel_id=1, source_target_pairs={{0,1},{1,0},{2,3},{3,2},{4,5},{5,4},{6,7},{7,6},{8,9},{9,8},{10,11... | collective-permute-start | bytes 638984 | tf_op jit(solution)/shard_map/ppermute | solution.py:483
  16.5 17.5 %copy-start = (f32[1,128]{1,0:T(1,128)S(1)}, f32[1,128]{1,0:T(1,128)}, u32[]{:S(2)}) copy-start(f32[1,128]{1,0:T(1,128)} %constant.11.clone.scale) | copy-start | bytes 1540
  17.8 6.1 %collective-permute-start.7 = (bf16[8,3328]{1,0:T(8,128)(2,1)S(1)}, bf16[8,3328]{1,0:T(8,128)(2,1)S(1)}, u32[]{:S(2)}, u32[]{:S(2)}) collective-permute-start(bf16[8,3328]{1,0:T(8,128)(2,1)S(1)} %get-tuple-element.65), channel_id=1, source_target_pairs={{0,16},{1,17},{2,18},{3,19},{4,20},{5,21},{6,22},{7,23},{8,24},{9,... | collective-permute-start | bytes 159752 | tf_op jit(solution)/shard_map/ppermute | solution.py:483
  19.2 5.8 %collective-permute-start.9 = (bf16[8,3328]{1,0:T(8,128)(2,1)S(1)}, bf16[8,3328]{1,0:T(8,128)(2,1)S(1)}, u32[]{:S(2)}, u32[]{:S(2)}) collective-permute-start(bf16[8,3328]{1,0:T(8,128)(2,1)S(1)} %get-tuple-element.66), channel_id=1, source_target_pairs={{0,9},{1,8},{2,11},{3,10},{4,13},{5,12},{6,15},{7,14},{8,17},{9,16... | collective-permute-start | bytes 159752 | tf_op jit(solution)/shard_map/ppermute | solution.py:483
  19.7 6.2 %collective-permute-start.8 = (bf16[8,3328]{1,0:T(8,128)(2,1)S(1)}, bf16[8,3328]{1,0:T(8,128)(2,1)S(1)}, u32[]{:S(2)}, u32[]{:S(2)}) collective-permute-start(bf16[8,3328]{1,0:T(8,128)(2,1)S(1)} %get-tuple-element.67), channel_id=1, source_target_pairs={{0,25},{1,24},{2,27},{3,26},{4,29},{5,28},{6,31},{7,30},{8,1},{9,0... | collective-permute-start | bytes 159752 | tf_op jit(solution)/shard_map/ppermute | solution.py:483
  25.9 5.1 %collective-permute-start.12 = (bf16[8,3328]{1,0:T(8,128)(2,1)S(1)}, bf16[8,3328]{1,0:T(8,128)(2,1)S(1)}, u32[]{:S(2)}, u32[]{:S(2)}) collective-permute-start(bf16[8,3328]{1,0:T(8,128)(2,1)S(1)} %fusion.2), channel_id=1, source_target_pairs={{0,6},{1,7},{2,4},{3,5},{4,2},{5,3},{6,0},{7,1},{8,14},{9,15},{10,... | collective-permute-start | bytes 159752 | tf_op jit(solution)/shard_map/ppermute | solution.py:483
  28.5 4.1 %collective-permute-start.11 = (bf16[8,3328]{1,0:T(8,128)(2,1)S(1)}, bf16[8,3328]{1,0:T(8,128)(2,1)S(1)}, u32[]{:S(2)}, u32[]{:S(2)}) collective-permute-start(bf16[8,3328]{1,0:T(8,128)(2,1)S(1)} %fusion.2), channel_id=1, source_target_pairs={{0,5},{1,4},{2,7},{3,6},{4,1},{5,0},{6,3},{7,2},{8,13},{9,12},{10,... | collective-permute-start | bytes 159752 | tf_op jit(solution)/shard_map/ppermute | solution.py:483
  28.5 4.1 %collective-permute-start.10 = (bf16[8,3328]{1,0:T(8,128)(2,1)S(1)}, bf16[8,3328]{1,0:T(8,128)(2,1)S(1)}, u32[]{:S(2)}, u32[]{:S(2)}) collective-permute-start(bf16[8,3328]{1,0:T(8,128)(2,1)S(1)} %fusion.2), channel_id=1, source_target_pairs={{0,3},{1,2},{2,1},{3,0},{4,7},{5,6},{6,5},{7,4},{8,11},{9,10},{10,... | collective-permute-start | bytes 159752 | tf_op jit(solution)/shard_map/ppermute | solution.py:483
  32.6 1.4 %collective-permute-start.13 = (f32[8,3328]{1,0:T(8,128)S(1)}, f32[8,3328]{1,0:T(8,128)S(1)}, u32[]{:S(2)}, u32[]{:S(2)}) collective-permute-start(f32[8,3328]{1,0:T(8,128)S(1)} %add_add_fusion.owned), channel_id=1, source_target_pairs={{0,1},{1,0},{2,3},{3,2},{4,5},{5,4},{6,7},{7,6},{8,9},{9,8},{10,11... | collective-permute-start | bytes 319496 | tf_op jit(solution)/shard_map/ppermute | solution.py:483
